TPU v7x, 32 devices: a whole 2x2x4 slice. The times are simulated.
32 devices in a mesh: leaf: 4 (over z), dom: 2 (over core), rep: 4 (over y, x).
Axes of the slice: x: 2, y: 2, z: 4, core: 2. Of those that a mesh axis runs over, the one named last changes fastest.
Arguments:
- leaf_basis: bfloat16 [128, 512, 128], P(('leaf', 'dom', 'rep')), as said below
- transfer: float32 [224, 128, 128], P(('leaf', 'dom', 'rep')), as said below
- transfer_top: float32 [16, 128, 128], P(('leaf', 'dom')), as said below
- coupling_parts: bfloat16 [4, 512, 128, 128], P('rep', ('leaf', 'dom')), may hold values from -1 to 1
- row_slot: int32 [512], P(('leaf', 'dom', 'rep')), may hold values from 0 to 6, as said below
- col_node: int32 [512], P(('leaf', 'dom', 'rep')), may hold values from 0 to 223, as said below
Outputs:
- leaf_orth: bfloat16 [128, 512, 128], P(('leaf', 'dom', 'rep'))
- new_transfer: float32 [224, 128, 128], P(('leaf', 'dom', 'rep'))
- new_top: float32 [16, 128, 128], P(('leaf', 'dom'), 'rep')
- top_factor: float32 [8, 128, 128], P(('leaf', 'dom'), 'rep')
- coupling_new: bfloat16 [512, 128, 128], P(('leaf', 'dom', 'rep'))
Inputs may be any that keep to these rules, and one draw needn't show every extreme that they name: `leaf_basis`: every leaf block has full column rank. Every transfer factor is invertible. `transfer_top`: every transfer factor is invertible. `row_slot`: slots 0 to 3 are the holding device's four leaves, 4 and 5 its two level-1 nodes, 6 its level-2 node; the holder of block k is device position k // 16 along leaf+dom+rep. col_node[k] = 7 d + c, where d is a device position along leaf+dom+rep at most 2 away from the holder of block k and c is a slot of the same level as row_slot[k] (0 to 3, 4 to 5, or 6); the first block of every device has its column node exactly 2 positions away.
All inputs are finite; a program needn't handle non-finite values.
Results may differ from a plain program's by a relative error of at most 0.013.
Values may be sent and summed in bfloat16 or wider, within the bound.
No kernel may reach another device: no remote copies, remote signals or barrier semaphores. Data moves between devices by JAX's collectives and lax.ppermute only.
A program may use at most 64 MiB of HBM per device.

v0:
```python
import functools

import jax
import jax.numpy as jnp
from jax import lax
from jax.experimental import pallas as pl
from jax.experimental.pallas import tpu as pltpu
from jax.sharding import PartitionSpec as P

PTS = 512
REACH = 2
PANEL = 8
ALL = ("leaf", "dom", "rep")
F32 = jnp.float32
BF16 = jnp.bfloat16
VMEM = pl.BlockSpec(memory_space=pltpu.VMEM)
SMEM = pl.BlockSpec(memory_space=pltpu.SMEM)
ANY = pl.BlockSpec(memory_space=pl.ANY)


def dot_nn(a, b):
    return lax.dot_general(
        a, b, (((1,), (0,)), ((), ())),
        precision=lax.Precision.HIGHEST, preferred_element_type=F32,
    )


def dot_tn(a, b):
    return lax.dot_general(
        a, b, (((0,), (0,)), ((), ())),
        precision=lax.Precision.HIGHEST, preferred_element_type=F32,
    )


def dot_nt(a, b):
    return lax.dot_general(
        a, b, (((1,), (1,)), ((), ())),
        precision=lax.Precision.HIGHEST, preferred_element_type=F32,
    )


def congruence(gram, trans):
    return dot_tn(trans, dot_nn(gram, trans))


def split3(x):
    high = x.astype(BF16).astype(F32)
    rest = x - high
    mid = rest.astype(BF16).astype(F32)
    return high, mid, rest - mid


def factorize(work, upper, inverse, mats):
    size = work.shape[-1]
    shape = (PANEL, size)
    sub = lax.broadcasted_iota(jnp.int32, shape, 0)
    lane = lax.broadcasted_iota(jnp.int32, shape, 1)

    def row(value, at):
        return jnp.broadcast_to(value[at : at + 1, :], shape)

    for start in range(0, size, PANEL):
        stop = start + PANEL
        in_panel = (lane >= start) & (lane < stop)
        eye = (lane == sub + start).astype(F32)
        tops = [work[m, start:stop, :] for m in mats]
        cols = [
            [jnp.broadcast_to(top[:, start + k : start + k + 1], shape) for k in range(PANEL)]
            for top in tops
        ]
        both = [jnp.where(in_panel, eye, top) for top in tops]
        for j in range(PANEL):
            for t in range(len(mats)):
                scale = lax.rsqrt(row(cols[t][j], j))
                low = cols[t][j] * scale
                below = jnp.where(sub > j, low, 0.0)
                for k in range(j + 1, PANEL):
                    cols[t][k] = cols[t][k] - below * row(low, k)
                pivot = row(tops[t], j) * scale
                tops[t] = jnp.where(sub == j, pivot, tops[t] - below * pivot)
                pivot = row(both[t], j) * scale
                both[t] = jnp.where(sub == j, pivot, both[t] - below * pivot)
        for t, m in enumerate(mats):
            upper[m, start:stop, :] = jnp.where(lane >= sub + start, tops[t], 0.0)
            inverse[m, start:stop, :] = jnp.where(lane < stop, both[t], 0.0)
            if stop < size:
                high, mid, low = split3(both[t])
                left = jnp.concatenate([high, high, mid, mid, high, low], axis=0)
                right = jnp.concatenate([high, mid, high, mid, low, high], axis=0)
                update = lax.dot_general(
                    left.astype(BF16), right.astype(BF16), (((0,), (0,)), ((), ())),
                    preferred_element_type=F32,
                )
                rest = lax.broadcasted_iota(jnp.int32, (size - stop, size), 1)
                drop = (rest >= start) & (rest < stop)
                old = jnp.where(drop, 0.0, work[m, stop:, :])
                work[m, stop:, :] = old - update[stop:, :]


def gram_kernel(basis, trans, grams, sent):
    leaves = basis.shape[0]
    for i in range(leaves):
        rows = basis[i]
        grams[i] = lax.dot_general(
            rows, rows, (((0,), (0,)), ((), ())), preferred_element_type=F32
        ) * (1.0 / PTS)
    base, count = 0, leaves
    while count > 1:
        for pair in range(count // 2):
            one, two = base + 2 * pair, base + 2 * pair + 1
            grams[base + count + pair] = congruence(grams[one], trans[one]) + congruence(
                grams[two], trans[two]
            )
        base, count = base + count, count // 2
    sent[...] = congruence(grams[base], trans[base])


def factor_kernel(rep, grams, own, near, far_a, far_b, trans_top, pool, upper, inverse, work):
    slots = grams.shape[0]
    high = rep[0] // 2
    mine = own[...] + near[...]
    other = far_a[...] + far_b[...]
    three_a = jnp.where(high == 0, mine, other)
    three_b = jnp.where(high == 0, other, mine)
    work[:slots] = grams[...]
    work[slots] = three_a
    work[slots + 1] = three_b
    work[slots + 2] = congruence(three_a, trans_top[0]) + congruence(three_b, trans_top[1])
    factorize(work, upper, inverse, list(range(slots + 3)))
    pool[...] = upper[:slots].astype(BF16)


def finish_kernel(rep, basis, trans, trans_top, upper, inverse, orth, fresh, top, four):
    leaves = basis.shape[0]
    for i in range(leaves):
        orth[i] = lax.dot_general(
            basis[i], inverse[i].astype(BF16), (((1,), (1,)), ((), ())),
            preferred_element_type=F32,
        ).astype(BF16)
    base, count = 0, leaves
    while count > 1:
        for child in range(count):
            node = base + child
            fresh[node] = dot_nt(
                dot_nn(upper[node], trans[node]), inverse[base + count + child // 2]
            )
        base, count = base + count, count // 2
    share = four.shape[1]
    rows = pl.ds(pl.multiple_of(rep[0] * share, share), share)
    three = base + 1
    own_three = inverse[three + rep[0] // 2]
    fresh[base] = dot_nt(dot_nn(upper[base], trans[base]), own_three)
    for c in range(2):
        top[c] = dot_nt(dot_nn(upper[three + c, rows, :], trans_top[c]), inverse[three + 2])
    four[0] = upper[three + 2, rows, :]


def project_kernel(row_slot, col_at, got, *refs):
    pieces, (out, pool, sem) = refs[: 2 * REACH + 1], refs[2 * REACH + 1 :]
    slots = pieces[0].shape[0]
    tiles = out.shape[0]
    copies = [
        pltpu.make_async_copy(piece, pool.at[pl.ds(i * slots, slots)], sem.at[i])
        for i, piece in enumerate(pieces)
    ]
    for copy in copies:
        copy.start()
    for copy in copies:
        copy.wait()
    for k in range(tiles):
        total = got[0, k].astype(F32)
        for i in range(1, got.shape[0]):
            total = total + got[i, k].astype(F32)
        half = jnp.dot(
            pool[REACH * slots + row_slot[k]], total.astype(BF16), preferred_element_type=F32
        ).astype(BF16)
        out[k] = lax.dot_general(
            half, pool[col_at[k]], (((1,), (1,)), ((), ())), preferred_element_type=F32
        ).astype(BF16)


def from_behind(value, axis, steps):
    count = lax.axis_size(axis)
    leading, last = (max(0, -steps), min(count, count - steps))
    return lax.ppermute(value, axis, [(source, source + steps) for source in range(leading, last)])


def swapped(value, flip):
    return lax.ppermute(value, "rep", [(i, i ^ flip) for i in range(lax.axis_size("rep"))])


def per_device(leaf_basis, transfer, transfer_top, coupling_parts, row_slot, col_node):
    rank = transfer.shape[1]
    slots = transfer.shape[0]
    leaves = leaf_basis.shape[0]
    reps = lax.axis_size("rep")
    tiles = row_slot.shape[0]
    square = (rank, rank)
    rep = lax.axis_index("rep").astype(jnp.int32).reshape(1)

    got = lax.all_to_all(
        coupling_parts.reshape(reps, tiles, rank, rank), "rep", 0, 0, tiled=True
    )

    grams, sent = pl.pallas_call(
        gram_kernel,
        out_shape=[
            jax.ShapeDtypeStruct((slots, *square), F32),
            jax.ShapeDtypeStruct(square, F32),
        ],
        in_specs=[VMEM, VMEM],
        out_specs=[VMEM, VMEM],
        name="grams",
    )(leaf_basis, transfer)
    near, far_a, far_b = (swapped(sent, flip) for flip in (1, 2, 3))
    pool, upper, inverse = pl.pallas_call(
        factor_kernel,
        out_shape=[
            jax.ShapeDtypeStruct((slots, *square), BF16),
            jax.ShapeDtypeStruct((slots + 3, *square), F32),
            jax.ShapeDtypeStruct((slots + 3, *square), F32),
        ],
        in_specs=[SMEM] + [VMEM] * 6,
        out_specs=[VMEM] * 3,
        scratch_shapes=[pltpu.VMEM((slots + 3, *square), F32)],
        name="factor",
    )(rep, grams, sent, near, far_a, far_b, transfer_top)
    pieces = [
        pool if offset == 0 else from_behind(pool, ALL, -offset)
        for offset in range(-REACH, REACH + 1)
    ]
    share = rank // reps
    orth, fresh, top, four = pl.pallas_call(
        finish_kernel,
        out_shape=[
            jax.ShapeDtypeStruct(leaf_basis.shape, BF16),
            jax.ShapeDtypeStruct(transfer.shape, F32),
            jax.ShapeDtypeStruct((2, share, rank), F32),
            jax.ShapeDtypeStruct((1, share, rank), F32),
        ],
        in_specs=[SMEM] + [VMEM] * 5,
        out_specs=[VMEM] * 4,
        name="finish",
    )(rep, leaf_basis, transfer, transfer_top, upper, inverse)
    my_index = lax.axis_index(ALL)
    col_at = (col_node // slots - my_index + REACH) * slots + col_node % slots
    projected = pl.pallas_call(
        project_kernel,
        out_shape=jax.ShapeDtypeStruct((tiles, *square), BF16),
        in_specs=[SMEM] * 2 + [VMEM] + [ANY] * (2 * REACH + 1),
        out_specs=VMEM,
        scratch_shapes=[
            pltpu.VMEM(((2 * REACH + 1) * slots, *square), BF16),
            pltpu.SemaphoreType.DMA((2 * REACH + 1,)),
        ],
        name="project",
    )(row_slot, col_at, got, *pieces)
    return (orth, fresh, top, four, projected)


def solution(mesh):
    return jax.shard_map(
        per_device,
        mesh=mesh,
        in_specs=(
            P(ALL, None, None),
            P(ALL, None, None),
            P(("leaf", "dom"), None, None),
            P("rep", ("leaf", "dom"), None, None),
            P(ALL),
            P(ALL),
        ),
        out_specs=(
            P(ALL, None, None),
            P(ALL, None, None),
            P(("leaf", "dom"), "rep", None),
            P(("leaf", "dom"), "rep", None),
            P(ALL, None, None),
        ),
        check_vma=False,
    )
```

profile of v0, /device:TPU:28, one launch (start us, length us, event | category | flops | bytes accessed | tf_op | source)
XLA Modules:
  0.0 73.7 jit_solution(9565849441362241294)
XLA Ops:
  0.6 0.0 copy-start.8
  0.6 4.2 %all-to-all-start = ((bf16[4,16,128,128]{3,2,1,0:T(8,128)(2,1)}), bf16[4,16,128,128]{3,2,1,0:T(8,128)(2,1)S(1)}, u32[]{:S(2)}, u32[]{:S(2)}) async-start(bf16[4,16,128,128]{3,2,1,0:T(8,128)(2,1)} %bitcast.2), calls=%async_computation | async-start | bytes 4194304 | tf_op jit(solution)/shard_map/all_to_all | solution.py:201
  4.9 3.8 %grams.1 = (f32[7,128,128]{2,1,0:T(8,128)}, f32[128,128]{1,0:T(8,128)}) custom-call(bf16[4,512,128]{2,1,0:T(8,128)(2,1)} %basis.3, f32[7,128,128]{2,1,0:T(8,128)} %trans.3), custom_call_target="tpu_custom_call" | custom-call | tf_op jit(solution)/shard_map/grams/pallas_call | solution.py:205
  8.7 1.5 %collective-permute-start.2 = (f32[128,128]{1,0:T(8,128)}, f32[128,128]{1,0:T(8,128)S(1)}, u32[]{:S(2)}, u32[]{:S(2)}) collective-permute-start(f32[128,128]{1,0:T(8,128)} %get-tuple-element.15.own), channel_id=1, source_target_pairs={{0,3},{1,2},{2,1},{3,0},{4,7},{5,6},{6,5},{7,4},{8,11},{9,10},{10,... | collective-permute-start | bytes 196616 | tf_op jit(solution)/shard_map/ppermute | solution.py:189
  10.1 1.5 %collective-permute-start.1 = (f32[128,128]{1,0:T(8,128)}, f32[128,128]{1,0:T(8,128)S(1)}, u32[]{:S(2)}, u32[]{:S(2)}) collective-permute-start(f32[128,128]{1,0:T(8,128)} %get-tuple-element.15.own), channel_id=1, source_target_pairs={{0,2},{1,3},{2,0},{3,1},{4,6},{5,7},{6,4},{7,5},{8,10},{9,11},{10,... | collective-permute-start | bytes 196616 | tf_op jit(solution)/shard_map/ppermute | solution.py:189
  11.6 0.6 collective-permute-start
  12.1 19.3 %collective-permute-done.2.far_b = f32[128,128]{1,0:T(8,128)S(1)} collective-permute-done((f32[128,128]{1,0:T(8,128)}, f32[128,128]{1,0:T(8,128)S(1)}, u32[]{:S(2)}, u32[]{:S(2)}) %collective-permute-start.2) | collective-permute-done | bytes 65568 | tf_op jit(solution)/shard_map/ppermute | solution.py:189
  31.4 0.0 copy-start.5
  31.4 0.0 collective-permute-done.1.far_a
  31.4 0.0 copy-start.6
  31.4 0.7 collective-permute-done.near
  32.1 0.0 copy-start.7
  32.1 0.0 copy-done.5
  32.1 0.0 copy-done.6
  32.1 0.6 copy-done.7
  32.8 11.6 %factor.1 = (bf16[7,128,128]{2,1,0:T(8,128)(2,1)}, f32[10,128,128]{2,1,0:T(8,128)}, f32[10,128,128]{2,1,0:T(8,128)}) custom-call(s32[1]{0:T(128)} %bitcast.rep, f32[7,128,128]{2,1,0:T(8,128)} %get-tuple-element.14.grams, f32[128,128]{1,0:T(8,128)} %get-tuple-element.15.own, f32[128,128]{1,0:T(8,128)} %copy-done.7, f32[128,128]{1,0:T(8,128)} %copy-done.6, ...), custom_call_target="tpu_custom_call" | custom-call | tf_op jit(solution)/shard_map/factor/pallas_call | solution.py:216
  44.4 2.7 %collective-permute-start.6 = (bf16[7,128,128]{2,1,0:T(8,128)(2,1)}, bf16[7,128,128]{2,1,0:T(8,128)(2,1)S(1)}, u32[]{:S(2)}, u32[]{:S(2)}) collective-permute-start(bf16[7,128,128]{2,1,0:T(8,128)(2,1)} %get-tuple-element.22.refs_2_), channel_id=1, source_target_pairs={{2,0},{3,1},{4,2},{5,3},{6,4},{7,5},{8,6},{9,7},{10,8},{11,9},{12,... | collective-permute-start | bytes 688136 | tf_op jit(solution)/shard_map/ppermute | solution.py:185
  47.1 2.6 %collective-permute-start.5 = (bf16[7,128,128]{2,1,0:T(8,128)(2,1)}, bf16[7,128,128]{2,1,0:T(8,128)(2,1)S(1)}, u32[]{:S(2)}, u32[]{:S(2)}) collective-permute-start(bf16[7,128,128]{2,1,0:T(8,128)(2,1)} %get-tuple-element.22.refs_2_), channel_id=1, source_target_pairs={{1,0},{2,1},{3,2},{4,3},{5,4},{6,5},{7,6},{8,7},{9,8},{10,9},{11,1... | collective-permute-start | bytes 688136 | tf_op jit(solution)/shard_map/ppermute | solution.py:185
  49.7 3.3 %collective-permute-start.4 = (bf16[7,128,128]{2,1,0:T(8,128)(2,1)}, bf16[7,128,128]{2,1,0:T(8,128)(2,1)S(1)}, u32[]{:S(2)}, u32[]{:S(2)}) collective-permute-start(bf16[7,128,128]{2,1,0:T(8,128)(2,1)} %get-tuple-element.22.refs_2_), channel_id=1, source_target_pairs={{0,1},{1,2},{2,3},{3,4},{4,5},{5,6},{6,7},{7,8},{8,9},{9,10},{10,1... | collective-permute-start | bytes 688136 | tf_op jit(solution)/shard_map/ppermute | solution.py:185
  53.0 2.3 %collective-permute-start.3 = (bf16[7,128,128]{2,1,0:T(8,128)(2,1)}, bf16[7,128,128]{2,1,0:T(8,128)(2,1)S(1)}, u32[]{:S(2)}, u32[]{:S(2)}) collective-permute-start(bf16[7,128,128]{2,1,0:T(8,128)(2,1)} %get-tuple-element.22.refs_2_), channel_id=1, source_target_pairs={{0,2},{1,3},{2,4},{3,5},{4,6},{5,7},{6,8},{7,9},{8,10},{9,11},{10,... | collective-permute-start | bytes 688136 | tf_op jit(solution)/shard_map/ppermute | solution.py:185
  55.3 0.0 copy-done.8
  55.3 0.5 fusion.col_at
  55.8 4.5 %finish.1 = (bf16[4,512,128]{2,1,0:T(8,128)(2,1)}, f32[7,128,128]{2,1,0:T(8,128)}, f32[2,32,128]{2,1,0:T(8,128)}, f32[1,32,128]{2,1,0:T(8,128)}) custom-call(s32[1]{0:T(128)} %bitcast.rep, bf16[4,512,128]{2,1,0:T(8,128)(2,1)} %basis.3, f32[7,128,128]{2,1,0:T(8,128)} %trans.3, f32[2,128,128]{2,1,0:T(8,128)} %trans_top.3, ...), custom_call_target="tpu_custom_call" | custom-call | tf_op jit(solution)/shard_map/finish/pallas_call | solution.py:233
  60.3 0.0 collective-permute-done.6.refs_4_
  60.3 0.0 copy-start.1
  60.3 0.0 collective-permute-done.5.refs_3_
  60.3 0.0 copy-start.2
  60.3 1.5 %collective-permute-done.4.refs_1_ = bf16[7,128,128]{2,1,0:T(8,128)(2,1)S(1)} collective-permute-done((bf16[7,128,128]{2,1,0:T(8,128)(2,1)}, bf16[7,128,128]{2,1,0:T(8,128)(2,1)S(1)}, u32[]{:S(2)}, u32[]{:S(2)}) %collective-permute-start.4) | collective-permute-done | bytes 229408 | tf_op jit(solution)/shard_map/ppermute | solution.py:185
  61.8 0.0 copy-start.3
  61.8 4.7 %collective-permute-done.3.refs_0_ = bf16[7,128,128]{2,1,0:T(8,128)(2,1)S(1)} collective-permute-done((bf16[7,128,128]{2,1,0:T(8,128)(2,1)}, bf16[7,128,128]{2,1,0:T(8,128)(2,1)S(1)}, u32[]{:S(2)}, u32[]{:S(2)}) %collective-permute-start.3) | collective-permute-done | bytes 229408 | tf_op jit(solution)/shard_map/ppermute | solution.py:185
  66.5 0.0 copy-start.4
  66.5 0.0 all-to-all-done.got
  66.6 0.0 copy-done.1
  66.6 0.0 copy-done.2
  66.6 0.0 copy-done.3
  66.6 0.7 copy-done.4
  67.3 0.0 copy-start
  67.3 1.3 %copy-done = bf16[4,16,128,128]{3,2,1,0:T(8,128)(2,1)} copy-done((bf16[4,16,128,128]{3,2,1,0:T(8,128)(2,1)}, bf16[4,16,128,128]{3,2,1,0:T(8,128)(2,1)S(1)}, u32[]{:S(2)}) %copy-start) | copy-done | bytes 2097176
  68.6 5.1 %project.1 = bf16[16,128,128]{2,1,0:T(8,128)(2,1)} custom-call(s32[16]{0:T(128)} %row_slot.1, s32[16]{0:T(128)} %fusion.col_at, bf16[4,16,128,128]{3,2,1,0:T(8,128)(2,1)} %copy-done, bf16[7,128,128]{2,1,0:T(8,128)(2,1)} %copy-done.4, bf16[7,128,128]{2,1,0:T(8,128)(2,1)} %copy-done.3, bf16[7,128,128]{2,1,0:T(8,128)(2,1)} %get-tuple-element.22.refs_2_, ...), custom_call_target="tpu_custom_call" | custom-call | tf_op jit(solution)/shard_map/project/pallas_call | solution.py:247
Async XLA Ops:
  0.6 54.7 %copy-start.8 = (s32[16]{0:T(128)S(1)}, s32[16]{0:T(128)}, u32[]{:S(2)}) copy-start(s32[16]{0:T(128)} %param.11) | copy-start | bytes 196
  0.6 65.9 %all-to-all-start = ((bf16[4,16,128,128]{3,2,1,0:T(8,128)(2,1)}), bf16[4,16,128,128]{3,2,1,0:T(8,128)(2,1)S(1)}, u32[]{:S(2)}, u32[]{:S(2)}) async-start(bf16[4,16,128,128]{3,2,1,0:T(8,128)(2,1)} %bitcast.2), calls=%async_computation | async-start | bytes 4194304 | tf_op jit(solution)/shard_map/all_to_all | solution.py:201
  8.7 22.8 %collective-permute-start.2 = (f32[128,128]{1,0:T(8,128)}, f32[128,128]{1,0:T(8,128)S(1)}, u32[]{:S(2)}, u32[]{:S(2)}) collective-permute-start(f32[128,128]{1,0:T(8,128)} %get-tuple-element.15.own), channel_id=1, source_target_pairs={{0,3},{1,2},{2,1},{3,0},{4,7},{5,6},{6,5},{7,4},{8,11},{9,10},{10,... | collective-permute-start | bytes 196616 | tf_op jit(solution)/shard_map/ppermute | solution.py:189
  10.1 21.3 %collective-permute-start.1 = (f32[128,128]{1,0:T(8,128)}, f32[128,128]{1,0:T(8,128)S(1)}, u32[]{:S(2)}, u32[]{:S(2)}) collective-permute-start(f32[128,128]{1,0:T(8,128)} %get-tuple-element.15.own), channel_id=1, source_target_pairs={{0,2},{1,3},{2,0},{3,1},{4,6},{5,7},{6,4},{7,5},{8,10},{9,11},{10,... | collective-permute-start | bytes 196616 | tf_op jit(solution)/shard_map/ppermute | solution.py:189
  11.6 20.6 %collective-permute-start = (f32[128,128]{1,0:T(8,128)}, f32[128,128]{1,0:T(8,128)S(1)}, u32[]{:S(2)}, u32[]{:S(2)}) collective-permute-start(f32[128,128]{1,0:T(8,128)} %get-tuple-element.15.own), channel_id=1, source_target_pairs={{0,1},{1,0},{2,3},{3,2},{4,5},{5,4},{6,7},{7,6},{8,9},{9,8},{10,11... | collective-permute-start | bytes 196616 | tf_op jit(solution)/shard_map/ppermute | solution.py:189
  31.4 0.7 copy-start.5
  31.4 0.7 copy-start.6
  32.1 0.6 copy-start.7
  44.4 15.9 %collective-permute-start.6 = (bf16[7,128,128]{2,1,0:T(8,128)(2,1)}, bf16[7,128,128]{2,1,0:T(8,128)(2,1)S(1)}, u32[]{:S(2)}, u32[]{:S(2)}) collective-permute-start(bf16[7,128,128]{2,1,0:T(8,128)(2,1)} %get-tuple-element.22.refs_2_), channel_id=1, source_target_pairs={{2,0},{3,1},{4,2},{5,3},{6,4},{7,5},{8,6},{9,7},{10,8},{11,9},{12,... | collective-permute-start | bytes 688136 | tf_op jit(solution)/shard_map/ppermute | solution.py:185
  47.1 13.2 %collective-permute-start.5 = (bf16[7,128,128]{2,1,0:T(8,128)(2,1)}, bf16[7,128,128]{2,1,0:T(8,128)(2,1)S(1)}, u32[]{:S(2)}, u32[]{:S(2)}) collective-permute-start(bf16[7,128,128]{2,1,0:T(8,128)(2,1)} %get-tuple-element.22.refs_2_), channel_id=1, source_target_pairs={{1,0},{2,1},{3,2},{4,3},{5,4},{6,5},{7,6},{8,7},{9,8},{10,9},{11,1... | collective-permute-start | bytes 688136 | tf_op jit(solution)/shard_map/ppermute | solution.py:185
  49.7 12.1 %collective-permute-start.4 = (bf16[7,128,128]{2,1,0:T(8,128)(2,1)}, bf16[7,128,128]{2,1,0:T(8,128)(2,1)S(1)}, u32[]{:S(2)}, u32[]{:S(2)}) collective-permute-start(bf16[7,128,128]{2,1,0:T(8,128)(2,1)} %get-tuple-element.22.refs_2_), channel_id=1, source_target_pairs={{0,1},{1,2},{2,3},{3,4},{4,5},{5,6},{6,7},{7,8},{8,9},{9,10},{10,1... | collective-permute-start | bytes 688136 | tf_op jit(solution)/shard_map/ppermute | solution.py:185
  53.0 13.6 %collective-permute-start.3 = (bf16[7,128,128]{2,1,0:T(8,128)(2,1)}, bf16[7,128,128]{2,1,0:T(8,128)(2,1)S(1)}, u32[]{:S(2)}, u32[]{:S(2)}) collective-permute-start(bf16[7,128,128]{2,1,0:T(8,128)(2,1)} %get-tuple-element.22.refs_2_), channel_id=1, source_target_pairs={{0,2},{1,3},{2,4},{3,5},{4,6},{5,7},{6,8},{7,9},{8,10},{9,11},{10,... | collective-permute-start | bytes 688136 | tf_op jit(solution)/shard_map/ppermute | solution.py:185
  60.3 6.3 %copy-start.1 = (bf16[7,128,128]{2,1,0:T(8,128)(2,1)}, bf16[7,128,128]{2,1,0:T(8,128)(2,1)S(1)}, u32[]{:S(2)}) copy-start(bf16[7,128,128]{2,1,0:T(8,128)(2,1)S(1)} %collective-permute-done.6.refs_4_) | copy-start | bytes 688132
  60.3 6.2 %copy-start.2 = (bf16[7,128,128]{2,1,0:T(8,128)(2,1)}, bf16[7,128,128]{2,1,0:T(8,128)(2,1)S(1)}, u32[]{:S(2)}) copy-start(bf16[7,128,128]{2,1,0:T(8,128)(2,1)S(1)} %collective-permute-done.5.refs_3_) | copy-start | bytes 688132
  61.8 4.7 %copy-start.3 = (bf16[7,128,128]{2,1,0:T(8,128)(2,1)}, bf16[7,128,128]{2,1,0:T(8,128)(2,1)S(1)}, u32[]{:S(2)}) copy-start(bf16[7,128,128]{2,1,0:T(8,128)(2,1)S(1)} %collective-permute-done.4.refs_1_) | copy-start | bytes 688132
  66.5 0.7 copy-start.4
  67.3 1.3 %copy-start = (bf16[4,16,128,128]{3,2,1,0:T(8,128)(2,1)}, bf16[4,16,128,128]{3,2,1,0:T(8,128)(2,1)S(1)}, u32[]{:S(2)}) copy-start(bf16[4,16,128,128]{3,2,1,0:T(8,128)(2,1)S(1)} %all-to-all-done.got) | copy-start | bytes 6291460
where the time goes:
time: 74.1 us; the launch traced here: 73.7 us
  waiting for transfers between devices  26.2 us (35%)
  Pallas kernels  25 us (34%)
  starting transfers between devices  18.6 us (25%)
  local copies, waits for them, and re-layouts  2.66 us (4%)
    ppermute x3, waiting for transfers between devices, swapped(): lax.ppermute(value, 'rep', [(i, i ^ flip) for i in range(lax.axis_size('r...  20 us
    pallas_call x1, Pallas kernels, per_device(): pl.pallas_call(factor_kernel, out_shape=[jax.ShapeDtypeStruct((slots, *sq...  11.6 us
    ppermute x4, starting transfers between devices, from_behind(): lax.ppermute(value, axis, [(source, source + steps) for source in range(l...  10.8 us
    ppermute x4, waiting for transfers between devices, from_behind(): lax.ppermute(value, axis, [(source, source + steps) for source in range(l...  6.23 us
    pallas_call x1, Pallas kernels, per_device(): pl.pallas_call(project_kernel, out_shape=jax.ShapeDtypeStruct((tiles, *sq...  5.09 us
    pallas_call x1, Pallas kernels, per_device(): pl.pallas_call(finish_kernel, out_shape=[jax.ShapeDtypeStruct(leaf_basis....  4.45 us
    all_to_all x1, starting transfers between devices, per_device(): lax.all_to_all(coupling_parts.reshape(reps, tiles, rank, rank), 'rep', 0,...  4.23 us
    pallas_call x1, Pallas kernels, per_device(): pl.pallas_call(gram_kernel, out_shape=[jax.ShapeDtypeStruct((slots, *squa...  3.78 us
  transfers between devices with their start and end apart: 8, of which 4 were waited for; matrix products, arithmetic and copies ran while one was open for 1% of the time, Pallas kernels for 27%

commit v1 on v0

--- a/solution.py
+++ b/solution.py
@@ -7,15 +7,18 @@
 from jax.experimental.pallas import tpu as pltpu
 from jax.sharding import PartitionSpec as P
 
+
 PTS = 512
 REACH = 2
 PANEL = 8
+TILE = 16
 ALL = ("leaf", "dom", "rep")
 F32 = jnp.float32
 BF16 = jnp.bfloat16
 VMEM = pl.BlockSpec(memory_space=pltpu.VMEM)
 SMEM = pl.BlockSpec(memory_space=pltpu.SMEM)
 ANY = pl.BlockSpec(memory_space=pl.ANY)
+PARAMS = pltpu.CompilerParams(vmem_limit_bytes=16 * 1024 * 1024)
 
 
 def dot_nn(a, b):
@@ -115,8 +118,11 @@
     sent[...] = congruence(grams[base], trans[base])
 
 
-def factor_kernel(rep, grams, own, near, far_a, far_b, trans_top, pool, upper, inverse, work):
+def factor_kernel(
+    rep, grams, own, near, far_a, far_b, trans_top, packed, pool, upper, inverse, work
+):
     slots = grams.shape[0]
+    size = grams.shape[1]
     high = rep[0] // 2
     mine = own[...] + near[...]
     other = far_a[...] + far_b[...]
@@ -128,6 +134,19 @@
     work[slots + 2] = congruence(three_a, trans_top[0]) + congruence(three_b, trans_top[1])
     factorize(work, upper, inverse, list(range(slots + 3)))
     pool[...] = upper[:slots].astype(BF16)
+    sub = lax.broadcasted_iota(jnp.int32, (size, size), 0)
+    lane = lax.broadcasted_iota(jnp.int32, (size, size), 1)
+    pairs = (slots + 1) // 2
+    for even in range(0, slots, 2):
+        square = upper[even]
+        if even + 1 < slots:
+            odd = upper[even + 1]
+            square = jnp.where(lane >= sub, square, odd.T)
+            diagonal = jnp.sum(jnp.where(lane == sub, odd, 0.0), axis=0, keepdims=True)
+            at = pairs * size + even // 2 * TILE
+            packed[at : at + TILE, :] = jnp.broadcast_to(diagonal, (TILE, size)).astype(BF16)
+        at = even // 2 * size
+        packed[at : at + size, :] = square.astype(BF16)
 
 
 def finish_kernel(rep, basis, trans, trans_top, upper, inverse, orth, fresh, top, four):
@@ -155,34 +174,81 @@
     four[0] = upper[three + 2, rows, :]
 
 
-def project_kernel(row_slot, col_at, got, *refs):
-    pieces, (out, pool, sem) = refs[: 2 * REACH + 1], refs[2 * REACH + 1 :]
-    slots = pieces[0].shape[0]
-    tiles = out.shape[0]
+def cut_kernel(rep, parts, lead, tail, sem):
+    me = rep[0]
     copies = [
-        pltpu.make_async_copy(piece, pool.at[pl.ds(i * slots, slots)], sem.at[i])
+        pltpu.make_async_copy(parts.at[me ^ flip, which], out.at[at], sem.at[2 * which + at])
+        for which, (out, flips) in enumerate(((lead, (1, 3)), (tail, (2, 3))))
+        for at, flip in enumerate(flips)
+    ]
+    for copy in copies:
+        copy.start()
+    for copy in copies:
+        copy.wait()
+
+
+def fold_kernel(rep, parts, lead, tail, lead_sum, tail_sum, own, sem):
+    me = rep[0]
+    copies = [
+        pltpu.make_async_copy(parts.at[me ^ flip, which], own.at[which], sem.at[which])
+        for which, flip in enumerate((2, 1))
+    ]
+    for copy in copies:
+        copy.start()
+    for which, (came, out) in enumerate(((lead, lead_sum), (tail, tail_sum))):
+        copies[which].wait()
+        out[...] = (came[1].astype(F32) + own[which].astype(F32)).astype(BF16)
+
+
+def half_kernel(rep, row_slot, parts, lead, tail, lead_rest, tail_rest, pool, half, own, sem):
+    copy = pltpu.make_async_copy(parts.at[rep[0]], own, sem)
+    copy.start()
+    copy.wait()
+    for which, (near, rest) in enumerate(((lead, lead_rest), (tail, tail_rest))):
+        for i in range(rest.shape[0]):
+            total = own[which, i].astype(F32) + near[0, i].astype(F32) + rest[i].astype(F32)
+            k = which * rest.shape[0] + i
+            half[k] = jnp.dot(
+                pool[row_slot[k]], total.astype(BF16), preferred_element_type=F32
+            ).astype(BF16)
+
+
+def project_kernel(slots, mine, col_node, half, *refs):
+    count = 2 * REACH + 1
+    pieces, (out, pool, sem) = refs[:count], refs[count:]
+    rows = pieces[0].shape[0]
+    size = out.shape[1]
+    copies = [
+        pltpu.make_async_copy(piece, pool.at[pl.ds(i * rows, rows)], sem.at[i])
         for i, piece in enumerate(pieces)
     ]
     for copy in copies:
         copy.start()
+    sub = lax.broadcasted_iota(jnp.int32, (size, size), 0)
+    lane = lax.broadcasted_iota(jnp.int32, (size, size), 1)
+    above = (lane >= sub).astype(F32).astype(BF16)
+    below = (lane < sub).astype(F32).astype(BF16)
+    eye = (lane == sub).astype(F32).astype(BF16)
+    pairs = (slots + 1) // 2
     for copy in copies:
         copy.wait()
-    for k in range(tiles):
-        total = got[0, k].astype(F32)
-        for i in range(1, got.shape[0]):
-            total = total + got[i, k].astype(F32)
-        half = jnp.dot(
-            pool[REACH * slots + row_slot[k]], total.astype(BF16), preferred_element_type=F32
-        ).astype(BF16)
-        out[k] = lax.dot_general(
-            half, pool[col_at[k]], (((1,), (1,)), ((), ())), preferred_element_type=F32
-        ).astype(BF16)
-
-
-def from_behind(value, axis, steps):
-    count = lax.axis_size(axis)
-    leading, last = (max(0, -steps), min(count, count - steps))
-    return lax.ppermute(value, axis, [(source, source + steps) for source in range(leading, last)])
+    for k in range(out.shape[0]):
+        piece, slot = col_node[k] // slots - mine[0] + REACH, col_node[k] % slots
+        base = piece * rows
+        square = pool[pl.ds(pl.multiple_of(base + slot // 2 * size, TILE), size), :]
+        spot = jnp.minimum(slot // 2, slots // 2 - 1)
+        at = pl.multiple_of(base + pairs * size + spot * TILE, TILE)
+        diagonal = jnp.concatenate([pool[pl.ds(at, TILE), :]] * (size // TILE), axis=0)
+        even = lax.dot_general(
+            half[k], square * above, (((1,), (1,)), ((), ())), preferred_element_type=F32
+        )
+        odd = jnp.dot(half[k], square * below + diagonal * eye, preferred_element_type=F32)
+        out[k] = jnp.where(slot % 2 == 0, even, odd).astype(BF16)
+
+
+def shifted(value, steps):
+    count = lax.axis_size(ALL)
+    return lax.ppermute(value, ALL, [(i, (i + steps) % count) for i in range(count)])
 
 
 def swapped(value, flip):
@@ -192,15 +258,10 @@
 def per_device(leaf_basis, transfer, transfer_top, coupling_parts, row_slot, col_node):
     rank = transfer.shape[1]
     slots = transfer.shape[0]
-    leaves = leaf_basis.shape[0]
     reps = lax.axis_size("rep")
     tiles = row_slot.shape[0]
     square = (rank, rank)
     rep = lax.axis_index("rep").astype(jnp.int32).reshape(1)
-
-    got = lax.all_to_all(
-        coupling_parts.reshape(reps, tiles, rank, rank), "rep", 0, 0, tiled=True
-    )
 
     grams, sent = pl.pallas_call(
         gram_kernel,
@@ -210,23 +271,52 @@
         ],
         in_specs=[VMEM, VMEM],
         out_specs=[VMEM, VMEM],
+        compiler_params=PARAMS,
         name="grams",
     )(leaf_basis, transfer)
     near, far_a, far_b = (swapped(sent, flip) for flip in (1, 2, 3))
-    pool, upper, inverse = pl.pallas_call(
+    parts = coupling_parts.reshape(reps, 2, tiles // 2, rank, rank)
+    pair = jax.ShapeDtypeStruct((2, tiles // 2, *square), BF16)
+    single = jax.ShapeDtypeStruct((tiles // 2, *square), BF16)
+    lead_out, tail_out = pl.pallas_call(
+        cut_kernel,
+        out_shape=[pair, pair],
+        in_specs=[SMEM, ANY],
+        out_specs=[VMEM, VMEM],
+        scratch_shapes=[pltpu.SemaphoreType.DMA((4,))],
+        compiler_params=PARAMS,
+        name="cut",
+    )(rep, parts)
+    lead = swapped(lead_out, 1)
+    tail = swapped(tail_out, 2)
+    lead_sum, tail_sum = pl.pallas_call(
+        fold_kernel,
+        out_shape=[single, single],
+        in_specs=[SMEM, ANY, VMEM, VMEM],
+        out_specs=[VMEM, VMEM],
+        scratch_shapes=[pltpu.VMEM(pair.shape, BF16), pltpu.SemaphoreType.DMA((2,))],
+        compiler_params=PARAMS,
+        name="fold",
+    )(rep, parts, lead, tail)
+    lead_rest = swapped(lead_sum, 2)
+    tail_rest = swapped(tail_sum, 1)
+    pairs = (slots + 1) // 2
+    packed, pool, upper, inverse = pl.pallas_call(
         factor_kernel,
         out_shape=[
+            jax.ShapeDtypeStruct((pairs * rank + slots // 2 * TILE, rank), BF16),
             jax.ShapeDtypeStruct((slots, *square), BF16),
             jax.ShapeDtypeStruct((slots + 3, *square), F32),
             jax.ShapeDtypeStruct((slots + 3, *square), F32),
         ],
         in_specs=[SMEM] + [VMEM] * 6,
-        out_specs=[VMEM] * 3,
+        out_specs=[VMEM] * 4,
         scratch_shapes=[pltpu.VMEM((slots + 3, *square), F32)],
+        compiler_params=PARAMS,
         name="factor",
     )(rep, grams, sent, near, far_a, far_b, transfer_top)
     pieces = [
-        pool if offset == 0 else from_behind(pool, ALL, -offset)
+        packed if offset == 0 else shifted(packed, -offset)
         for offset in range(-REACH, REACH + 1)
     ]
     share = rank // reps
@@ -240,21 +330,34 @@
         ],
         in_specs=[SMEM] + [VMEM] * 5,
         out_specs=[VMEM] * 4,
+        compiler_params=PARAMS,
         name="finish",
     )(rep, leaf_basis, transfer, transfer_top, upper, inverse)
-    my_index = lax.axis_index(ALL)
-    col_at = (col_node // slots - my_index + REACH) * slots + col_node % slots
-    projected = pl.pallas_call(
-        project_kernel,
+    half = pl.pallas_call(
+        half_kernel,
         out_shape=jax.ShapeDtypeStruct((tiles, *square), BF16),
-        in_specs=[SMEM] * 2 + [VMEM] + [ANY] * (2 * REACH + 1),
+        in_specs=[SMEM, SMEM, ANY] + [VMEM] * 5,
         out_specs=VMEM,
         scratch_shapes=[
-            pltpu.VMEM(((2 * REACH + 1) * slots, *square), BF16),
+            pltpu.VMEM((2, tiles // 2, *square), BF16),
+            pltpu.SemaphoreType.DMA,
+        ],
+        compiler_params=PARAMS,
+        name="half",
+    )(rep, row_slot, parts, lead, tail, lead_rest, tail_rest, pool)
+    mine = lax.axis_index(ALL).astype(jnp.int32).reshape(1)
+    projected = pl.pallas_call(
+        functools.partial(project_kernel, slots),
+        out_shape=jax.ShapeDtypeStruct((tiles, *square), BF16),
+        in_specs=[SMEM, SMEM, VMEM] + [ANY] * (2 * REACH + 1),
+        out_specs=VMEM,
+        scratch_shapes=[
+            pltpu.VMEM(((2 * REACH + 1) * packed.shape[0], rank), BF16),
             pltpu.SemaphoreType.DMA((2 * REACH + 1,)),
         ],
+        compiler_params=PARAMS,
         name="project",
-    )(row_slot, col_at, got, *pieces)
+    )(mine, col_node, half, *pieces)
     return (orth, fresh, top, four, projected)
 
 

time: 74.1 us -> 64 us (0.86)
  the two profiles are of different devices: /device:TPU:28 before, /device:TPU:0 now
where the time goes in v1:
time: 64 us; the launch traced here: 63.6 us
  Pallas kernels  21.7 us (34%)
  starting transfers between devices  17.1 us (27%)
  waiting for transfers between devices  15.6 us (24%)
  local copies, waits for them, and re-layouts  8.31 us (13%)
  between operations  0.94 us (1%)
    ppermute x7, waiting for transfers between devices, swapped(): lax.ppermute(value, 'rep', [(i, i ^ flip) for i in range(lax.axis_size('r...  15.5 us
    pallas_call x1, Pallas kernels, per_device(): pl.pallas_call(factor_kernel, out_shape=[jax.ShapeDtypeStruct((pairs * ra...  11.3 us
    ppermute x7, starting transfers between devices, swapped(): lax.ppermute(value, 'rep', [(i, i ^ flip) for i in range(lax.axis_size('r...  10.2 us
    unnamed x30, local copies, waits for them, and re-layouts  8.31 us
    ppermute x4, starting transfers between devices, shifted(): lax.ppermute(value, ALL, [(i, (i + steps) % count) for i in range(count)])  6.86 us
    pallas_call x1, Pallas kernels, per_device(): pl.pallas_call(functools.partial(project_kernel, slots), out_shape=jax.Sh...  3.17 us
    pallas_call x1, Pallas kernels, per_device(): pl.pallas_call(finish_kernel, out_shape=[jax.ShapeDtypeStruct(leaf_basis....  2.86 us
    pallas_call x1, Pallas kernels, per_device(): pl.pallas_call(gram_kernel, out_shape=[jax.ShapeDtypeStruct((slots, *squa...  1.97 us
  transfers between devices with their start and end apart: 11, of which 4 were waited for; matrix products, arithmetic and copies ran while one was open for 0% of the time, Pallas kernels for 28%

profile of v1, /device:TPU:0, one launch (start us, length us, event | category | flops | bytes accessed | tf_op | source)
XLA Modules:
  0.0 63.6 jit_solution(1643862010380623798)
XLA Ops:
  0.6 0.0 copy-start
  0.6 1.6 %copy-done = bf16[1,64,128,128]{3,2,1,0:T(8,128)(2,1)S(1)} copy-done((bf16[1,64,128,128]{3,2,1,0:T(8,128)(2,1)S(1)}, bf16[1,64,128,128]{3,2,1,0:T(8,128)(2,1)}, u32[]{:S(2)}) %copy-start) | copy-done | bytes 2097176
  2.2 0.1 cut.1
  2.4 0.0 copy-start.2
  2.4 0.0 copy-start.4
  2.4 0.0 copy-start.10
  2.4 3.0 %collective-permute-start.3 = (bf16[2,8,128,128]{3,2,1,0:T(8,128)(2,1)S(1)}, bf16[2,8,128,128]{3,2,1,0:T(8,128)(2,1)S(1)}, u32[]{:S(2)}, u32[]{:S(2)}) collective-permute-start(bf16[2,8,128,128]{3,2,1,0:T(8,128)(2,1)S(1)} %get-tuple-element.27), channel_id=1, source_target_pairs={{0,1},{1,0},{2,3},{3,2},{4,5},{5,4},{6,7},{7,6},{8,9},{9,8},{10,11... | collective-permute-start | bytes 1572872 | tf_op jit(solution)/shard_map/ppermute | solution.py:255
  5.4 1.5 %collective-permute-start.4 = (bf16[2,8,128,128]{3,2,1,0:T(8,128)(2,1)S(1)}, bf16[2,8,128,128]{3,2,1,0:T(8,128)(2,1)S(1)}, u32[]{:S(2)}, u32[]{:S(2)}) collective-permute-start(bf16[2,8,128,128]{3,2,1,0:T(8,128)(2,1)S(1)} %get-tuple-element.28), channel_id=1, source_target_pairs={{0,2},{1,3},{2,0},{3,1},{4,6},{5,7},{6,4},{7,5},{8,10},{9,11},{10,... | collective-permute-start | bytes 1572872 | tf_op jit(solution)/shard_map/ppermute | solution.py:255
  6.9 10.4 %collective-permute-done.3.lead = bf16[2,8,128,128]{3,2,1,0:T(8,128)(2,1)S(1)} collective-permute-done((bf16[2,8,128,128]{3,2,1,0:T(8,128)(2,1)S(1)}, bf16[2,8,128,128]{3,2,1,0:T(8,128)(2,1)S(1)}, u32[]{:S(2)}, u32[]{:S(2)}) %collective-permute-start.3) | collective-permute-done | bytes 524320 | tf_op jit(solution)/shard_map/ppermute | solution.py:255
  17.3 1.5 %collective-permute-done.4.tail = bf16[2,8,128,128]{3,2,1,0:T(8,128)(2,1)S(1)} collective-permute-done((bf16[2,8,128,128]{3,2,1,0:T(8,128)(2,1)S(1)}, bf16[2,8,128,128]{3,2,1,0:T(8,128)(2,1)S(1)}, u32[]{:S(2)}, u32[]{:S(2)}) %collective-permute-start.4) | collective-permute-done | bytes 524320 | tf_op jit(solution)/shard_map/ppermute | solution.py:255
  18.8 0.9 %fold.1 = (bf16[8,128,128]{2,1,0:T(8,128)(2,1)S(1)}, bf16[8,128,128]{2,1,0:T(8,128)(2,1)}) custom-call(s32[1]{0:T(128)} %bitcast.rep, bf16[4,2,8,128,128]{4,3,2,1,0:T(8,128)(2,1)S(1)} %bitcast.4, bf16[2,8,128,128]{3,2,1,0:T(8,128)(2,1)S(1)} %collective-permute-done.3.lead, bf16[2,8,128,128]{3,2,1,0:T(8,128)(2,1)S(1)} %collective-permute-done.4.tail), custom_call_target="tpu_custom_call" | custom-call | tf_op jit(solution)/shard_map/fold/pallas_call | solution.py:292
  19.7 1.6 %collective-permute-start.5 = (bf16[8,128,128]{2,1,0:T(8,128)(2,1)S(1)}, bf16[8,128,128]{2,1,0:T(8,128)(2,1)S(1)}, u32[]{:S(2)}, u32[]{:S(2)}) collective-permute-start(bf16[8,128,128]{2,1,0:T(8,128)(2,1)S(1)} %get-tuple-element.29), channel_id=1, source_target_pairs={{0,2},{1,3},{2,0},{3,1},{4,6},{5,7},{6,4},{7,5},{8,10},{9,11},{10,... | collective-permute-start | bytes 786440 | tf_op jit(solution)/shard_map/ppermute | solution.py:255
  21.3 0.0 copy-start.13
  21.3 0.0 copy-start.1
  21.3 0.5 collective-permute-start.6
  21.8 0.0 copy-done.2
  21.8 0.0 copy-done.4
  21.8 2.0 %grams.1 = (f32[7,128,128]{2,1,0:T(8,128)S(1)}, f32[128,128]{1,0:T(8,128)S(1)}) custom-call(bf16[4,512,128]{2,1,0:T(8,128)(2,1)S(1)} %copy-done.2, f32[7,128,128]{2,1,0:T(8,128)S(1)} %copy-done.4), custom_call_target="tpu_custom_call" | custom-call | tf_op jit(solution)/shard_map/grams/pallas_call | solution.py:266
  23.8 1.6 %collective-permute-start = (f32[128,128]{1,0:T(8,128)S(1)}, f32[128,128]{1,0:T(8,128)S(1)}, u32[]{:S(2)}, u32[]{:S(2)}) collective-permute-start(f32[128,128]{1,0:T(8,128)S(1)} %get-tuple-element.20.own), channel_id=1, source_target_pairs={{0,1},{1,0},{2,3},{3,2},{4,5},{5,4},{6,7},{7,6},{8,9},{9,8},{10,11... | collective-permute-start | bytes 196616 | tf_op jit(solution)/shard_map/ppermute | solution.py:255
  25.4 0.5 collective-permute-start.1
  25.9 1.5 %collective-permute-start.2 = (f32[128,128]{1,0:T(8,128)S(1)}, f32[128,128]{1,0:T(8,128)S(1)}, u32[]{:S(2)}, u32[]{:S(2)}) collective-permute-start(f32[128,128]{1,0:T(8,128)S(1)} %get-tuple-element.20.own), channel_id=1, source_target_pairs={{0,3},{1,2},{2,1},{3,0},{4,7},{5,6},{6,5},{7,4},{8,11},{9,10},{10,... | collective-permute-start | bytes 196616 | tf_op jit(solution)/shard_map/ppermute | solution.py:255
  27.4 2.9 %collective-permute-done.near = f32[128,128]{1,0:T(8,128)S(1)} collective-permute-done((f32[128,128]{1,0:T(8,128)S(1)}, f32[128,128]{1,0:T(8,128)S(1)}, u32[]{:S(2)}, u32[]{:S(2)}) %collective-permute-start) | collective-permute-done | bytes 65568 | tf_op jit(solution)/shard_map/ppermute | solution.py:255
  30.2 0.0 collective-permute-done.1.far_a
  30.2 0.8 %collective-permute-done.2.far_b = f32[128,128]{1,0:T(8,128)S(1)} collective-permute-done((f32[128,128]{1,0:T(8,128)S(1)}, f32[128,128]{1,0:T(8,128)S(1)}, u32[]{:S(2)}, u32[]{:S(2)}) %collective-permute-start.2) | collective-permute-done | bytes 65568 | tf_op jit(solution)/shard_map/ppermute | solution.py:255
  31.0 0.0 copy-done.10
  31.0 11.3 %factor.1 = (bf16[560,128]{1,0:T(8,128)(2,1)}, bf16[7,128,128]{2,1,0:T(8,128)(2,1)S(1)}, f32[10,128,128]{2,1,0:T(8,128)S(1)}, f32[10,128,128]{2,1,0:T(8,128)S(1)}) custom-call(s32[1]{0:T(128)} %bitcast.rep, f32[7,128,128]{2,1,0:T(8,128)S(1)} %get-tuple-element.19.grams, f32[128,128]{1,0:T(8,128)S(1)} %get-tuple-element.20.own, ...), custom_call_target="tpu_custom_call" | custom-call | tf_op jit(solution)/shard_map/factor/pallas_call | solution.py:304
  42.3 0.0 copy-start.6
  42.3 0.8 %copy-done.6 = f32[10,128,128]{2,1,0:T(8,128)} copy-done((f32[10,128,128]{2,1,0:T(8,128)}, f32[10,128,128]{2,1,0:T(8,128)S(1)}, u32[]{:S(2)}) %copy-start.6) | copy-done | bytes 655384
  43.2 0.0 copy-start.8
  43.2 0.9 %copy-done.8 = f32[10,128,128]{2,1,0:T(8,128)} copy-done((f32[10,128,128]{2,1,0:T(8,128)}, f32[10,128,128]{2,1,0:T(8,128)S(1)}, u32[]{:S(2)}) %copy-start.8) | copy-done | bytes 655384
  44.1 0.0 copy-start.11
  44.1 0.7 %copy-done.11 = bf16[7,128,128]{2,1,0:T(8,128)(2,1)} copy-done((bf16[7,128,128]{2,1,0:T(8,128)(2,1)}, bf16[7,128,128]{2,1,0:T(8,128)(2,1)S(1)}, u32[]{:S(2)}) %copy-start.11) | copy-done | bytes 229400
  44.8 1.5 %collective-permute-start.7 = (bf16[560,128]{1,0:T(8,128)(2,1)}, bf16[560,128]{1,0:T(8,128)(2,1)}, u32[]{:S(2)}, u32[]{:S(2)}) collective-permute-start(bf16[560,128]{1,0:T(8,128)(2,1)} %get-tuple-element.32.refs_2_), channel_id=1, source_target_pairs={{0,2},{1,3},{2,4},{3,5},{4,6},{5,7},{6,8},{7,9},{8,10},{9,11},{10,... | collective-permute-start | bytes 430088 | tf_op jit(solution)/shard_map/ppermute | solution.py:251
  46.3 0.5 collective-permute-start.8
  46.9 4.8 %collective-permute-start.9 = (bf16[560,128]{1,0:T(8,128)(2,1)}, bf16[560,128]{1,0:T(8,128)(2,1)}, u32[]{:S(2)}, u32[]{:S(2)}) collective-permute-start(bf16[560,128]{1,0:T(8,128)(2,1)} %get-tuple-element.32.refs_2_), channel_id=1, source_target_pairs={{0,31},{1,0},{2,1},{3,2},{4,3},{5,4},{6,5},{7,6},{8,7},{9,8},{10,9... | collective-permute-start | bytes 430088 | tf_op jit(solution)/shard_map/ppermute | solution.py:251
  51.7 0.0 collective-permute-done.5.lead_rest
  51.7 0.0 collective-permute-start.10
  51.7 0.0 copy-start.3
  51.7 1.0 %copy-done.3 = bf16[4,512,128]{2,1,0:T(8,128)(2,1)S(1)} copy-done((bf16[4,512,128]{2,1,0:T(8,128)(2,1)S(1)}, bf16[4,512,128]{2,1,0:T(8,128)(2,1)}, u32[]{:S(2)}) %copy-start.3) | copy-done | bytes 524312
  52.7 0.0 copy-start.5
  52.7 1.0 %copy-done.5 = f32[7,128,128]{2,1,0:T(8,128)S(1)} copy-done((f32[7,128,128]{2,1,0:T(8,128)S(1)}, f32[7,128,128]{2,1,0:T(8,128)}, u32[]{:S(2)}) %copy-start.5) | copy-done | bytes 458776
  53.7 0.0 copy-start.7
  53.7 1.1 %copy-done.7 = f32[10,128,128]{2,1,0:T(8,128)S(1)} copy-done((f32[10,128,128]{2,1,0:T(8,128)S(1)}, f32[10,128,128]{2,1,0:T(8,128)}, u32[]{:S(2)}) %copy-start.7) | copy-done | bytes 655384
  54.8 0.0 copy-start.9
  54.8 1.1 %copy-done.9 = f32[10,128,128]{2,1,0:T(8,128)S(1)} copy-done((f32[10,128,128]{2,1,0:T(8,128)S(1)}, f32[10,128,128]{2,1,0:T(8,128)}, u32[]{:S(2)}) %copy-start.9) | copy-done | bytes 655384
  55.9 0.0 copy-start.12
  55.9 2.9 %finish.1 = (bf16[4,512,128]{2,1,0:T(8,128)(2,1)}, f32[7,128,128]{2,1,0:T(8,128)}, f32[2,32,128]{2,1,0:T(8,128)}, f32[1,32,128]{2,1,0:T(8,128)}) custom-call(s32[1]{0:T(128)} %bitcast.rep, bf16[4,512,128]{2,1,0:T(8,128)(2,1)S(1)} %copy-done.3, f32[7,128,128]{2,1,0:T(8,128)S(1)} %copy-done.5, f32[2,128,128]{2,1,0:T(8,128)S(1)} %copy-done.10, ...), custom_call_target="tpu_custom_call" | custom-call | tf_op jit(solution)/shard_map/finish/pallas_call | solution.py:323
  58.8 0.0 collective-permute-done.6.tail_rest
  58.8 0.0 copy-done.13
  58.8 0.0 copy-done.1
  58.8 0.0 copy-done.12
  58.8 0.0 copy-start.14
  58.8 1.4 %half.1 = bf16[16,128,128]{2,1,0:T(8,128)(2,1)S(1)} custom-call(s32[1]{0:T(128)} %bitcast.rep, s32[16]{0:T(128)S(1)} %copy-done.13, bf16[4,2,8,128,128]{4,3,2,1,0:T(8,128)(2,1)S(1)} %bitcast.5, bf16[2,8,128,128]{3,2,1,0:T(8,128)(2,1)S(1)} %collective-permute-done.3.lead, bf16[2,8,128,128]{3,2,1,0:T(8,128)(2,1)S(1)} %collective-permute-done.4.tail, ...), custom_call_target="tpu_custom_call" | custom-call | tf_op jit(solution)/shard_map/half/pallas_call | solution.py:336
  60.2 0.0 collective-permute-done.7.refs_0_
  60.2 0.0 collective-permute-done.8.refs_1_
  60.2 0.0 collective-permute-done.9.refs_3_
  60.2 0.0 collective-permute-done.10.refs_4_
  60.2 0.0 copy-done.14
  60.3 3.2 %project.1 = bf16[16,128,128]{2,1,0:T(8,128)(2,1)} custom-call(s32[1]{0:T(128)} %bitcast.1.mine, s32[16]{0:T(128)S(1)} %copy-done.14, bf16[16,128,128]{2,1,0:T(8,128)(2,1)S(1)} %half.1, bf16[560,128]{1,0:T(8,128)(2,1)} %collective-permute-done.7.refs_0_, bf16[560,128]{1,0:T(8,128)(2,1)} %collective-permute-done.8.refs_1_, ...), custom_call_target="tpu_custom_call" | custom-call | tf_op jit(solution)/shard_map/project/pallas_call | solution.py:349
Async XLA Ops:
  0.6 1.6 %copy-start = (bf16[1,64,128,128]{3,2,1,0:T(8,128)(2,1)S(1)}, bf16[1,64,128,128]{3,2,1,0:T(8,128)(2,1)}, u32[]{:S(2)}) copy-start(bf16[1,64,128,128]{3,2,1,0:T(8,128)(2,1)} %param.9) | copy-start | bytes 6291460
  2.4 19.5 %copy-start.2 = (bf16[4,512,128]{2,1,0:T(8,128)(2,1)S(1)}, bf16[4,512,128]{2,1,0:T(8,128)(2,1)}, u32[]{:S(2)}) copy-start(bf16[4,512,128]{2,1,0:T(8,128)(2,1)} %basis.3) | copy-start | bytes 1572868
  2.4 19.5 %copy-start.4 = (f32[7,128,128]{2,1,0:T(8,128)S(1)}, f32[7,128,128]{2,1,0:T(8,128)}, u32[]{:S(2)}) copy-start(f32[7,128,128]{2,1,0:T(8,128)} %trans.3) | copy-start | bytes 1376260
  2.4 28.7 %copy-start.10 = (f32[2,128,128]{2,1,0:T(8,128)S(1)}, f32[2,128,128]{2,1,0:T(8,128)}, u32[]{:S(2)}) copy-start(f32[2,128,128]{2,1,0:T(8,128)} %trans_top.3) | copy-start | bytes 393220
  2.4 15.0 %collective-permute-start.3 = (bf16[2,8,128,128]{3,2,1,0:T(8,128)(2,1)S(1)}, bf16[2,8,128,128]{3,2,1,0:T(8,128)(2,1)S(1)}, u32[]{:S(2)}, u32[]{:S(2)}) collective-permute-start(bf16[2,8,128,128]{3,2,1,0:T(8,128)(2,1)S(1)} %get-tuple-element.27), channel_id=1, source_target_pairs={{0,1},{1,0},{2,3},{3,2},{4,5},{5,4},{6,7},{7,6},{8,9},{9,8},{10,11... | collective-permute-start | bytes 1572872 | tf_op jit(solution)/shard_map/ppermute | solution.py:255
  5.4 13.4 %collective-permute-start.4 = (bf16[2,8,128,128]{3,2,1,0:T(8,128)(2,1)S(1)}, bf16[2,8,128,128]{3,2,1,0:T(8,128)(2,1)S(1)}, u32[]{:S(2)}, u32[]{:S(2)}) collective-permute-start(bf16[2,8,128,128]{3,2,1,0:T(8,128)(2,1)S(1)} %get-tuple-element.28), channel_id=1, source_target_pairs={{0,2},{1,3},{2,0},{3,1},{4,6},{5,7},{6,4},{7,5},{8,10},{9,11},{10,... | collective-permute-start | bytes 1572872 | tf_op jit(solution)/shard_map/ppermute | solution.py:255
  19.7 32.0 %collective-permute-start.5 = (bf16[8,128,128]{2,1,0:T(8,128)(2,1)S(1)}, bf16[8,128,128]{2,1,0:T(8,128)(2,1)S(1)}, u32[]{:S(2)}, u32[]{:S(2)}) collective-permute-start(bf16[8,128,128]{2,1,0:T(8,128)(2,1)S(1)} %get-tuple-element.29), channel_id=1, source_target_pairs={{0,2},{1,3},{2,0},{3,1},{4,6},{5,7},{6,4},{7,5},{8,10},{9,11},{10,... | collective-permute-start | bytes 786440 | tf_op jit(solution)/shard_map/ppermute | solution.py:255
  21.3 37.5 %copy-start.13 = (s32[16]{0:T(128)S(1)}, s32[16]{0:T(128)}, u32[]{:S(2)}) copy-start(s32[16]{0:T(128)} %row_slot.1) | copy-start | bytes 196
  21.3 37.5 %copy-start.1 = (bf16[1,64,128,128]{3,2,1,0:T(8,128)(2,1)S(1)}, bf16[1,64,128,128]{3,2,1,0:T(8,128)(2,1)}, u32[]{:S(2)}) copy-start(bf16[1,64,128,128]{3,2,1,0:T(8,128)(2,1)} %param.9) | copy-start | bytes 6291460
  21.3 37.5 %collective-permute-start.6 = (bf16[8,128,128]{2,1,0:T(8,128)(2,1)}, bf16[8,128,128]{2,1,0:T(8,128)(2,1)}, u32[]{:S(2)}, u32[]{:S(2)}) collective-permute-start(bf16[8,128,128]{2,1,0:T(8,128)(2,1)} %get-tuple-element.30), channel_id=1, source_target_pairs={{0,1},{1,0},{2,3},{3,2},{4,5},{5,4},{6,7},{7,6},{8,9},{9,8},{10,11... | collective-permute-start | bytes 786440 | tf_op jit(solution)/shard_map/ppermute | solution.py:255
  23.8 6.4 %collective-permute-start = (f32[128,128]{1,0:T(8,128)S(1)}, f32[128,128]{1,0:T(8,128)S(1)}, u32[]{:S(2)}, u32[]{:S(2)}) collective-permute-start(f32[128,128]{1,0:T(8,128)S(1)} %get-tuple-element.20.own), channel_id=1, source_target_pairs={{0,1},{1,0},{2,3},{3,2},{4,5},{5,4},{6,7},{7,6},{8,9},{9,8},{10,11... | collective-permute-start | bytes 196616 | tf_op jit(solution)/shard_map/ppermute | solution.py:255
  25.4 4.9 %collective-permute-start.1 = (f32[128,128]{1,0:T(8,128)S(1)}, f32[128,128]{1,0:T(8,128)S(1)}, u32[]{:S(2)}, u32[]{:S(2)}) collective-permute-start(f32[128,128]{1,0:T(8,128)S(1)} %get-tuple-element.20.own), channel_id=1, source_target_pairs={{0,2},{1,3},{2,0},{3,1},{4,6},{5,7},{6,4},{7,5},{8,10},{9,11},{10,... | collective-permute-start | bytes 196616 | tf_op jit(solution)/shard_map/ppermute | solution.py:255
  25.9 5.2 %collective-permute-start.2 = (f32[128,128]{1,0:T(8,128)S(1)}, f32[128,128]{1,0:T(8,128)S(1)}, u32[]{:S(2)}, u32[]{:S(2)}) collective-permute-start(f32[128,128]{1,0:T(8,128)S(1)} %get-tuple-element.20.own), channel_id=1, source_target_pairs={{0,3},{1,2},{2,1},{3,0},{4,7},{5,6},{6,5},{7,4},{8,11},{9,10},{10,... | collective-permute-start | bytes 196616 | tf_op jit(solution)/shard_map/ppermute | solution.py:255
  42.3 0.8 %copy-start.6 = (f32[10,128,128]{2,1,0:T(8,128)}, f32[10,128,128]{2,1,0:T(8,128)S(1)}, u32[]{:S(2)}) copy-start(f32[10,128,128]{2,1,0:T(8,128)S(1)} %get-tuple-element.21.upper) | copy-start | bytes 1966084
  43.2 0.9 %copy-start.8 = (f32[10,128,128]{2,1,0:T(8,128)}, f32[10,128,128]{2,1,0:T(8,128)S(1)}, u32[]{:S(2)}) copy-start(f32[10,128,128]{2,1,0:T(8,128)S(1)} %get-tuple-element.22.inverse) | copy-start | bytes 1966084
  44.1 0.7 %copy-start.11 = (bf16[7,128,128]{2,1,0:T(8,128)(2,1)}, bf16[7,128,128]{2,1,0:T(8,128)(2,1)S(1)}, u32[]{:S(2)}) copy-start(bf16[7,128,128]{2,1,0:T(8,128)(2,1)S(1)} %get-tuple-element.31.pool) | copy-start | bytes 688132
  44.8 15.4 %collective-permute-start.7 = (bf16[560,128]{1,0:T(8,128)(2,1)}, bf16[560,128]{1,0:T(8,128)(2,1)}, u32[]{:S(2)}, u32[]{:S(2)}) collective-permute-start(bf16[560,128]{1,0:T(8,128)(2,1)} %get-tuple-element.32.refs_2_), channel_id=1, source_target_pairs={{0,2},{1,3},{2,4},{3,5},{4,6},{5,7},{6,8},{7,9},{8,10},{9,11},{10,... | collective-permute-start | bytes 430088 | tf_op jit(solution)/shard_map/ppermute | solution.py:251
  46.3 13.9 %collective-permute-start.8 = (bf16[560,128]{1,0:T(8,128)(2,1)}, bf16[560,128]{1,0:T(8,128)(2,1)}, u32[]{:S(2)}, u32[]{:S(2)}) collective-permute-start(bf16[560,128]{1,0:T(8,128)(2,1)} %get-tuple-element.32.refs_2_), channel_id=1, source_target_pairs={{0,1},{1,2},{2,3},{3,4},{4,5},{5,6},{6,7},{7,8},{8,9},{9,10},{10,1... | collective-permute-start | bytes 430088 | tf_op jit(solution)/shard_map/ppermute | solution.py:251
  46.9 13.4 %collective-permute-start.9 = (bf16[560,128]{1,0:T(8,128)(2,1)}, bf16[560,128]{1,0:T(8,128)(2,1)}, u32[]{:S(2)}, u32[]{:S(2)}) collective-permute-start(bf16[560,128]{1,0:T(8,128)(2,1)} %get-tuple-element.32.refs_2_), channel_id=1, source_target_pairs={{0,31},{1,0},{2,1},{3,2},{4,3},{5,4},{6,5},{7,6},{8,7},{9,8},{10,9... | collective-permute-start | bytes 430088 | tf_op jit(solution)/shard_map/ppermute | solution.py:251
  51.7 8.6 %collective-permute-start.10 = (bf16[560,128]{1,0:T(8,128)(2,1)}, bf16[560,128]{1,0:T(8,128)(2,1)}, u32[]{:S(2)}, u32[]{:S(2)}) collective-permute-start(bf16[560,128]{1,0:T(8,128)(2,1)} %get-tuple-element.32.refs_2_), channel_id=1, source_target_pairs={{0,30},{1,31},{2,0},{3,1},{4,2},{5,3},{6,4},{7,5},{8,6},{9,7},{10,... | collective-permute-start | bytes 430088 | tf_op jit(solution)/shard_map/ppermute | solution.py:251
  51.7 1.0 %copy-start.3 = (bf16[4,512,128]{2,1,0:T(8,128)(2,1)S(1)}, bf16[4,512,128]{2,1,0:T(8,128)(2,1)}, u32[]{:S(2)}) copy-start(bf16[4,512,128]{2,1,0:T(8,128)(2,1)} %basis.3) | copy-start | bytes 1572868
  52.7 1.0 %copy-start.5 = (f32[7,128,128]{2,1,0:T(8,128)S(1)}, f32[7,128,128]{2,1,0:T(8,128)}, u32[]{:S(2)}) copy-start(f32[7,128,128]{2,1,0:T(8,128)} %trans.3) | copy-start | bytes 1376260
  53.7 1.1 %copy-start.7 = (f32[10,128,128]{2,1,0:T(8,128)S(1)}, f32[10,128,128]{2,1,0:T(8,128)}, u32[]{:S(2)}) copy-start(f32[10,128,128]{2,1,0:T(8,128)} %copy-done.6) | copy-start | bytes 1966084
  54.8 1.1 %copy-start.9 = (f32[10,128,128]{2,1,0:T(8,128)S(1)}, f32[10,128,128]{2,1,0:T(8,128)}, u32[]{:S(2)}) copy-start(f32[10,128,128]{2,1,0:T(8,128)} %copy-done.8) | copy-start | bytes 1966084
  55.9 2.9 %copy-start.12 = (bf16[7,128,128]{2,1,0:T(8,128)(2,1)S(1)}, bf16[7,128,128]{2,1,0:T(8,128)(2,1)}, u32[]{:S(2)}) copy-start(bf16[7,128,128]{2,1,0:T(8,128)(2,1)} %copy-done.11) | copy-start | bytes 688132
  58.8 1.4 %copy-start.14 = (s32[16]{0:T(128)S(1)}, s32[16]{0:T(128)}, u32[]{:S(2)}) copy-start(s32[16]{0:T(128)} %col_node.1) | copy-start | bytes 196

commit v2 on v1

--- a/solution.py
+++ b/solution.py
@@ -100,26 +100,54 @@
                 work[m, stop:, :] = old - update[stop:, :]
 
 
-def gram_kernel(basis, trans, grams, sent):
+def start_all(moves, sems, first=0):
+    copies = [
+        pltpu.make_async_copy(source, target, sems.at[first + i])
+        for i, (source, target) in enumerate(moves)
+    ]
+    for copy in copies:
+        copy.start()
+    return copies
+
+
+def wait_all(copies):
+    for copy in copies:
+        copy.wait()
+
+
+def gram_kernel(rep, basis, trans, parts, grams, sent, lead, tail, rows, factors, sems):
+    me = rep[0]
     leaves = basis.shape[0]
+    came = start_all([(basis.at[i], rows.at[i]) for i in range(leaves)], sems)
+    ready = start_all([(trans, factors)], sems, leaves)
+    cut = start_all(
+        [
+            (parts.at[me ^ flip, which], out.at[at])
+            for which, (out, flips) in enumerate(((lead, (1, 3)), (tail, (2, 3))))
+            for at, flip in enumerate(flips)
+        ],
+        sems, leaves + 1,
+    )
     for i in range(leaves):
-        rows = basis[i]
+        came[i].wait()
         grams[i] = lax.dot_general(
-            rows, rows, (((0,), (0,)), ((), ())), preferred_element_type=F32
+            rows[i], rows[i], (((0,), (0,)), ((), ())), preferred_element_type=F32
         ) * (1.0 / PTS)
+    wait_all(ready)
     base, count = 0, leaves
     while count > 1:
         for pair in range(count // 2):
             one, two = base + 2 * pair, base + 2 * pair + 1
-            grams[base + count + pair] = congruence(grams[one], trans[one]) + congruence(
-                grams[two], trans[two]
+            grams[base + count + pair] = congruence(grams[one], factors[one]) + congruence(
+                grams[two], factors[two]
             )
         base, count = base + count, count // 2
-    sent[...] = congruence(grams[base], trans[base])
+    sent[...] = congruence(grams[base], factors[base])
+    wait_all(cut)
 
 
 def factor_kernel(
-    rep, grams, own, near, far_a, far_b, trans_top, packed, pool, upper, inverse, work
+    rep, grams, own, near, far_a, far_b, trans_top, packed, upper, inverse, work
 ):
     slots = grams.shape[0]
     size = grams.shape[1]
@@ -133,7 +161,6 @@
     work[slots + 1] = three_b
     work[slots + 2] = congruence(three_a, trans_top[0]) + congruence(three_b, trans_top[1])
     factorize(work, upper, inverse, list(range(slots + 3)))
-    pool[...] = upper[:slots].astype(BF16)
     sub = lax.broadcasted_iota(jnp.int32, (size, size), 0)
     lane = lax.broadcasted_iota(jnp.int32, (size, size), 1)
     pairs = (slots + 1) // 2
@@ -149,65 +176,66 @@
         packed[at : at + size, :] = square.astype(BF16)
 
 
-def finish_kernel(rep, basis, trans, trans_top, upper, inverse, orth, fresh, top, four):
-    leaves = basis.shape[0]
-    for i in range(leaves):
-        orth[i] = lax.dot_general(
-            basis[i], inverse[i].astype(BF16), (((1,), (1,)), ((), ())),
-            preferred_element_type=F32,
-        ).astype(BF16)
+def finish_kernel(
+    rep, basis, trans, trans_top, upper, inverse, orth, fresh, pool, top, four,
+    rows, factors, orth_held, fresh_held, sems,
+):
+    leaves, slots = basis.shape[0], trans.shape[0]
+    came = start_all([(trans, factors), (basis, rows)], sems)
+    pool[...] = upper[:slots].astype(BF16)
+    came[0].wait()
+    gone = []
     base, count = 0, leaves
     while count > 1:
         for child in range(count):
             node = base + child
-            fresh[node] = dot_nt(
-                dot_nn(upper[node], trans[node]), inverse[base + count + child // 2]
+            fresh_held[node] = dot_nt(
+                dot_nn(upper[node], factors[node]), inverse[base + count + child // 2]
             )
         base, count = base + count, count // 2
-    share = four.shape[1]
-    rows = pl.ds(pl.multiple_of(rep[0] * share, share), share)
     three = base + 1
     own_three = inverse[three + rep[0] // 2]
-    fresh[base] = dot_nt(dot_nn(upper[base], trans[base]), own_three)
+    fresh_held[base] = dot_nt(dot_nn(upper[base], factors[base]), own_three)
+    gone += start_all([(fresh_held, fresh)], sems, 2)
+    came[1].wait()
+    for i in range(leaves):
+        orth_held[i] = lax.dot_general(
+            rows[i], inverse[i].astype(BF16), (((1,), (1,)), ((), ())),
+            preferred_element_type=F32,
+        ).astype(BF16)
+        gone += start_all([(orth_held.at[i], orth.at[i])], sems, 3 + i)
+    share = four.shape[1]
+    part = pl.ds(pl.multiple_of(rep[0] * share, share), share)
     for c in range(2):
-        top[c] = dot_nt(dot_nn(upper[three + c, rows, :], trans_top[c]), inverse[three + 2])
-    four[0] = upper[three + 2, rows, :]
-
-
-def cut_kernel(rep, parts, lead, tail, sem):
+        top[c] = dot_nt(dot_nn(upper[three + c, part, :], trans_top[c]), inverse[three + 2])
+    four[0] = upper[three + 2, part, :]
+    wait_all(gone)
+
+
+def fold_kernel(rep, parts, lead, tail, lead_sum, tail_sum, kept, own, sems):
     me = rep[0]
-    copies = [
-        pltpu.make_async_copy(parts.at[me ^ flip, which], out.at[at], sem.at[2 * which + at])
-        for which, (out, flips) in enumerate(((lead, (1, 3)), (tail, (2, 3))))
-        for at, flip in enumerate(flips)
-    ]
-    for copy in copies:
-        copy.start()
-    for copy in copies:
-        copy.wait()
-
-
-def fold_kernel(rep, parts, lead, tail, lead_sum, tail_sum, own, sem):
-    me = rep[0]
-    copies = [
-        pltpu.make_async_copy(parts.at[me ^ flip, which], own.at[which], sem.at[which])
-        for which, flip in enumerate((2, 1))
-    ]
-    for copy in copies:
-        copy.start()
+    ready = start_all(
+        [
+            (parts.at[me ^ flip, which], own.at[at, which])
+            for at, flips in enumerate(((2, 1), (0, 0)))
+            for which, flip in enumerate(flips)
+        ],
+        sems,
+    )
     for which, (came, out) in enumerate(((lead, lead_sum), (tail, tail_sum))):
-        copies[which].wait()
-        out[...] = (came[1].astype(F32) + own[which].astype(F32)).astype(BF16)
-
-
-def half_kernel(rep, row_slot, parts, lead, tail, lead_rest, tail_rest, pool, half, own, sem):
-    copy = pltpu.make_async_copy(parts.at[rep[0]], own, sem)
-    copy.start()
-    copy.wait()
-    for which, (near, rest) in enumerate(((lead, lead_rest), (tail, tail_rest))):
-        for i in range(rest.shape[0]):
-            total = own[which, i].astype(F32) + near[0, i].astype(F32) + rest[i].astype(F32)
-            k = which * rest.shape[0] + i
+        ready[which].wait()
+        out[...] = (came[1].astype(F32) + own[0, which].astype(F32)).astype(BF16)
+    for which, came in enumerate((lead, tail)):
+        ready[2 + which].wait()
+        kept[which] = (came[0].astype(F32) + own[1, which].astype(F32)).astype(BF16)
+
+
+def half_kernel(row_slot, kept, lead_rest, tail_rest, pool, half):
+    tiles = lead_rest.shape[0]
+    for which, rest in enumerate((lead_rest, tail_rest)):
+        for i in range(tiles):
+            total = kept[which, i].astype(F32) + rest[i].astype(F32)
+            k = which * tiles + i
             half[k] = jnp.dot(
                 pool[row_slot[k]], total.astype(BF16), preferred_element_type=F32
             ).astype(BF16)
@@ -258,60 +286,66 @@
 def per_device(leaf_basis, transfer, transfer_top, coupling_parts, row_slot, col_node):
     rank = transfer.shape[1]
     slots = transfer.shape[0]
+    leaves = leaf_basis.shape[0]
     reps = lax.axis_size("rep")
     tiles = row_slot.shape[0]
     square = (rank, rank)
     rep = lax.axis_index("rep").astype(jnp.int32).reshape(1)
 
-    grams, sent = pl.pallas_call(
+    parts = coupling_parts.reshape(reps, 2, tiles // 2, rank, rank)
+    pair = jax.ShapeDtypeStruct((2, tiles // 2, *square), BF16)
+    single = jax.ShapeDtypeStruct((tiles // 2, *square), BF16)
+    leaf_basis, transfer, parts = (
+        pltpu.with_memory_space_constraint(value, pltpu.HBM)
+        for value in (leaf_basis, transfer, parts)
+    )
+    grams, sent, lead_out, tail_out = pl.pallas_call(
         gram_kernel,
         out_shape=[
             jax.ShapeDtypeStruct((slots, *square), F32),
             jax.ShapeDtypeStruct(square, F32),
-        ],
-        in_specs=[VMEM, VMEM],
-        out_specs=[VMEM, VMEM],
+            pair,
+            pair,
+        ],
+        in_specs=[SMEM] + [ANY] * 3,
+        out_specs=[VMEM] * 4,
+        scratch_shapes=[
+            pltpu.VMEM(leaf_basis.shape, BF16),
+            pltpu.VMEM(transfer.shape, F32),
+            pltpu.SemaphoreType.DMA((leaves + 5,)),
+        ],
         compiler_params=PARAMS,
         name="grams",
-    )(leaf_basis, transfer)
+    )(rep, leaf_basis, transfer, parts)
     near, far_a, far_b = (swapped(sent, flip) for flip in (1, 2, 3))
-    parts = coupling_parts.reshape(reps, 2, tiles // 2, rank, rank)
-    pair = jax.ShapeDtypeStruct((2, tiles // 2, *square), BF16)
-    single = jax.ShapeDtypeStruct((tiles // 2, *square), BF16)
-    lead_out, tail_out = pl.pallas_call(
-        cut_kernel,
-        out_shape=[pair, pair],
-        in_specs=[SMEM, ANY],
-        out_specs=[VMEM, VMEM],
-        scratch_shapes=[pltpu.SemaphoreType.DMA((4,))],
-        compiler_params=PARAMS,
-        name="cut",
-    )(rep, parts)
     lead = swapped(lead_out, 1)
     tail = swapped(tail_out, 2)
-    lead_sum, tail_sum = pl.pallas_call(
+    lead_sum, tail_sum, kept = pl.pallas_call(
         fold_kernel,
-        out_shape=[single, single],
+        out_shape=[single, single, pair],
         in_specs=[SMEM, ANY, VMEM, VMEM],
-        out_specs=[VMEM, VMEM],
-        scratch_shapes=[pltpu.VMEM(pair.shape, BF16), pltpu.SemaphoreType.DMA((2,))],
+        out_specs=[VMEM] * 3,
+        scratch_shapes=[
+            pltpu.VMEM((2, *pair.shape), BF16),
+            pltpu.SemaphoreType.DMA((4,)),
+        ],
         compiler_params=PARAMS,
         name="fold",
     )(rep, parts, lead, tail)
     lead_rest = swapped(lead_sum, 2)
     tail_rest = swapped(tail_sum, 1)
     pairs = (slots + 1) // 2
-    packed, pool, upper, inverse = pl.pallas_call(
+    nodes = (slots + 3, *square)
+    packed, upper, inverse = pl.pallas_call(
         factor_kernel,
         out_shape=[
             jax.ShapeDtypeStruct((pairs * rank + slots // 2 * TILE, rank), BF16),
-            jax.ShapeDtypeStruct((slots, *square), BF16),
-            jax.ShapeDtypeStruct((slots + 3, *square), F32),
-            jax.ShapeDtypeStruct((slots + 3, *square), F32),
+            jax.ShapeDtypeStruct(nodes, F32),
+            jax.ShapeDtypeStruct(nodes, F32),
         ],
         in_specs=[SMEM] + [VMEM] * 6,
-        out_specs=[VMEM] * 4,
-        scratch_shapes=[pltpu.VMEM((slots + 3, *square), F32)],
+        out_specs=[VMEM] * 3,
+        scratch_shapes=[pltpu.VMEM(nodes, F32)],
         compiler_params=PARAMS,
         name="factor",
     )(rep, grams, sent, near, far_a, far_b, transfer_top)
@@ -320,31 +354,35 @@
         for offset in range(-REACH, REACH + 1)
     ]
     share = rank // reps
-    orth, fresh, top, four = pl.pallas_call(
+    orth, fresh, pool, top, four = pl.pallas_call(
         finish_kernel,
         out_shape=[
             jax.ShapeDtypeStruct(leaf_basis.shape, BF16),
             jax.ShapeDtypeStruct(transfer.shape, F32),
+            jax.ShapeDtypeStruct((slots, *square), BF16),
             jax.ShapeDtypeStruct((2, share, rank), F32),
             jax.ShapeDtypeStruct((1, share, rank), F32),
         ],
-        in_specs=[SMEM] + [VMEM] * 5,
-        out_specs=[VMEM] * 4,
+        in_specs=[SMEM, ANY, ANY, VMEM, VMEM, VMEM],
+        out_specs=[ANY, ANY, VMEM, VMEM, VMEM],
+        scratch_shapes=[
+            pltpu.VMEM(leaf_basis.shape, BF16),
+            pltpu.VMEM(transfer.shape, F32),
+            pltpu.VMEM(leaf_basis.shape, BF16),
+            pltpu.VMEM(transfer.shape, F32),
+            pltpu.SemaphoreType.DMA((3 + leaves,)),
+        ],
         compiler_params=PARAMS,
         name="finish",
     )(rep, leaf_basis, transfer, transfer_top, upper, inverse)
     half = pl.pallas_call(
         half_kernel,
         out_shape=jax.ShapeDtypeStruct((tiles, *square), BF16),
-        in_specs=[SMEM, SMEM, ANY] + [VMEM] * 5,
+        in_specs=[SMEM] + [VMEM] * 4,
         out_specs=VMEM,
-        scratch_shapes=[
-            pltpu.VMEM((2, tiles // 2, *square), BF16),
-            pltpu.SemaphoreType.DMA,
-        ],
         compiler_params=PARAMS,
         name="half",
-    )(rep, row_slot, parts, lead, tail, lead_rest, tail_rest, pool)
+    )(row_slot, kept, lead_rest, tail_rest, pool)
     mine = lax.axis_index(ALL).astype(jnp.int32).reshape(1)
     projected = pl.pallas_call(
         functools.partial(project_kernel, slots),

time: 64 us -> 58.5 us (0.914)
  local copies, waits for them, and re-layouts: 8.31 us -> 0.02 us
  waiting for transfers between devices: 15.6 us -> 19.2 us
  starting transfers between devices: 17.1 us -> 14.3 us
  Pallas kernels: 21.7 us -> 24 us
    unnamed x30 -> x6, local copies, waits for them, and re-layouts: 8.31 us -> 0.02 us
    ppermute x4, starting transfers between devices: 6.86 us -> 4.11 us  [shifted(): lax.ppermute(value, ALL, [(i, (i + steps) % count) for i in range(count)])]
    ppermute x4, waiting for transfers between devices: 0.01 us -> 1.92 us  [shifted(): lax.ppermute(value, ALL, [(i, (i + steps) % count) for i in range(count)])]
    pallas_call x1, Pallas kernels: 2.86 us -> 4.64 us  [per_device(): pl.pallas_call(finish_kernel, out_shape=[jax.ShapeDtypeStruct(leaf_basis....]
    ppermute x7, waiting for transfers between devices: 15.5 us -> 17.3 us  [swapped(): lax.ppermute(value, 'rep', [(i, i ^ flip) for i in range(lax.axis_size('r...]
    pallas_call x1, Pallas kernels: 1.97 us -> 3.66 us  [per_device(): pl.pallas_call(gram_kernel, out_shape=[jax.ShapeDtypeStruct((slots, *squa...]
    pallas_call x1, Pallas kernels: 11.3 us -> 10.6 us  [per_device(): pl.pallas_call(factor_kernel, out_shape=[jax.ShapeDtypeStruct((pairs * ra...]
    pallas_call x2 -> x1, Pallas kernels: 1 us -> 1.28 us  [per_device(): pl.pallas_call(fold_kernel, out_shape=[single, single, pair], in_specs=[S...]
  transfers between devices with their start and end apart: 11 -> 11, of which waited for: 4 -> 5; matrix products, arithmetic and copies ran while one was open for 0% -> 0% of each run, Pallas kernels for 28% -> 28%
where the time goes in v2:
time: 58.5 us; the launch traced here: 58.4 us
  Pallas kernels  24 us (41%)
  waiting for transfers between devices  19.2 us (33%)
  starting transfers between devices  14.3 us (24%)
  between operations  0.89 us (2%)
    ppermute x7, waiting for transfers between devices, swapped(): lax.ppermute(value, 'rep', [(i, i ^ flip) for i in range(lax.axis_size('r...  17.3 us
    pallas_call x1, Pallas kernels, per_device(): pl.pallas_call(factor_kernel, out_shape=[jax.ShapeDtypeStruct((pairs * ra...  10.6 us
    ppermute x7, starting transfers between devices, swapped(): lax.ppermute(value, 'rep', [(i, i ^ flip) for i in range(lax.axis_size('r...  10.2 us
    pallas_call x1, Pallas kernels, per_device(): pl.pallas_call(finish_kernel, out_shape=[jax.ShapeDtypeStruct(leaf_basis....  4.64 us
    ppermute x4, starting transfers between devices, shifted(): lax.ppermute(value, ALL, [(i, (i + steps) % count) for i in range(count)])  4.11 us
    pallas_call x1, Pallas kernels, per_device(): pl.pallas_call(gram_kernel, out_shape=[jax.ShapeDtypeStruct((slots, *squa...  3.66 us
    pallas_call x1, Pallas kernels, per_device(): pl.pallas_call(functools.partial(project_kernel, slots), out_shape=jax.Sh...  2.94 us
    ppermute x4, waiting for transfers between devices, shifted(): lax.ppermute(value, ALL, [(i, (i + steps) % count) for i in range(count)])  1.92 us
  transfers between devices with their start and end apart: 11, of which 5 were waited for; matrix products, arithmetic and copies ran while one was open for 0% of the time, Pallas kernels for 28%

profile of v2, /device:TPU:0, one launch (start us, length us, event | category | flops | bytes accessed | tf_op | source)
XLA Modules:
  0.0 58.4 jit_solution(16771032251102009081)
XLA Ops:
  0.6 3.7 %grams.1 = (f32[7,128,128]{2,1,0:T(8,128)S(1)}, f32[128,128]{1,0:T(8,128)S(1)}, bf16[2,8,128,128]{3,2,1,0:T(8,128)(2,1)S(1)}, bf16[2,8,128,128]{3,2,1,0:T(8,128)(2,1)S(1)}) custom-call(s32[1]{0:T(128)} %bitcast.rep, bf16[4,512,128]{2,1,0:T(8,128)(2,1)} %basis.3, f32[7,128,128]{2,1,0:T(8,128)} %trans.3, bf16[4,2,8,128,128]{4,3,2,1,0:T(8,128)(2,1)} %bitcast.3), custom_call_target="tpu_custom_call" | custom-call | tf_op jit(solution)/shard_map/grams/pallas_call | solution.py:302
  4.3 0.0 copy-start
  4.3 3.0 %collective-permute-start.3 = (bf16[2,8,128,128]{3,2,1,0:T(8,128)(2,1)S(1)}, bf16[2,8,128,128]{3,2,1,0:T(8,128)(2,1)S(1)}, u32[]{:S(2)}, u32[]{:S(2)}) collective-permute-start(bf16[2,8,128,128]{3,2,1,0:T(8,128)(2,1)S(1)} %get-tuple-element.28), channel_id=1, source_target_pairs={{0,1},{1,0},{2,3},{3,2},{4,5},{5,4},{6,7},{7,6},{8,9},{9,8},{10,11... | collective-permute-start | bytes 1572872 | tf_op jit(solution)/shard_map/ppermute | solution.py:283
  7.3 1.5 %collective-permute-start.4 = (bf16[2,8,128,128]{3,2,1,0:T(8,128)(2,1)S(1)}, bf16[2,8,128,128]{3,2,1,0:T(8,128)(2,1)S(1)}, u32[]{:S(2)}, u32[]{:S(2)}) collective-permute-start(bf16[2,8,128,128]{3,2,1,0:T(8,128)(2,1)S(1)} %get-tuple-element.29), channel_id=1, source_target_pairs={{0,2},{1,3},{2,0},{3,1},{4,6},{5,7},{6,4},{7,5},{8,10},{9,11},{10,... | collective-permute-start | bytes 1572872 | tf_op jit(solution)/shard_map/ppermute | solution.py:283
  8.9 10.4 %collective-permute-done.3.lead = bf16[2,8,128,128]{3,2,1,0:T(8,128)(2,1)S(1)} collective-permute-done((bf16[2,8,128,128]{3,2,1,0:T(8,128)(2,1)S(1)}, bf16[2,8,128,128]{3,2,1,0:T(8,128)(2,1)S(1)}, u32[]{:S(2)}, u32[]{:S(2)}) %collective-permute-start.3) | collective-permute-done | bytes 524320 | tf_op jit(solution)/shard_map/ppermute | solution.py:283
  19.3 1.5 %collective-permute-done.4.tail = bf16[2,8,128,128]{3,2,1,0:T(8,128)(2,1)S(1)} collective-permute-done((bf16[2,8,128,128]{3,2,1,0:T(8,128)(2,1)S(1)}, bf16[2,8,128,128]{3,2,1,0:T(8,128)(2,1)S(1)}, u32[]{:S(2)}, u32[]{:S(2)}) %collective-permute-start.4) | collective-permute-done | bytes 524320 | tf_op jit(solution)/shard_map/ppermute | solution.py:283
  20.7 1.3 %fold.1 = (bf16[8,128,128]{2,1,0:T(8,128)(2,1)S(1)}, bf16[8,128,128]{2,1,0:T(8,128)(2,1)S(1)}, bf16[2,8,128,128]{3,2,1,0:T(8,128)(2,1)S(1)}) custom-call(s32[1]{0:T(128)} %bitcast.rep, bf16[4,2,8,128,128]{4,3,2,1,0:T(8,128)(2,1)} %bitcast.4, bf16[2,8,128,128]{3,2,1,0:T(8,128)(2,1)S(1)} %collective-permute-done.3.lead, ...), custom_call_target="tpu_custom_call" | custom-call | tf_op jit(solution)/shard_map/fold/pallas_call | solution.py:323
  22.0 0.0 copy-start.2
  22.0 1.6 %collective-permute-start.5 = (bf16[8,128,128]{2,1,0:T(8,128)(2,1)S(1)}, bf16[8,128,128]{2,1,0:T(8,128)(2,1)S(1)}, u32[]{:S(2)}, u32[]{:S(2)}) collective-permute-start(bf16[8,128,128]{2,1,0:T(8,128)(2,1)S(1)} %get-tuple-element.31), channel_id=1, source_target_pairs={{0,2},{1,3},{2,0},{3,1},{4,6},{5,7},{6,4},{7,5},{8,10},{9,11},{10,... | collective-permute-start | bytes 786440 | tf_op jit(solution)/shard_map/ppermute | solution.py:283
  23.6 0.5 collective-permute-start.6
  24.2 1.4 %collective-permute-start.2 = (f32[128,128]{1,0:T(8,128)S(1)}, f32[128,128]{1,0:T(8,128)S(1)}, u32[]{:S(2)}, u32[]{:S(2)}) collective-permute-start(f32[128,128]{1,0:T(8,128)S(1)} %get-tuple-element.21.own), channel_id=1, source_target_pairs={{0,3},{1,2},{2,1},{3,0},{4,7},{5,6},{6,5},{7,4},{8,11},{9,10},{10,... | collective-permute-start | bytes 196616 | tf_op jit(solution)/shard_map/ppermute | solution.py:283
  25.6 1.5 %collective-permute-start.1 = (f32[128,128]{1,0:T(8,128)S(1)}, f32[128,128]{1,0:T(8,128)S(1)}, u32[]{:S(2)}, u32[]{:S(2)}) collective-permute-start(f32[128,128]{1,0:T(8,128)S(1)} %get-tuple-element.21.own), channel_id=1, source_target_pairs={{0,2},{1,3},{2,0},{3,1},{4,6},{5,7},{6,4},{7,5},{8,10},{9,11},{10,... | collective-permute-start | bytes 196616 | tf_op jit(solution)/shard_map/ppermute | solution.py:283
  27.1 0.5 collective-permute-start
  27.6 4.7 %collective-permute-done.2.far_b = f32[128,128]{1,0:T(8,128)S(1)} collective-permute-done((f32[128,128]{1,0:T(8,128)S(1)}, f32[128,128]{1,0:T(8,128)S(1)}, u32[]{:S(2)}, u32[]{:S(2)}) %collective-permute-start.2) | collective-permute-done | bytes 65568 | tf_op jit(solution)/shard_map/ppermute | solution.py:283
  32.3 0.0 collective-permute-done.1.far_a
  32.3 0.8 %collective-permute-done.near = f32[128,128]{1,0:T(8,128)S(1)} collective-permute-done((f32[128,128]{1,0:T(8,128)S(1)}, f32[128,128]{1,0:T(8,128)S(1)}, u32[]{:S(2)}, u32[]{:S(2)}) %collective-permute-start) | collective-permute-done | bytes 65568 | tf_op jit(solution)/shard_map/ppermute | solution.py:283
  33.1 0.0 copy-done
  33.1 10.6 %factor.1 = (bf16[560,128]{1,0:T(8,128)(2,1)S(1)}, f32[10,128,128]{2,1,0:T(8,128)S(1)}, f32[10,128,128]{2,1,0:T(8,128)S(1)}) custom-call(s32[1]{0:T(128)} %bitcast.rep, f32[7,128,128]{2,1,0:T(8,128)S(1)} %get-tuple-element.20.grams, f32[128,128]{1,0:T(8,128)S(1)} %get-tuple-element.21.own, f32[128,128]{1,0:T(8,128)S(1)} %collective-permute-done.near, ...), custom_call_target="tpu_custom_call" | custom-call | tf_op jit(solution)/shard_map/factor/pallas_call | solution.py:339
  43.7 0.8 %collective-permute-start.10 = (bf16[560,128]{1,0:T(8,128)(2,1)S(1)}, bf16[560,128]{1,0:T(8,128)(2,1)S(1)}, u32[]{:S(2)}, u32[]{:S(2)}) collective-permute-start(bf16[560,128]{1,0:T(8,128)(2,1)S(1)} %get-tuple-element.34.refs_2_), channel_id=1, source_target_pairs={{0,30},{1,31},{2,0},{3,1},{4,2},{5,3},{6,4},{7,5},{8,6},{9,7},{10,... | collective-permute-start | bytes 430088 | tf_op jit(solution)/shard_map/ppermute | solution.py:279
  44.5 1.3 %collective-permute-start.9 = (bf16[560,128]{1,0:T(8,128)(2,1)S(1)}, bf16[560,128]{1,0:T(8,128)(2,1)S(1)}, u32[]{:S(2)}, u32[]{:S(2)}) collective-permute-start(bf16[560,128]{1,0:T(8,128)(2,1)S(1)} %get-tuple-element.34.refs_2_), channel_id=1, source_target_pairs={{0,31},{1,0},{2,1},{3,2},{4,3},{5,4},{6,5},{7,6},{8,7},{9,8},{10,9... | collective-permute-start | bytes 430088 | tf_op jit(solution)/shard_map/ppermute | solution.py:279
  45.7 0.7 %collective-permute-start.8 = (bf16[560,128]{1,0:T(8,128)(2,1)S(1)}, bf16[560,128]{1,0:T(8,128)(2,1)S(1)}, u32[]{:S(2)}, u32[]{:S(2)}) collective-permute-start(bf16[560,128]{1,0:T(8,128)(2,1)S(1)} %get-tuple-element.34.refs_2_), channel_id=1, source_target_pairs={{0,1},{1,2},{2,3},{3,4},{4,5},{5,6},{6,7},{7,8},{8,9},{9,10},{10,1... | collective-permute-start | bytes 430088 | tf_op jit(solution)/shard_map/ppermute | solution.py:279
  46.5 0.0 collective-permute-done.5.lead_rest
  46.5 1.3 %collective-permute-start.7 = (bf16[560,128]{1,0:T(8,128)(2,1)S(1)}, bf16[560,128]{1,0:T(8,128)(2,1)S(1)}, u32[]{:S(2)}, u32[]{:S(2)}) collective-permute-start(bf16[560,128]{1,0:T(8,128)(2,1)S(1)} %get-tuple-element.34.refs_2_), channel_id=1, source_target_pairs={{0,2},{1,3},{2,4},{3,5},{4,6},{5,7},{6,8},{7,9},{8,10},{9,11},{10,... | collective-permute-start | bytes 430088 | tf_op jit(solution)/shard_map/ppermute | solution.py:279
  47.8 0.0 copy-start.1
  47.8 4.6 %finish.1 = (bf16[4,512,128]{2,1,0:T(8,128)(2,1)}, f32[7,128,128]{2,1,0:T(8,128)}, bf16[7,128,128]{2,1,0:T(8,128)(2,1)S(1)}, f32[2,32,128]{2,1,0:T(8,128)}, f32[1,32,128]{2,1,0:T(8,128)}) custom-call(s32[1]{0:T(128)} %bitcast.rep, bf16[4,512,128]{2,1,0:T(8,128)(2,1)} %basis.3, f32[7,128,128]{2,1,0:T(8,128)} %trans.3, f32[2,128,128]{2,1,0:T(8,128)S(1)} %copy-done, ...), custom_call_target="tpu_custom_call" | custom-call | tf_op jit(solution)/shard_map/finish/pallas_call | solution.py:357
  52.5 0.0 collective-permute-done.6.tail_rest
  52.5 0.0 copy-done.2
  52.5 0.8 %half.1 = bf16[16,128,128]{2,1,0:T(8,128)(2,1)S(1)} custom-call(s32[16]{0:T(128)S(1)} %copy-done.2, bf16[2,8,128,128]{3,2,1,0:T(8,128)(2,1)S(1)} %get-tuple-element.30.kept, bf16[8,128,128]{2,1,0:T(8,128)(2,1)S(1)} %collective-permute-done.5.lead_rest, bf16[8,128,128]{2,1,0:T(8,128)(2,1)S(1)} %collective-permute-done.6.tail_rest, ...), custom_call_target="tpu_custom_call" | custom-call | tf_op jit(solution)/shard_map/half/pallas_call | solution.py:378
  53.3 0.0 collective-permute-done.10.refs_4_
  53.3 0.0 collective-permute-done.9.refs_3_
  53.4 1.9 %collective-permute-done.8.refs_1_ = bf16[560,128]{1,0:T(8,128)(2,1)S(1)} collective-permute-done((bf16[560,128]{1,0:T(8,128)(2,1)S(1)}, bf16[560,128]{1,0:T(8,128)(2,1)S(1)}, u32[]{:S(2)}, u32[]{:S(2)}) %collective-permute-start.8) | collective-permute-done | bytes 143392 | tf_op jit(solution)/shard_map/ppermute | solution.py:279
  55.3 0.0 collective-permute-done.7.refs_0_
  55.3 0.0 copy-done.1
  55.3 2.9 %project.1 = bf16[16,128,128]{2,1,0:T(8,128)(2,1)} custom-call(s32[1]{0:T(128)} %bitcast.2.mine, s32[16]{0:T(128)S(1)} %copy-done.1, bf16[16,128,128]{2,1,0:T(8,128)(2,1)S(1)} %half.1, bf16[560,128]{1,0:T(8,128)(2,1)S(1)} %collective-permute-done.7.refs_0_, bf16[560,128]{1,0:T(8,128)(2,1)S(1)} %collective-permute-done.8.refs_1_, ...), custom_call_target="tpu_custom_call" | custom-call | tf_op jit(solution)/shard_map/project/pallas_call | solution.py:387
Async XLA Ops:
  4.3 28.8 %copy-start = (f32[2,128,128]{2,1,0:T(8,128)S(1)}, f32[2,128,128]{2,1,0:T(8,128)}, u32[]{:S(2)}) copy-start(f32[2,128,128]{2,1,0:T(8,128)} %trans_top.3) | copy-start | bytes 393220
  4.3 15.0 %collective-permute-start.3 = (bf16[2,8,128,128]{3,2,1,0:T(8,128)(2,1)S(1)}, bf16[2,8,128,128]{3,2,1,0:T(8,128)(2,1)S(1)}, u32[]{:S(2)}, u32[]{:S(2)}) collective-permute-start(bf16[2,8,128,128]{3,2,1,0:T(8,128)(2,1)S(1)} %get-tuple-element.28), channel_id=1, source_target_pairs={{0,1},{1,0},{2,3},{3,2},{4,5},{5,4},{6,7},{7,6},{8,9},{9,8},{10,11... | collective-permute-start | bytes 1572872 | tf_op jit(solution)/shard_map/ppermute | solution.py:283
  7.3 13.4 %collective-permute-start.4 = (bf16[2,8,128,128]{3,2,1,0:T(8,128)(2,1)S(1)}, bf16[2,8,128,128]{3,2,1,0:T(8,128)(2,1)S(1)}, u32[]{:S(2)}, u32[]{:S(2)}) collective-permute-start(bf16[2,8,128,128]{3,2,1,0:T(8,128)(2,1)S(1)} %get-tuple-element.29), channel_id=1, source_target_pairs={{0,2},{1,3},{2,0},{3,1},{4,6},{5,7},{6,4},{7,5},{8,10},{9,11},{10,... | collective-permute-start | bytes 1572872 | tf_op jit(solution)/shard_map/ppermute | solution.py:283
  22.0 30.5 %copy-start.2 = (s32[16]{0:T(128)S(1)}, s32[16]{0:T(128)}, u32[]{:S(2)}) copy-start(s32[16]{0:T(128)} %row_slot.1) | copy-start | bytes 196
  22.0 24.5 %collective-permute-start.5 = (bf16[8,128,128]{2,1,0:T(8,128)(2,1)S(1)}, bf16[8,128,128]{2,1,0:T(8,128)(2,1)S(1)}, u32[]{:S(2)}, u32[]{:S(2)}) collective-permute-start(bf16[8,128,128]{2,1,0:T(8,128)(2,1)S(1)} %get-tuple-element.31), channel_id=1, source_target_pairs={{0,2},{1,3},{2,0},{3,1},{4,6},{5,7},{6,4},{7,5},{8,10},{9,11},{10,... | collective-permute-start | bytes 786440 | tf_op jit(solution)/shard_map/ppermute | solution.py:283
  23.6 28.8 %collective-permute-start.6 = (bf16[8,128,128]{2,1,0:T(8,128)(2,1)S(1)}, bf16[8,128,128]{2,1,0:T(8,128)(2,1)S(1)}, u32[]{:S(2)}, u32[]{:S(2)}) collective-permute-start(bf16[8,128,128]{2,1,0:T(8,128)(2,1)S(1)} %get-tuple-element.32), channel_id=1, source_target_pairs={{0,1},{1,0},{2,3},{3,2},{4,5},{5,4},{6,7},{7,6},{8,9},{9,8},{10,11... | collective-permute-start | bytes 786440 | tf_op jit(solution)/shard_map/ppermute | solution.py:283
  24.2 8.1 %collective-permute-start.2 = (f32[128,128]{1,0:T(8,128)S(1)}, f32[128,128]{1,0:T(8,128)S(1)}, u32[]{:S(2)}, u32[]{:S(2)}) collective-permute-start(f32[128,128]{1,0:T(8,128)S(1)} %get-tuple-element.21.own), channel_id=1, source_target_pairs={{0,3},{1,2},{2,1},{3,0},{4,7},{5,6},{6,5},{7,4},{8,11},{9,10},{10,... | collective-permute-start | bytes 196616 | tf_op jit(solution)/shard_map/ppermute | solution.py:283
  25.6 6.7 %collective-permute-start.1 = (f32[128,128]{1,0:T(8,128)S(1)}, f32[128,128]{1,0:T(8,128)S(1)}, u32[]{:S(2)}, u32[]{:S(2)}) collective-permute-start(f32[128,128]{1,0:T(8,128)S(1)} %get-tuple-element.21.own), channel_id=1, source_target_pairs={{0,2},{1,3},{2,0},{3,1},{4,6},{5,7},{6,4},{7,5},{8,10},{9,11},{10,... | collective-permute-start | bytes 196616 | tf_op jit(solution)/shard_map/ppermute | solution.py:283
  27.1 5.9 %collective-permute-start = (f32[128,128]{1,0:T(8,128)S(1)}, f32[128,128]{1,0:T(8,128)S(1)}, u32[]{:S(2)}, u32[]{:S(2)}) collective-permute-start(f32[128,128]{1,0:T(8,128)S(1)} %get-tuple-element.21.own), channel_id=1, source_target_pairs={{0,1},{1,0},{2,3},{3,2},{4,5},{5,4},{6,7},{7,6},{8,9},{9,8},{10,11... | collective-permute-start | bytes 196616 | tf_op jit(solution)/shard_map/ppermute | solution.py:283
  43.7 9.6 %collective-permute-start.10 = (bf16[560,128]{1,0:T(8,128)(2,1)S(1)}, bf16[560,128]{1,0:T(8,128)(2,1)S(1)}, u32[]{:S(2)}, u32[]{:S(2)}) collective-permute-start(bf16[560,128]{1,0:T(8,128)(2,1)S(1)} %get-tuple-element.34.refs_2_), channel_id=1, source_target_pairs={{0,30},{1,31},{2,0},{3,1},{4,2},{5,3},{6,4},{7,5},{8,6},{9,7},{10,... | collective-permute-start | bytes 430088 | tf_op jit(solution)/shard_map/ppermute | solution.py:279
  44.5 8.9 %collective-permute-start.9 = (bf16[560,128]{1,0:T(8,128)(2,1)S(1)}, bf16[560,128]{1,0:T(8,128)(2,1)S(1)}, u32[]{:S(2)}, u32[]{:S(2)}) collective-permute-start(bf16[560,128]{1,0:T(8,128)(2,1)S(1)} %get-tuple-element.34.refs_2_), channel_id=1, source_target_pairs={{0,31},{1,0},{2,1},{3,2},{4,3},{5,4},{6,5},{7,6},{8,7},{9,8},{10,9... | collective-permute-start | bytes 430088 | tf_op jit(solution)/shard_map/ppermute | solution.py:279
  45.7 9.5 %collective-permute-start.8 = (bf16[560,128]{1,0:T(8,128)(2,1)S(1)}, bf16[560,128]{1,0:T(8,128)(2,1)S(1)}, u32[]{:S(2)}, u32[]{:S(2)}) collective-permute-start(bf16[560,128]{1,0:T(8,128)(2,1)S(1)} %get-tuple-element.34.refs_2_), channel_id=1, source_target_pairs={{0,1},{1,2},{2,3},{3,4},{4,5},{5,6},{6,7},{7,8},{8,9},{9,10},{10,1... | collective-permute-start | bytes 430088 | tf_op jit(solution)/shard_map/ppermute | solution.py:279
  46.5 8.8 %collective-permute-start.7 = (bf16[560,128]{1,0:T(8,128)(2,1)S(1)}, bf16[560,128]{1,0:T(8,128)(2,1)S(1)}, u32[]{:S(2)}, u32[]{:S(2)}) collective-permute-start(bf16[560,128]{1,0:T(8,128)(2,1)S(1)} %get-tuple-element.34.refs_2_), channel_id=1, source_target_pairs={{0,2},{1,3},{2,4},{3,5},{4,6},{5,7},{6,8},{7,9},{8,10},{9,11},{10,... | collective-permute-start | bytes 430088 | tf_op jit(solution)/shard_map/ppermute | solution.py:279
  47.8 7.4 %copy-start.1 = (s32[16]{0:T(128)S(1)}, s32[16]{0:T(128)}, u32[]{:S(2)}) copy-start(s32[16]{0:T(128)} %col_node.1) | copy-start | bytes 196

commit v3 on v2

--- a/solution.py
+++ b/solution.py
@@ -53,7 +53,7 @@
     return high, mid, rest - mid
 
 
-def factorize(work, upper, inverse, mats):
+def factorize(work, joint, mats):
     size = work.shape[-1]
     shape = (PANEL, size)
     sub = lax.broadcasted_iota(jnp.int32, shape, 0)
@@ -84,8 +84,7 @@
                 pivot = row(both[t], j) * scale
                 both[t] = jnp.where(sub == j, pivot, both[t] - below * pivot)
         for t, m in enumerate(mats):
-            upper[m, start:stop, :] = jnp.where(lane >= sub + start, tops[t], 0.0)
-            inverse[m, start:stop, :] = jnp.where(lane < stop, both[t], 0.0)
+            joint[m, start:stop, :] = jnp.where(lane >= sub + start, tops[t], both[t])
             if stop < size:
                 high, mid, low = split3(both[t])
                 left = jnp.concatenate([high, high, mid, mid, high, low], axis=0)
@@ -115,7 +114,7 @@
         copy.wait()
 
 
-def gram_kernel(rep, basis, trans, parts, grams, sent, lead, tail, rows, factors, sems):
+def gram_kernel(rep, basis, trans, parts, grams, sent, lead, tail, add, rows, factors, sems):
     me = rep[0]
     leaves = basis.shape[0]
     came = start_all([(basis.at[i], rows.at[i]) for i in range(leaves)], sems)
@@ -127,6 +126,9 @@
             for at, flip in enumerate(flips)
         ],
         sems, leaves + 1,
+    )
+    cut += start_all(
+        [(parts.at[me ^ 2, 0], add.at[0]), (parts.at[me ^ 1, 1], add.at[1])], sems, leaves + 5
     )
     for i in range(leaves):
         came[i].wait()
@@ -147,7 +149,7 @@
 
 
 def factor_kernel(
-    rep, grams, own, near, far_a, far_b, trans_top, packed, upper, inverse, work
+    rep, grams, own, near, far_a, far_b, trans_top, packed, joint, work
 ):
     slots = grams.shape[0]
     size = grams.shape[1]
@@ -160,28 +162,40 @@
     work[slots] = three_a
     work[slots + 1] = three_b
     work[slots + 2] = congruence(three_a, trans_top[0]) + congruence(three_b, trans_top[1])
-    factorize(work, upper, inverse, list(range(slots + 3)))
+    factorize(work, joint, list(range(slots + 3)))
     sub = lax.broadcasted_iota(jnp.int32, (size, size), 0)
     lane = lax.broadcasted_iota(jnp.int32, (size, size), 1)
     pairs = (slots + 1) // 2
+    tile_row = lax.broadcasted_iota(jnp.int32, (TILE, size), 0)
+    diagonals = jnp.zeros((TILE, size), F32)
     for even in range(0, slots, 2):
-        square = upper[even]
+        square = joint[even]
         if even + 1 < slots:
-            odd = upper[even + 1]
+            odd = joint[even + 1]
             square = jnp.where(lane >= sub, square, odd.T)
             diagonal = jnp.sum(jnp.where(lane == sub, odd, 0.0), axis=0, keepdims=True)
-            at = pairs * size + even // 2 * TILE
-            packed[at : at + TILE, :] = jnp.broadcast_to(diagonal, (TILE, size)).astype(BF16)
+            diagonals = jnp.where(tile_row == even // 2, diagonal, diagonals)
+        else:
+            square = jnp.where(lane >= sub, square, 0.0)
         at = even // 2 * size
         packed[at : at + size, :] = square.astype(BF16)
+    packed[pairs * size :, :] = diagonals.astype(BF16)
 
 
 def finish_kernel(
-    rep, basis, trans, trans_top, upper, inverse, orth, fresh, pool, top, four,
-    rows, factors, orth_held, fresh_held, sems,
+    rep, basis, trans, trans_top, joint, parts, orth, fresh, pool, top, four, own,
+    rows, factors, upper, inverse, orth_held, fresh_held, sems,
 ):
     leaves, slots = basis.shape[0], trans.shape[0]
     came = start_all([(trans, factors), (basis, rows)], sems)
+    late = start_all([(parts.at[rep[0]], own)], sems, 3 + leaves)
+    square = joint.shape[1:]
+    sub = lax.broadcasted_iota(jnp.int32, square, 0)
+    lane = lax.broadcasted_iota(jnp.int32, square, 1)
+    for node in range(joint.shape[0]):
+        both = joint[node]
+        upper[node] = jnp.where(lane >= sub, both, 0.0)
+        inverse[node] = jnp.where(lane < sub, both, jnp.where(lane == sub, 1.0 / both, 0.0))
     pool[...] = upper[:slots].astype(BF16)
     came[0].wait()
     gone = []
@@ -209,32 +223,22 @@
     for c in range(2):
         top[c] = dot_nt(dot_nn(upper[three + c, part, :], trans_top[c]), inverse[three + 2])
     four[0] = upper[three + 2, part, :]
-    wait_all(gone)
-
-
-def fold_kernel(rep, parts, lead, tail, lead_sum, tail_sum, kept, own, sems):
-    me = rep[0]
-    ready = start_all(
-        [
-            (parts.at[me ^ flip, which], own.at[at, which])
-            for at, flips in enumerate(((2, 1), (0, 0)))
-            for which, flip in enumerate(flips)
-        ],
-        sems,
-    )
+    wait_all(gone + late)
+
+
+def fold_kernel(add, lead, tail, lead_sum, tail_sum, kept):
     for which, (came, out) in enumerate(((lead, lead_sum), (tail, tail_sum))):
-        ready[which].wait()
-        out[...] = (came[1].astype(F32) + own[0, which].astype(F32)).astype(BF16)
-    for which, came in enumerate((lead, tail)):
-        ready[2 + which].wait()
-        kept[which] = (came[0].astype(F32) + own[1, which].astype(F32)).astype(BF16)
-
-
-def half_kernel(row_slot, kept, lead_rest, tail_rest, pool, half):
+        out[...] = (came[1].astype(F32) + add[which].astype(F32)).astype(BF16)
+        kept[which] = came[0]
+
+
+def half_kernel(row_slot, own, kept, lead_rest, tail_rest, pool, half):
     tiles = lead_rest.shape[0]
     for which, rest in enumerate((lead_rest, tail_rest)):
         for i in range(tiles):
-            total = kept[which, i].astype(F32) + rest[i].astype(F32)
+            total = (
+                own[which, i].astype(F32) + kept[which, i].astype(F32) + rest[i].astype(F32)
+            )
             k = which * tiles + i
             half[k] = jnp.dot(
                 pool[row_slot[k]], total.astype(BF16), preferred_element_type=F32
@@ -243,35 +247,34 @@
 
 def project_kernel(slots, mine, col_node, half, *refs):
     count = 2 * REACH + 1
-    pieces, (out, pool, sem) = refs[:count], refs[count:]
+    pieces, (out, pool, held, sems) = refs[:count], refs[count:]
     rows = pieces[0].shape[0]
     size = out.shape[1]
-    copies = [
-        pltpu.make_async_copy(piece, pool.at[pl.ds(i * rows, rows)], sem.at[i])
-        for i, piece in enumerate(pieces)
-    ]
-    for copy in copies:
-        copy.start()
+    for i, piece in enumerate(pieces):
+        pool[i * rows : (i + 1) * rows, :] = piece[...]
     sub = lax.broadcasted_iota(jnp.int32, (size, size), 0)
     lane = lax.broadcasted_iota(jnp.int32, (size, size), 1)
+    tile_row = lax.broadcasted_iota(jnp.int32, (TILE, size), 0)
     above = (lane >= sub).astype(F32).astype(BF16)
     below = (lane < sub).astype(F32).astype(BF16)
     eye = (lane == sub).astype(F32).astype(BF16)
     pairs = (slots + 1) // 2
-    for copy in copies:
-        copy.wait()
+    gone = []
     for k in range(out.shape[0]):
         piece, slot = col_node[k] // slots - mine[0] + REACH, col_node[k] % slots
         base = piece * rows
         square = pool[pl.ds(pl.multiple_of(base + slot // 2 * size, TILE), size), :]
-        spot = jnp.minimum(slot // 2, slots // 2 - 1)
-        at = pl.multiple_of(base + pairs * size + spot * TILE, TILE)
-        diagonal = jnp.concatenate([pool[pl.ds(at, TILE), :]] * (size // TILE), axis=0)
+        tile = pool[pl.ds(pl.multiple_of(base + pairs * size, TILE), TILE), :].astype(F32)
+        diagonal = jnp.sum(jnp.where(tile_row == slot // 2, tile, 0.0), axis=0, keepdims=True)
+        spread = jnp.broadcast_to(diagonal, (size, size)).astype(BF16)
         even = lax.dot_general(
             half[k], square * above, (((1,), (1,)), ((), ())), preferred_element_type=F32
         )
-        odd = jnp.dot(half[k], square * below + diagonal * eye, preferred_element_type=F32)
-        out[k] = jnp.where(slot % 2 == 0, even, odd).astype(BF16)
+        odd = jnp.dot(half[k], square * below + spread * eye, preferred_element_type=F32)
+        held[k] = jnp.where(slot % 2 == 0, even, odd).astype(BF16)
+        if k % 4 == 3:
+            gone += start_all([(held.at[k - 3 : k + 1], out.at[k - 3 : k + 1])], sems, k // 4)
+    wait_all(gone)
 
 
 def shifted(value, steps):
@@ -299,62 +302,59 @@
         pltpu.with_memory_space_constraint(value, pltpu.HBM)
         for value in (leaf_basis, transfer, parts)
     )
-    grams, sent, lead_out, tail_out = pl.pallas_call(
+    grams, sent, lead_out, tail_out, add = pl.pallas_call(
         gram_kernel,
         out_shape=[
             jax.ShapeDtypeStruct((slots, *square), F32),
             jax.ShapeDtypeStruct(square, F32),
             pair,
             pair,
+            pair,
         ],
         in_specs=[SMEM] + [ANY] * 3,
-        out_specs=[VMEM] * 4,
+        out_specs=[VMEM] * 5,
         scratch_shapes=[
             pltpu.VMEM(leaf_basis.shape, BF16),
             pltpu.VMEM(transfer.shape, F32),
-            pltpu.SemaphoreType.DMA((leaves + 5,)),
+            pltpu.SemaphoreType.DMA((leaves + 7,)),
         ],
         compiler_params=PARAMS,
         name="grams",
     )(rep, leaf_basis, transfer, parts)
-    near, far_a, far_b = (swapped(sent, flip) for flip in (1, 2, 3))
+    far_b = swapped(sent, 3)
+    near, far_a = swapped(sent, 1), swapped(sent, 2)
     lead = swapped(lead_out, 1)
     tail = swapped(tail_out, 2)
+    pairs = (slots + 1) // 2
+    nodes = (slots + 3, *square)
+    packed, joint = pl.pallas_call(
+        factor_kernel,
+        out_shape=[
+            jax.ShapeDtypeStruct((pairs * rank + TILE, rank), BF16),
+            jax.ShapeDtypeStruct(nodes, F32),
+        ],
+        in_specs=[SMEM] + [VMEM] * 6,
+        out_specs=[VMEM] * 2,
+        scratch_shapes=[pltpu.VMEM(nodes, F32)],
+        compiler_params=PARAMS,
+        name="factor",
+    )(rep, grams, sent, near, far_a, far_b, transfer_top)
     lead_sum, tail_sum, kept = pl.pallas_call(
         fold_kernel,
         out_shape=[single, single, pair],
-        in_specs=[SMEM, ANY, VMEM, VMEM],
+        in_specs=[VMEM] * 3,
         out_specs=[VMEM] * 3,
-        scratch_shapes=[
-            pltpu.VMEM((2, *pair.shape), BF16),
-            pltpu.SemaphoreType.DMA((4,)),
-        ],
         compiler_params=PARAMS,
         name="fold",
-    )(rep, parts, lead, tail)
+    )(add, lead, tail)
     lead_rest = swapped(lead_sum, 2)
     tail_rest = swapped(tail_sum, 1)
-    pairs = (slots + 1) // 2
-    nodes = (slots + 3, *square)
-    packed, upper, inverse = pl.pallas_call(
-        factor_kernel,
-        out_shape=[
-            jax.ShapeDtypeStruct((pairs * rank + slots // 2 * TILE, rank), BF16),
-            jax.ShapeDtypeStruct(nodes, F32),
-            jax.ShapeDtypeStruct(nodes, F32),
-        ],
-        in_specs=[SMEM] + [VMEM] * 6,
-        out_specs=[VMEM] * 3,
-        scratch_shapes=[pltpu.VMEM(nodes, F32)],
-        compiler_params=PARAMS,
-        name="factor",
-    )(rep, grams, sent, near, far_a, far_b, transfer_top)
     pieces = [
         packed if offset == 0 else shifted(packed, -offset)
         for offset in range(-REACH, REACH + 1)
     ]
     share = rank // reps
-    orth, fresh, pool, top, four = pl.pallas_call(
+    orth, fresh, pool, top, four, own = pl.pallas_call(
         finish_kernel,
         out_shape=[
             jax.ShapeDtypeStruct(leaf_basis.shape, BF16),
@@ -362,36 +362,40 @@
             jax.ShapeDtypeStruct((slots, *square), BF16),
             jax.ShapeDtypeStruct((2, share, rank), F32),
             jax.ShapeDtypeStruct((1, share, rank), F32),
-        ],
-        in_specs=[SMEM, ANY, ANY, VMEM, VMEM, VMEM],
-        out_specs=[ANY, ANY, VMEM, VMEM, VMEM],
+            pair,
+        ],
+        in_specs=[SMEM, ANY, ANY, VMEM, VMEM, ANY],
+        out_specs=[ANY, ANY, VMEM, VMEM, VMEM, VMEM],
         scratch_shapes=[
             pltpu.VMEM(leaf_basis.shape, BF16),
             pltpu.VMEM(transfer.shape, F32),
+            pltpu.VMEM(nodes, F32),
+            pltpu.VMEM(nodes, F32),
             pltpu.VMEM(leaf_basis.shape, BF16),
             pltpu.VMEM(transfer.shape, F32),
-            pltpu.SemaphoreType.DMA((3 + leaves,)),
+            pltpu.SemaphoreType.DMA((4 + leaves,)),
         ],
         compiler_params=PARAMS,
         name="finish",
-    )(rep, leaf_basis, transfer, transfer_top, upper, inverse)
+    )(rep, leaf_basis, transfer, transfer_top, joint, parts)
     half = pl.pallas_call(
         half_kernel,
         out_shape=jax.ShapeDtypeStruct((tiles, *square), BF16),
-        in_specs=[SMEM] + [VMEM] * 4,
+        in_specs=[SMEM] + [VMEM] * 5,
         out_specs=VMEM,
         compiler_params=PARAMS,
         name="half",
-    )(row_slot, kept, lead_rest, tail_rest, pool)
+    )(row_slot, own, kept, lead_rest, tail_rest, pool)
     mine = lax.axis_index(ALL).astype(jnp.int32).reshape(1)
     projected = pl.pallas_call(
         functools.partial(project_kernel, slots),
         out_shape=jax.ShapeDtypeStruct((tiles, *square), BF16),
-        in_specs=[SMEM, SMEM, VMEM] + [ANY] * (2 * REACH + 1),
-        out_specs=VMEM,
+        in_specs=[SMEM, SMEM, VMEM] + [VMEM] * (2 * REACH + 1),
+        out_specs=ANY,
         scratch_shapes=[
             pltpu.VMEM(((2 * REACH + 1) * packed.shape[0], rank), BF16),
-            pltpu.SemaphoreType.DMA((2 * REACH + 1,)),
+            pltpu.VMEM((tiles, *square), BF16),
+            pltpu.SemaphoreType.DMA((tiles // 4,)),
         ],
         compiler_params=PARAMS,
         name="project",

time: 58.5 us -> 56.2 us (0.961)
  Pallas kernels: 24 us -> 21.9 us
    pallas_call x1, Pallas kernels: 1.28 us -> 0.13 us  [per_device(): pl.pallas_call(fold_kernel, out_shape=[single, single, pair], in_specs=[V...]
    pallas_call x1, Pallas kernels: 2.94 us -> 1.9 us  [per_device(): pl.pallas_call(functools.partial(project_kernel, slots), out_shape=jax.Sh...]
  transfers between devices with their start and end apart: 11 -> 11, of which waited for: 5 -> 5; matrix products, arithmetic and copies ran while one was open for 0% -> 0% of each run, Pallas kernels for 28% -> 29%
where the time goes in v3:
time: 56.2 us; the launch traced here: 56 us
  Pallas kernels  21.9 us (39%)
  waiting for transfers between devices  18.9 us (34%)
  starting transfers between devices  14.3 us (25%)
  between operations  0.89 us (2%)
    ppermute x7, waiting for transfers between devices, swapped(): lax.ppermute(value, 'rep', [(i, i ^ flip) for i in range(lax.axis_size('r...  17.3 us
    pallas_call x1, Pallas kernels, per_device(): pl.pallas_call(factor_kernel, out_shape=[jax.ShapeDtypeStruct((pairs * ra...  10.6 us
    ppermute x7, starting transfers between devices, swapped(): lax.ppermute(value, 'rep', [(i, i ^ flip) for i in range(lax.axis_size('r...  10.2 us
    pallas_call x1, Pallas kernels, per_device(): pl.pallas_call(finish_kernel, out_shape=[jax.ShapeDtypeStruct(leaf_basis....  4.63 us
    ppermute x4, starting transfers between devices, shifted(): lax.ppermute(value, ALL, [(i, (i + steps) % count) for i in range(count)])  4.11 us
    pallas_call x1, Pallas kernels, per_device(): pl.pallas_call(gram_kernel, out_shape=[jax.ShapeDtypeStruct((slots, *squa...  3.71 us
    pallas_call x1, Pallas kernels, per_device(): pl.pallas_call(functools.partial(project_kernel, slots), out_shape=jax.Sh...  1.9 us
    ppermute x4, waiting for transfers between devices, shifted(): lax.ppermute(value, ALL, [(i, (i + steps) % count) for i in range(count)])  1.66 us
  transfers between devices with their start and end apart: 11, of which 5 were waited for; matrix products, arithmetic and copies ran while one was open for 0% of the time, Pallas kernels for 29%

profile of v3, /device:TPU:0, one launch (start us, length us, event | category | flops | bytes accessed | tf_op | source)
XLA Modules:
  0.0 56.0 jit_solution(5945705935057351302)
XLA Ops:
  0.6 0.0 copy-start
  0.6 3.7 %grams.1 = (f32[7,128,128]{2,1,0:T(8,128)S(1)}, f32[128,128]{1,0:T(8,128)S(1)}, bf16[2,8,128,128]{3,2,1,0:T(8,128)(2,1)S(1)}, bf16[2,8,128,128]{3,2,1,0:T(8,128)(2,1)S(1)}, bf16[2,8,128,128]{3,2,1,0:T(8,128)(2,1)S(1)}) custom-call(s32[1]{0:T(128)} %bitcast.rep, bf16[4,512,128]{2,1,0:T(8,128)(2,1)} %basis.3, f32[7,128,128]{2,1,0:T(8,128)} %trans.3, ...), custom_call_target="tpu_custom_call" | custom-call | tf_op jit(solution)/shard_map/grams/pallas_call | solution.py:305
  4.4 3.0 %collective-permute-start.3 = (bf16[2,8,128,128]{3,2,1,0:T(8,128)(2,1)S(1)}, bf16[2,8,128,128]{3,2,1,0:T(8,128)(2,1)S(1)}, u32[]{:S(2)}, u32[]{:S(2)}) collective-permute-start(bf16[2,8,128,128]{3,2,1,0:T(8,128)(2,1)S(1)} %get-tuple-element.30), channel_id=1, source_target_pairs={{0,1},{1,0},{2,3},{3,2},{4,5},{5,4},{6,7},{7,6},{8,9},{9,8},{10,11... | collective-permute-start | bytes 1572872 | tf_op jit(solution)/shard_map/ppermute | solution.py:286
  7.4 1.5 %collective-permute-start.4 = (bf16[2,8,128,128]{3,2,1,0:T(8,128)(2,1)S(1)}, bf16[2,8,128,128]{3,2,1,0:T(8,128)(2,1)S(1)}, u32[]{:S(2)}, u32[]{:S(2)}) collective-permute-start(bf16[2,8,128,128]{3,2,1,0:T(8,128)(2,1)S(1)} %get-tuple-element.31), channel_id=1, source_target_pairs={{0,2},{1,3},{2,0},{3,1},{4,6},{5,7},{6,4},{7,5},{8,10},{9,11},{10,... | collective-permute-start | bytes 1572872 | tf_op jit(solution)/shard_map/ppermute | solution.py:286
  8.9 10.4 %collective-permute-done.3.lead = bf16[2,8,128,128]{3,2,1,0:T(8,128)(2,1)S(1)} collective-permute-done((bf16[2,8,128,128]{3,2,1,0:T(8,128)(2,1)S(1)}, bf16[2,8,128,128]{3,2,1,0:T(8,128)(2,1)S(1)}, u32[]{:S(2)}, u32[]{:S(2)}) %collective-permute-start.3) | collective-permute-done | bytes 524320 | tf_op jit(solution)/shard_map/ppermute | solution.py:286
  19.3 1.5 %collective-permute-done.4.tail = bf16[2,8,128,128]{3,2,1,0:T(8,128)(2,1)S(1)} collective-permute-done((bf16[2,8,128,128]{3,2,1,0:T(8,128)(2,1)S(1)}, bf16[2,8,128,128]{3,2,1,0:T(8,128)(2,1)S(1)}, u32[]{:S(2)}, u32[]{:S(2)}) %collective-permute-start.4) | collective-permute-done | bytes 524320 | tf_op jit(solution)/shard_map/ppermute | solution.py:286
  20.8 0.1 fold.1
  20.9 1.6 %collective-permute-start.5 = (bf16[8,128,128]{2,1,0:T(8,128)(2,1)S(1)}, bf16[8,128,128]{2,1,0:T(8,128)(2,1)S(1)}, u32[]{:S(2)}, u32[]{:S(2)}) collective-permute-start(bf16[8,128,128]{2,1,0:T(8,128)(2,1)S(1)} %get-tuple-element.33), channel_id=1, source_target_pairs={{0,2},{1,3},{2,0},{3,1},{4,6},{5,7},{6,4},{7,5},{8,10},{9,11},{10,... | collective-permute-start | bytes 786440 | tf_op jit(solution)/shard_map/ppermute | solution.py:286
  22.5 0.5 collective-permute-start.6
  23.0 1.4 %collective-permute-start.2 = (f32[128,128]{1,0:T(8,128)S(1)}, f32[128,128]{1,0:T(8,128)S(1)}, u32[]{:S(2)}, u32[]{:S(2)}) collective-permute-start(f32[128,128]{1,0:T(8,128)S(1)} %get-tuple-element.22.own), channel_id=1, source_target_pairs={{0,3},{1,2},{2,1},{3,0},{4,7},{5,6},{6,5},{7,4},{8,11},{9,10},{10,... | collective-permute-start | bytes 196616 | tf_op jit(solution)/shard_map/ppermute | solution.py:286
  24.5 1.5 %collective-permute-start.1 = (f32[128,128]{1,0:T(8,128)S(1)}, f32[128,128]{1,0:T(8,128)S(1)}, u32[]{:S(2)}, u32[]{:S(2)}) collective-permute-start(f32[128,128]{1,0:T(8,128)S(1)} %get-tuple-element.22.own), channel_id=1, source_target_pairs={{0,2},{1,3},{2,0},{3,1},{4,6},{5,7},{6,4},{7,5},{8,10},{9,11},{10,... | collective-permute-start | bytes 196616 | tf_op jit(solution)/shard_map/ppermute | solution.py:286
  26.0 0.5 collective-permute-start
  26.5 4.7 %collective-permute-done.2.far_b = f32[128,128]{1,0:T(8,128)S(1)} collective-permute-done((f32[128,128]{1,0:T(8,128)S(1)}, f32[128,128]{1,0:T(8,128)S(1)}, u32[]{:S(2)}, u32[]{:S(2)}) %collective-permute-start.2) | collective-permute-done | bytes 65568 | tf_op jit(solution)/shard_map/ppermute | solution.py:286
  31.2 0.0 collective-permute-done.1.far_a
  31.2 0.8 %collective-permute-done.near = f32[128,128]{1,0:T(8,128)S(1)} collective-permute-done((f32[128,128]{1,0:T(8,128)S(1)}, f32[128,128]{1,0:T(8,128)S(1)}, u32[]{:S(2)}, u32[]{:S(2)}) %collective-permute-start) | collective-permute-done | bytes 65568 | tf_op jit(solution)/shard_map/ppermute | solution.py:286
  31.9 0.0 copy-done
  31.9 10.6 %factor.1 = (bf16[528,128]{1,0:T(8,128)(2,1)S(1)}, f32[10,128,128]{2,1,0:T(8,128)S(1)}) custom-call(s32[1]{0:T(128)} %bitcast.rep, f32[7,128,128]{2,1,0:T(8,128)S(1)} %get-tuple-element.21.grams, f32[128,128]{1,0:T(8,128)S(1)} %get-tuple-element.22.own, f32[128,128]{1,0:T(8,128)S(1)} %collective-permute-done.near, ...), custom_call_target="tpu_custom_call" | custom-call | tf_op jit(solution)/shard_map/factor/pallas_call | solution.py:330
  42.5 0.0 copy-start.1
  42.6 0.8 %collective-permute-start.10 = (bf16[528,128]{1,0:T(8,128)(2,1)S(1)}, bf16[528,128]{1,0:T(8,128)(2,1)S(1)}, u32[]{:S(2)}, u32[]{:S(2)}) collective-permute-start(bf16[528,128]{1,0:T(8,128)(2,1)S(1)} %get-tuple-element.36.refs_2_), channel_id=1, source_target_pairs={{0,30},{1,31},{2,0},{3,1},{4,2},{5,3},{6,4},{7,5},{8,6},{9,7},{10,... | collective-permute-start | bytes 405512 | tf_op jit(solution)/shard_map/ppermute | solution.py:282
  43.3 1.3 %collective-permute-start.9 = (bf16[528,128]{1,0:T(8,128)(2,1)S(1)}, bf16[528,128]{1,0:T(8,128)(2,1)S(1)}, u32[]{:S(2)}, u32[]{:S(2)}) collective-permute-start(bf16[528,128]{1,0:T(8,128)(2,1)S(1)} %get-tuple-element.36.refs_2_), channel_id=1, source_target_pairs={{0,31},{1,0},{2,1},{3,2},{4,3},{5,4},{6,5},{7,6},{8,7},{9,8},{10,9... | collective-permute-start | bytes 405512 | tf_op jit(solution)/shard_map/ppermute | solution.py:282
  44.6 0.8 %collective-permute-start.8 = (bf16[528,128]{1,0:T(8,128)(2,1)S(1)}, bf16[528,128]{1,0:T(8,128)(2,1)S(1)}, u32[]{:S(2)}, u32[]{:S(2)}) collective-permute-start(bf16[528,128]{1,0:T(8,128)(2,1)S(1)} %get-tuple-element.36.refs_2_), channel_id=1, source_target_pairs={{0,1},{1,2},{2,3},{3,4},{4,5},{5,6},{6,7},{7,8},{8,9},{9,10},{10,1... | collective-permute-start | bytes 405512 | tf_op jit(solution)/shard_map/ppermute | solution.py:282
  45.4 0.0 collective-permute-done.5.lead_rest
  45.4 1.3 %collective-permute-start.7 = (bf16[528,128]{1,0:T(8,128)(2,1)S(1)}, bf16[528,128]{1,0:T(8,128)(2,1)S(1)}, u32[]{:S(2)}, u32[]{:S(2)}) collective-permute-start(bf16[528,128]{1,0:T(8,128)(2,1)S(1)} %get-tuple-element.36.refs_2_), channel_id=1, source_target_pairs={{0,2},{1,3},{2,4},{3,5},{4,6},{5,7},{6,8},{7,9},{8,10},{9,11},{10,... | collective-permute-start | bytes 405512 | tf_op jit(solution)/shard_map/ppermute | solution.py:282
  46.7 4.6 %finish.1 = (bf16[4,512,128]{2,1,0:T(8,128)(2,1)}, f32[7,128,128]{2,1,0:T(8,128)}, bf16[7,128,128]{2,1,0:T(8,128)(2,1)S(1)}, f32[2,32,128]{2,1,0:T(8,128)}, f32[...) custom-call(s32[1]{0:T(128)} %bitcast.rep, bf16[4,512,128]{2,1,0:T(8,128)(2,1)} %basis.3, f32[7,128,128]{2,1,0:T(8,128)} %trans.3, ...), custom_call_target="tpu_custom_call" | custom-call | tf_op jit(solution)/shard_map/finish/pallas_call | solution.py:357
  51.3 0.0 copy-start.2
  51.3 0.0 collective-permute-done.6.tail_rest
  51.3 0.0 copy-done.1
  51.4 0.9 %half.1 = bf16[16,128,128]{2,1,0:T(8,128)(2,1)S(1)} custom-call(s32[16]{0:T(128)S(1)} %copy-done.1, bf16[2,8,128,128]{3,2,1,0:T(8,128)(2,1)S(1)} %get-tuple-element.28.own, bf16[2,8,128,128]{3,2,1,0:T(8,128)(2,1)S(1)} %get-tuple-element.32.kept, bf16[8,128,128]{2,1,0:T(8,128)(2,1)S(1)} %collective-permute-done.5.lead_rest, ...), custom_call_target="tpu_custom_call" | custom-call | tf_op jit(solution)/shard_map/half/pallas_call | solution.py:381
  52.3 0.0 collective-permute-done.10.refs_4_
  52.3 0.0 collective-permute-done.9.refs_3_
  52.3 1.7 %collective-permute-done.8.refs_1_ = bf16[528,128]{1,0:T(8,128)(2,1)S(1)} collective-permute-done((bf16[528,128]{1,0:T(8,128)(2,1)S(1)}, bf16[528,128]{1,0:T(8,128)(2,1)S(1)}, u32[]{:S(2)}, u32[]{:S(2)}) %collective-permute-start.8) | collective-permute-done | bytes 135200 | tf_op jit(solution)/shard_map/ppermute | solution.py:282
  54.0 0.0 collective-permute-done.7.refs_0_
  54.0 0.0 copy-done.2
  54.0 1.9 %project.1 = bf16[16,128,128]{2,1,0:T(8,128)(2,1)} custom-call(s32[1]{0:T(128)} %bitcast.2.mine, s32[16]{0:T(128)S(1)} %copy-done.2, bf16[16,128,128]{2,1,0:T(8,128)(2,1)S(1)} %half.1, bf16[528,128]{1,0:T(8,128)(2,1)S(1)} %collective-permute-done.7.refs_0_, bf16[528,128]{1,0:T(8,128)(2,1)S(1)} %collective-permute-done.8.refs_1_, ...), custom_call_target="tpu_custom_call" | custom-call | tf_op jit(solution)/shard_map/project/pallas_call | solution.py:390
Async XLA Ops:
  0.6 31.3 %copy-start = (f32[2,128,128]{2,1,0:T(8,128)S(1)}, f32[2,128,128]{2,1,0:T(8,128)}, u32[]{:S(2)}) copy-start(f32[2,128,128]{2,1,0:T(8,128)} %trans_top.3) | copy-start | bytes 393220
  4.4 15.0 %collective-permute-start.3 = (bf16[2,8,128,128]{3,2,1,0:T(8,128)(2,1)S(1)}, bf16[2,8,128,128]{3,2,1,0:T(8,128)(2,1)S(1)}, u32[]{:S(2)}, u32[]{:S(2)}) collective-permute-start(bf16[2,8,128,128]{3,2,1,0:T(8,128)(2,1)S(1)} %get-tuple-element.30), channel_id=1, source_target_pairs={{0,1},{1,0},{2,3},{3,2},{4,5},{5,4},{6,7},{7,6},{8,9},{9,8},{10,11... | collective-permute-start | bytes 1572872 | tf_op jit(solution)/shard_map/ppermute | solution.py:286
  7.4 13.4 %collective-permute-start.4 = (bf16[2,8,128,128]{3,2,1,0:T(8,128)(2,1)S(1)}, bf16[2,8,128,128]{3,2,1,0:T(8,128)(2,1)S(1)}, u32[]{:S(2)}, u32[]{:S(2)}) collective-permute-start(bf16[2,8,128,128]{3,2,1,0:T(8,128)(2,1)S(1)} %get-tuple-element.31), channel_id=1, source_target_pairs={{0,2},{1,3},{2,0},{3,1},{4,6},{5,7},{6,4},{7,5},{8,10},{9,11},{10,... | collective-permute-start | bytes 1572872 | tf_op jit(solution)/shard_map/ppermute | solution.py:286
  20.9 24.4 %collective-permute-start.5 = (bf16[8,128,128]{2,1,0:T(8,128)(2,1)S(1)}, bf16[8,128,128]{2,1,0:T(8,128)(2,1)S(1)}, u32[]{:S(2)}, u32[]{:S(2)}) collective-permute-start(bf16[8,128,128]{2,1,0:T(8,128)(2,1)S(1)} %get-tuple-element.33), channel_id=1, source_target_pairs={{0,2},{1,3},{2,0},{3,1},{4,6},{5,7},{6,4},{7,5},{8,10},{9,11},{10,... | collective-permute-start | bytes 786440 | tf_op jit(solution)/shard_map/ppermute | solution.py:286
  22.5 28.8 %collective-permute-start.6 = (bf16[8,128,128]{2,1,0:T(8,128)(2,1)S(1)}, bf16[8,128,128]{2,1,0:T(8,128)(2,1)S(1)}, u32[]{:S(2)}, u32[]{:S(2)}) collective-permute-start(bf16[8,128,128]{2,1,0:T(8,128)(2,1)S(1)} %get-tuple-element.34), channel_id=1, source_target_pairs={{0,1},{1,0},{2,3},{3,2},{4,5},{5,4},{6,7},{7,6},{8,9},{9,8},{10,11... | collective-permute-start | bytes 786440 | tf_op jit(solution)/shard_map/ppermute | solution.py:286
  23.0 8.1 %collective-permute-start.2 = (f32[128,128]{1,0:T(8,128)S(1)}, f32[128,128]{1,0:T(8,128)S(1)}, u32[]{:S(2)}, u32[]{:S(2)}) collective-permute-start(f32[128,128]{1,0:T(8,128)S(1)} %get-tuple-element.22.own), channel_id=1, source_target_pairs={{0,3},{1,2},{2,1},{3,0},{4,7},{5,6},{6,5},{7,4},{8,11},{9,10},{10,... | collective-permute-start | bytes 196616 | tf_op jit(solution)/shard_map/ppermute | solution.py:286
  24.5 6.7 %collective-permute-start.1 = (f32[128,128]{1,0:T(8,128)S(1)}, f32[128,128]{1,0:T(8,128)S(1)}, u32[]{:S(2)}, u32[]{:S(2)}) collective-permute-start(f32[128,128]{1,0:T(8,128)S(1)} %get-tuple-element.22.own), channel_id=1, source_target_pairs={{0,2},{1,3},{2,0},{3,1},{4,6},{5,7},{6,4},{7,5},{8,10},{9,11},{10,... | collective-permute-start | bytes 196616 | tf_op jit(solution)/shard_map/ppermute | solution.py:286
  26.0 6.0 %collective-permute-start = (f32[128,128]{1,0:T(8,128)S(1)}, f32[128,128]{1,0:T(8,128)S(1)}, u32[]{:S(2)}, u32[]{:S(2)}) collective-permute-start(f32[128,128]{1,0:T(8,128)S(1)} %get-tuple-element.22.own), channel_id=1, source_target_pairs={{0,1},{1,0},{2,3},{3,2},{4,5},{5,4},{6,7},{7,6},{8,9},{9,8},{10,11... | collective-permute-start | bytes 196616 | tf_op jit(solution)/shard_map/ppermute | solution.py:286
  42.5 8.8 %copy-start.1 = (s32[16]{0:T(128)S(1)}, s32[16]{0:T(128)}, u32[]{:S(2)}) copy-start(s32[16]{0:T(128)} %row_slot.1) | copy-start | bytes 196
  42.6 9.7 %collective-permute-start.10 = (bf16[528,128]{1,0:T(8,128)(2,1)S(1)}, bf16[528,128]{1,0:T(8,128)(2,1)S(1)}, u32[]{:S(2)}, u32[]{:S(2)}) collective-permute-start(bf16[528,128]{1,0:T(8,128)(2,1)S(1)} %get-tuple-element.36.refs_2_), channel_id=1, source_target_pairs={{0,30},{1,31},{2,0},{3,1},{4,2},{5,3},{6,4},{7,5},{8,6},{9,7},{10,... | collective-permute-start | bytes 405512 | tf_op jit(solution)/shard_map/ppermute | solution.py:282
  43.3 9.0 %collective-permute-start.9 = (bf16[528,128]{1,0:T(8,128)(2,1)S(1)}, bf16[528,128]{1,0:T(8,128)(2,1)S(1)}, u32[]{:S(2)}, u32[]{:S(2)}) collective-permute-start(bf16[528,128]{1,0:T(8,128)(2,1)S(1)} %get-tuple-element.36.refs_2_), channel_id=1, source_target_pairs={{0,31},{1,0},{2,1},{3,2},{4,3},{5,4},{6,5},{7,6},{8,7},{9,8},{10,9... | collective-permute-start | bytes 405512 | tf_op jit(solution)/shard_map/ppermute | solution.py:282
  44.6 9.4 %collective-permute-start.8 = (bf16[528,128]{1,0:T(8,128)(2,1)S(1)}, bf16[528,128]{1,0:T(8,128)(2,1)S(1)}, u32[]{:S(2)}, u32[]{:S(2)}) collective-permute-start(bf16[528,128]{1,0:T(8,128)(2,1)S(1)} %get-tuple-element.36.refs_2_), channel_id=1, source_target_pairs={{0,1},{1,2},{2,3},{3,4},{4,5},{5,6},{6,7},{7,8},{8,9},{9,10},{10,1... | collective-permute-start | bytes 405512 | tf_op jit(solution)/shard_map/ppermute | solution.py:282
  45.4 8.6 %collective-permute-start.7 = (bf16[528,128]{1,0:T(8,128)(2,1)S(1)}, bf16[528,128]{1,0:T(8,128)(2,1)S(1)}, u32[]{:S(2)}, u32[]{:S(2)}) collective-permute-start(bf16[528,128]{1,0:T(8,128)(2,1)S(1)} %get-tuple-element.36.refs_2_), channel_id=1, source_target_pairs={{0,2},{1,3},{2,4},{3,5},{4,6},{5,7},{6,8},{7,9},{8,10},{9,11},{10,... | collective-permute-start | bytes 405512 | tf_op jit(solution)/shard_map/ppermute | solution.py:282
  51.3 2.6 %copy-start.2 = (s32[16]{0:T(128)S(1)}, s32[16]{0:T(128)}, u32[]{:S(2)}) copy-start(s32[16]{0:T(128)} %col_node.1) | copy-start | bytes 196

commit v4 on v3

--- a/solution.py
+++ b/solution.py
@@ -72,19 +72,22 @@
             for top in tops
         ]
         both = [jnp.where(in_panel, eye, top) for top in tops]
+        block = [jnp.zeros(shape, F32) for _ in mats]
+        scales = [jnp.zeros(shape, F32) for _ in mats]
         for j in range(PANEL):
             for t in range(len(mats)):
                 scale = lax.rsqrt(row(cols[t][j], j))
+                scales[t] = jnp.where(sub == j, scale, scales[t])
+                block[t] = jnp.where(lane == start + j, cols[t][j], block[t])
                 low = cols[t][j] * scale
                 below = jnp.where(sub > j, low, 0.0)
                 for k in range(j + 1, PANEL):
                     cols[t][k] = cols[t][k] - below * row(low, k)
-                pivot = row(tops[t], j) * scale
-                tops[t] = jnp.where(sub == j, pivot, tops[t] - below * pivot)
                 pivot = row(both[t], j) * scale
                 both[t] = jnp.where(sub == j, pivot, both[t] - below * pivot)
+        upper = in_panel & (lane >= sub + start)
         for t, m in enumerate(mats):
-            joint[m, start:stop, :] = jnp.where(lane >= sub + start, tops[t], both[t])
+            joint[m, start:stop, :] = jnp.where(upper, block[t] * scales[t], both[t])
             if stop < size:
                 high, mid, low = split3(both[t])
                 left = jnp.concatenate([high, high, mid, mid, high, low], axis=0)
@@ -112,6 +115,30 @@
 def wait_all(copies):
     for copy in copies:
         copy.wait()
+
+
+def fold_symmetric(value):
+    size = value.shape[0]
+    block = size // 4
+    lane = lax.broadcasted_iota(jnp.int32, (block, size), 1)
+    last = pltpu.roll(value[3 * block :], block, 1)
+    near = jnp.where(lane >= block, value[block : 2 * block], last)
+    low = pltpu.roll(value[5 * block // 2 : 3 * block], 2 * block, 1)
+    half = lane[: block // 2] >= 2 * block
+    return value[:block], near, jnp.where(half, value[2 * block : 5 * block // 2], low)
+
+
+def unfold_symmetric(rows):
+    size = rows.shape[1]
+    block = size // 4
+    near, far = rows[block : 2 * block], rows[2 * block :]
+    whole = jnp.concatenate(
+        [rows[: 2 * block], far, pltpu.roll(far, 2 * block, 1), pltpu.roll(near, 3 * block, 1)],
+        axis=0,
+    )
+    sub = lax.broadcasted_iota(jnp.int32, whole.shape, 0)
+    lane = lax.broadcasted_iota(jnp.int32, whole.shape, 1)
+    return jnp.where(lane >= sub, whole, whole.T)
 
 
 def gram_kernel(rep, basis, trans, parts, grams, sent, lead, tail, add, rows, factors, sems):
@@ -144,18 +171,20 @@
                 grams[two], factors[two]
             )
         base, count = base + count, count // 2
-    sent[...] = congruence(grams[base], factors[base])
+    at = 0
+    for rows_of in fold_symmetric(congruence(grams[base], factors[base])):
+        sent[at : at + rows_of.shape[0], :] = rows_of
+        at += rows_of.shape[0]
     wait_all(cut)
 
 
 def factor_kernel(
-    rep, grams, own, near, far_a, far_b, trans_top, packed, joint, work
+    rep, grams, own, near, far_a, far_b, trans_top, joint, work
 ):
     slots = grams.shape[0]
-    size = grams.shape[1]
     high = rep[0] // 2
-    mine = own[...] + near[...]
-    other = far_a[...] + far_b[...]
+    mine = unfold_symmetric(own[...] + near[...])
+    other = unfold_symmetric(far_a[...] + far_b[...])
     three_a = jnp.where(high == 0, mine, other)
     three_b = jnp.where(high == 0, other, mine)
     work[:slots] = grams[...]
@@ -163,6 +192,10 @@
     work[slots + 1] = three_b
     work[slots + 2] = congruence(three_a, trans_top[0]) + congruence(three_b, trans_top[1])
     factorize(work, joint, list(range(slots + 3)))
+
+
+def pack_kernel(slots, joint, packed):
+    size = joint.shape[1]
     sub = lax.broadcasted_iota(jnp.int32, (size, size), 0)
     lane = lax.broadcasted_iota(jnp.int32, (size, size), 1)
     pairs = (slots + 1) // 2
@@ -306,7 +339,7 @@
         gram_kernel,
         out_shape=[
             jax.ShapeDtypeStruct((slots, *square), F32),
-            jax.ShapeDtypeStruct(square, F32),
+            jax.ShapeDtypeStruct((5 * rank // 8, rank), F32),
             pair,
             pair,
             pair,
@@ -327,14 +360,11 @@
     tail = swapped(tail_out, 2)
     pairs = (slots + 1) // 2
     nodes = (slots + 3, *square)
-    packed, joint = pl.pallas_call(
+    joint = pl.pallas_call(
         factor_kernel,
-        out_shape=[
-            jax.ShapeDtypeStruct((pairs * rank + TILE, rank), BF16),
-            jax.ShapeDtypeStruct(nodes, F32),
-        ],
+        out_shape=jax.ShapeDtypeStruct(nodes, F32),
         in_specs=[SMEM] + [VMEM] * 6,
-        out_specs=[VMEM] * 2,
+        out_specs=VMEM,
         scratch_shapes=[pltpu.VMEM(nodes, F32)],
         compiler_params=PARAMS,
         name="factor",
@@ -349,6 +379,14 @@
     )(add, lead, tail)
     lead_rest = swapped(lead_sum, 2)
     tail_rest = swapped(tail_sum, 1)
+    packed = pl.pallas_call(
+        functools.partial(pack_kernel, slots),
+        out_shape=jax.ShapeDtypeStruct((pairs * rank + TILE, rank), BF16),
+        in_specs=[VMEM],
+        out_specs=VMEM,
+        compiler_params=PARAMS,
+        name="pack",
+    )(joint)
     pieces = [
         packed if offset == 0 else shifted(packed, -offset)
         for offset in range(-REACH, REACH + 1)

time: 56.2 us -> 53.8 us (0.957)
  Pallas kernels: 21.9 us -> 20.6 us
  waiting for transfers between devices: 18.9 us -> 17.8 us
    pallas_call x1 -> x2, Pallas kernels: 10.6 us -> 9.24 us  [the longest x1 9.13 us: per_device(): pl.pallas_call(factor_kernel, out_shape=jax.ShapeDtypeStruct(nodes, F32),...]
    ppermute x7, waiting for transfers between devices: 17.3 us -> 16.2 us  [swapped(): lax.ppermute(value, 'rep', [(i, i ^ flip) for i in range(lax.axis_size('r...]
  transfers between devices with their start and end apart: 11 -> 11, of which waited for: 5 -> 5; matrix products, arithmetic and copies ran while one was open for 0% -> 0% of each run, Pallas kernels for 29% -> 28%
where the time goes in v4:
time: 53.8 us; the launch traced here: 53.7 us
  Pallas kernels  20.6 us (38%)
  waiting for transfers between devices  17.8 us (33%)
  starting transfers between devices  14.3 us (27%)
  between operations  0.9 us (2%)
    ppermute x7, waiting for transfers between devices, swapped(): lax.ppermute(value, 'rep', [(i, i ^ flip) for i in range(lax.axis_size('r...  16.2 us
    ppermute x7, starting transfers between devices, swapped(): lax.ppermute(value, 'rep', [(i, i ^ flip) for i in range(lax.axis_size('r...  10.2 us
    pallas_call x1, Pallas kernels, per_device(): pl.pallas_call(factor_kernel, out_shape=jax.ShapeDtypeStruct(nodes, F32),...  9.13 us
    pallas_call x1, Pallas kernels, per_device(): pl.pallas_call(finish_kernel, out_shape=[jax.ShapeDtypeStruct(leaf_basis....  4.64 us
    ppermute x4, starting transfers between devices, shifted(): lax.ppermute(value, ALL, [(i, (i + steps) % count) for i in range(count)])  4.11 us
    pallas_call x1, Pallas kernels, per_device(): pl.pallas_call(gram_kernel, out_shape=[jax.ShapeDtypeStruct((slots, *squa...  3.78 us
    pallas_call x1, Pallas kernels, per_device(): pl.pallas_call(functools.partial(project_kernel, slots), out_shape=jax.Sh...  1.9 us
    ppermute x4, waiting for transfers between devices, shifted(): lax.ppermute(value, ALL, [(i, (i + steps) % count) for i in range(count)])  1.61 us
  transfers between devices with their start and end apart: 11, of which 5 were waited for; matrix products, arithmetic and copies ran while one was open for 0% of the time, Pallas kernels for 28%

profile of v4, /device:TPU:0, one launch (start us, length us, event | category | flops | bytes accessed | tf_op | source)
XLA Modules:
  0.0 53.7 jit_solution(17695157168648016685)
XLA Ops:
  0.6 0.0 copy-start
  0.6 3.8 %grams.1 = (f32[7,128,128]{2,1,0:T(8,128)S(1)}, f32[80,128]{1,0:T(8,128)S(1)}, bf16[2,8,128,128]{3,2,1,0:T(8,128)(2,1)S(1)}, bf16[2,8,128,128]{3,2,1,0:T(8,128)(2,1)S(1)}, bf16[2,8,128,128]{3,2,1,0:T(8,128)(2,1)S(1)}) custom-call(s32[1]{0:T(128)} %bitcast.rep, bf16[4,512,128]{2,1,0:T(8,128)(2,1)} %basis.3, f32[7,128,128]{2,1,0:T(8,128)} %trans.3, ...), custom_call_target="tpu_custom_call" | custom-call | tf_op jit(solution)/shard_map/grams/pallas_call | solution.py:338
  4.4 3.0 %collective-permute-start.3 = (bf16[2,8,128,128]{3,2,1,0:T(8,128)(2,1)S(1)}, bf16[2,8,128,128]{3,2,1,0:T(8,128)(2,1)S(1)}, u32[]{:S(2)}, u32[]{:S(2)}) collective-permute-start(bf16[2,8,128,128]{3,2,1,0:T(8,128)(2,1)S(1)} %get-tuple-element.27), channel_id=1, source_target_pairs={{0,1},{1,0},{2,3},{3,2},{4,5},{5,4},{6,7},{7,6},{8,9},{9,8},{10,11... | collective-permute-start | bytes 1572872 | tf_op jit(solution)/shard_map/ppermute | solution.py:319
  7.5 1.5 %collective-permute-start.4 = (bf16[2,8,128,128]{3,2,1,0:T(8,128)(2,1)S(1)}, bf16[2,8,128,128]{3,2,1,0:T(8,128)(2,1)S(1)}, u32[]{:S(2)}, u32[]{:S(2)}) collective-permute-start(bf16[2,8,128,128]{3,2,1,0:T(8,128)(2,1)S(1)} %get-tuple-element.28), channel_id=1, source_target_pairs={{0,2},{1,3},{2,0},{3,1},{4,6},{5,7},{6,4},{7,5},{8,10},{9,11},{10,... | collective-permute-start | bytes 1572872 | tf_op jit(solution)/shard_map/ppermute | solution.py:319
  9.0 10.4 %collective-permute-done.3.lead = bf16[2,8,128,128]{3,2,1,0:T(8,128)(2,1)S(1)} collective-permute-done((bf16[2,8,128,128]{3,2,1,0:T(8,128)(2,1)S(1)}, bf16[2,8,128,128]{3,2,1,0:T(8,128)(2,1)S(1)}, u32[]{:S(2)}, u32[]{:S(2)}) %collective-permute-start.3) | collective-permute-done | bytes 524320 | tf_op jit(solution)/shard_map/ppermute | solution.py:319
  19.4 1.5 %collective-permute-done.4.tail = bf16[2,8,128,128]{3,2,1,0:T(8,128)(2,1)S(1)} collective-permute-done((bf16[2,8,128,128]{3,2,1,0:T(8,128)(2,1)S(1)}, bf16[2,8,128,128]{3,2,1,0:T(8,128)(2,1)S(1)}, u32[]{:S(2)}, u32[]{:S(2)}) %collective-permute-start.4) | collective-permute-done | bytes 524320 | tf_op jit(solution)/shard_map/ppermute | solution.py:319
  20.9 0.1 fold.1
  21.0 1.6 %collective-permute-start.5 = (bf16[8,128,128]{2,1,0:T(8,128)(2,1)S(1)}, bf16[8,128,128]{2,1,0:T(8,128)(2,1)S(1)}, u32[]{:S(2)}, u32[]{:S(2)}) collective-permute-start(bf16[8,128,128]{2,1,0:T(8,128)(2,1)S(1)} %get-tuple-element.30), channel_id=1, source_target_pairs={{0,2},{1,3},{2,0},{3,1},{4,6},{5,7},{6,4},{7,5},{8,10},{9,11},{10,... | collective-permute-start | bytes 786440 | tf_op jit(solution)/shard_map/ppermute | solution.py:319
  22.6 0.5 collective-permute-start.6
  23.1 1.4 %collective-permute-start.2 = (f32[80,128]{1,0:T(8,128)S(1)}, f32[80,128]{1,0:T(8,128)S(1)}, u32[]{:S(2)}, u32[]{:S(2)}) collective-permute-start(f32[80,128]{1,0:T(8,128)S(1)} %get-tuple-element.20.own), channel_id=1, source_target_pairs={{0,3},{1,2},{2,1},{3,0},{4,7},{5,6},{6,5},{7,4},{8,11},{9,10},{10,... | collective-permute-start | bytes 122888 | tf_op jit(solution)/shard_map/ppermute | solution.py:319
  24.5 1.5 %collective-permute-start.1 = (f32[80,128]{1,0:T(8,128)S(1)}, f32[80,128]{1,0:T(8,128)S(1)}, u32[]{:S(2)}, u32[]{:S(2)}) collective-permute-start(f32[80,128]{1,0:T(8,128)S(1)} %get-tuple-element.20.own), channel_id=1, source_target_pairs={{0,2},{1,3},{2,0},{3,1},{4,6},{5,7},{6,4},{7,5},{8,10},{9,11},{10,... | collective-permute-start | bytes 122888 | tf_op jit(solution)/shard_map/ppermute | solution.py:319
  26.1 0.5 collective-permute-start
  26.6 3.9 %collective-permute-done.2.far_b = f32[80,128]{1,0:T(8,128)S(1)} collective-permute-done((f32[80,128]{1,0:T(8,128)S(1)}, f32[80,128]{1,0:T(8,128)S(1)}, u32[]{:S(2)}, u32[]{:S(2)}) %collective-permute-start.2) | collective-permute-done | bytes 40992 | tf_op jit(solution)/shard_map/ppermute | solution.py:319
  30.5 0.0 collective-permute-done.1.far_a
  30.5 0.5 collective-permute-done.near
  31.0 0.0 copy-done
  31.0 9.1 %factor.1.joint = f32[10,128,128]{2,1,0:T(8,128)S(1)} custom-call(s32[1]{0:T(128)} %bitcast.rep, f32[7,128,128]{2,1,0:T(8,128)S(1)} %get-tuple-element.19.grams, f32[80,128]{1,0:T(8,128)S(1)} %get-tuple-element.20.own, f32[80,128]{1,0:T(8,128)S(1)} %collective-permute-done.near, f32[80,128]{1,0:T(8,128)S(1)} %collective-permute-done.1.far_a, ...), custom_call_target="tpu_custom_call" | custom-call | tf_op jit(solution)/shard_map/factor/pallas_call | solution.py:363
  40.1 0.1 pack.1.refs_2_
  40.2 0.0 copy-start.1
  40.2 0.8 %collective-permute-start.10 = (bf16[528,128]{1,0:T(8,128)(2,1)S(1)}, bf16[528,128]{1,0:T(8,128)(2,1)S(1)}, u32[]{:S(2)}, u32[]{:S(2)}) collective-permute-start(bf16[528,128]{1,0:T(8,128)(2,1)S(1)} %pack.1.refs_2_), channel_id=1, source_target_pairs={{0,30},{1,31},{2,0},{3,1},{4,2},{5,3},{6,4},{7,5},{8,6},{9,7},{10,... | collective-permute-start | bytes 405512 | tf_op jit(solution)/shard_map/ppermute | solution.py:315
  41.0 1.3 %collective-permute-start.9 = (bf16[528,128]{1,0:T(8,128)(2,1)S(1)}, bf16[528,128]{1,0:T(8,128)(2,1)S(1)}, u32[]{:S(2)}, u32[]{:S(2)}) collective-permute-start(bf16[528,128]{1,0:T(8,128)(2,1)S(1)} %pack.1.refs_2_), channel_id=1, source_target_pairs={{0,31},{1,0},{2,1},{3,2},{4,3},{5,4},{6,5},{7,6},{8,7},{9,8},{10,9... | collective-permute-start | bytes 405512 | tf_op jit(solution)/shard_map/ppermute | solution.py:315
  42.3 0.8 %collective-permute-start.8 = (bf16[528,128]{1,0:T(8,128)(2,1)S(1)}, bf16[528,128]{1,0:T(8,128)(2,1)S(1)}, u32[]{:S(2)}, u32[]{:S(2)}) collective-permute-start(bf16[528,128]{1,0:T(8,128)(2,1)S(1)} %pack.1.refs_2_), channel_id=1, source_target_pairs={{0,1},{1,2},{2,3},{3,4},{4,5},{5,6},{6,7},{7,8},{8,9},{9,10},{10,1... | collective-permute-start | bytes 405512 | tf_op jit(solution)/shard_map/ppermute | solution.py:315
  43.0 0.0 collective-permute-done.5.lead_rest
  43.0 1.3 %collective-permute-start.7 = (bf16[528,128]{1,0:T(8,128)(2,1)S(1)}, bf16[528,128]{1,0:T(8,128)(2,1)S(1)}, u32[]{:S(2)}, u32[]{:S(2)}) collective-permute-start(bf16[528,128]{1,0:T(8,128)(2,1)S(1)} %pack.1.refs_2_), channel_id=1, source_target_pairs={{0,2},{1,3},{2,4},{3,5},{4,6},{5,7},{6,8},{7,9},{8,10},{9,11},{10,... | collective-permute-start | bytes 405512 | tf_op jit(solution)/shard_map/ppermute | solution.py:315
  44.3 4.6 %finish.1 = (bf16[4,512,128]{2,1,0:T(8,128)(2,1)}, f32[7,128,128]{2,1,0:T(8,128)}, bf16[7,128,128]{2,1,0:T(8,128)(2,1)S(1)}, f32[2,32,128]{2,1,0:T(8,128)}, f32[...) custom-call(s32[1]{0:T(128)} %bitcast.rep, bf16[4,512,128]{2,1,0:T(8,128)(2,1)} %basis.3, f32[7,128,128]{2,1,0:T(8,128)} %trans.3, ...), custom_call_target="tpu_custom_call" | custom-call | tf_op jit(solution)/shard_map/finish/pallas_call | solution.py:395
  49.0 0.0 copy-start.2
  49.0 0.0 collective-permute-done.6.tail_rest
  49.0 0.0 copy-done.1
  49.0 1.0 %half.1 = bf16[16,128,128]{2,1,0:T(8,128)(2,1)S(1)} custom-call(s32[16]{0:T(128)S(1)} %copy-done.1, bf16[2,8,128,128]{3,2,1,0:T(8,128)(2,1)S(1)} %get-tuple-element.25.own, bf16[2,8,128,128]{3,2,1,0:T(8,128)(2,1)S(1)} %get-tuple-element.29.kept, bf16[8,128,128]{2,1,0:T(8,128)(2,1)S(1)} %collective-permute-done.5.lead_rest, ...), custom_call_target="tpu_custom_call" | custom-call | tf_op jit(solution)/shard_map/half/pallas_call | solution.py:419
  50.0 0.0 collective-permute-done.10.refs_4_
  50.0 0.0 collective-permute-done.9.refs_3_
  50.0 1.6 %collective-permute-done.8.refs_1_ = bf16[528,128]{1,0:T(8,128)(2,1)S(1)} collective-permute-done((bf16[528,128]{1,0:T(8,128)(2,1)S(1)}, bf16[528,128]{1,0:T(8,128)(2,1)S(1)}, u32[]{:S(2)}, u32[]{:S(2)}) %collective-permute-start.8) | collective-permute-done | bytes 135200 | tf_op jit(solution)/shard_map/ppermute | solution.py:315
  51.6 0.0 collective-permute-done.7.refs_0_
  51.6 0.0 copy-done.2
  51.6 1.9 %project.1 = bf16[16,128,128]{2,1,0:T(8,128)(2,1)} custom-call(s32[1]{0:T(128)} %bitcast.2.mine, s32[16]{0:T(128)S(1)} %copy-done.2, bf16[16,128,128]{2,1,0:T(8,128)(2,1)S(1)} %half.1, bf16[528,128]{1,0:T(8,128)(2,1)S(1)} %collective-permute-done.7.refs_0_, bf16[528,128]{1,0:T(8,128)(2,1)S(1)} %collective-permute-done.8.refs_1_, ...), custom_call_target="tpu_custom_call" | custom-call | tf_op jit(solution)/shard_map/project/pallas_call | solution.py:428
Async XLA Ops:
  0.6 30.3 %copy-start = (f32[2,128,128]{2,1,0:T(8,128)S(1)}, f32[2,128,128]{2,1,0:T(8,128)}, u32[]{:S(2)}) copy-start(f32[2,128,128]{2,1,0:T(8,128)} %trans_top.3) | copy-start | bytes 393220
  4.4 15.0 %collective-permute-start.3 = (bf16[2,8,128,128]{3,2,1,0:T(8,128)(2,1)S(1)}, bf16[2,8,128,128]{3,2,1,0:T(8,128)(2,1)S(1)}, u32[]{:S(2)}, u32[]{:S(2)}) collective-permute-start(bf16[2,8,128,128]{3,2,1,0:T(8,128)(2,1)S(1)} %get-tuple-element.27), channel_id=1, source_target_pairs={{0,1},{1,0},{2,3},{3,2},{4,5},{5,4},{6,7},{7,6},{8,9},{9,8},{10,11... | collective-permute-start | bytes 1572872 | tf_op jit(solution)/shard_map/ppermute | solution.py:319
  7.5 13.4 %collective-permute-start.4 = (bf16[2,8,128,128]{3,2,1,0:T(8,128)(2,1)S(1)}, bf16[2,8,128,128]{3,2,1,0:T(8,128)(2,1)S(1)}, u32[]{:S(2)}, u32[]{:S(2)}) collective-permute-start(bf16[2,8,128,128]{3,2,1,0:T(8,128)(2,1)S(1)} %get-tuple-element.28), channel_id=1, source_target_pairs={{0,2},{1,3},{2,0},{3,1},{4,6},{5,7},{6,4},{7,5},{8,10},{9,11},{10,... | collective-permute-start | bytes 1572872 | tf_op jit(solution)/shard_map/ppermute | solution.py:319
  21.0 22.0 %collective-permute-start.5 = (bf16[8,128,128]{2,1,0:T(8,128)(2,1)S(1)}, bf16[8,128,128]{2,1,0:T(8,128)(2,1)S(1)}, u32[]{:S(2)}, u32[]{:S(2)}) collective-permute-start(bf16[8,128,128]{2,1,0:T(8,128)(2,1)S(1)} %get-tuple-element.30), channel_id=1, source_target_pairs={{0,2},{1,3},{2,0},{3,1},{4,6},{5,7},{6,4},{7,5},{8,10},{9,11},{10,... | collective-permute-start | bytes 786440 | tf_op jit(solution)/shard_map/ppermute | solution.py:319
  22.6 26.4 %collective-permute-start.6 = (bf16[8,128,128]{2,1,0:T(8,128)(2,1)S(1)}, bf16[8,128,128]{2,1,0:T(8,128)(2,1)S(1)}, u32[]{:S(2)}, u32[]{:S(2)}) collective-permute-start(bf16[8,128,128]{2,1,0:T(8,128)(2,1)S(1)} %get-tuple-element.31), channel_id=1, source_target_pairs={{0,1},{1,0},{2,3},{3,2},{4,5},{5,4},{6,7},{7,6},{8,9},{9,8},{10,11... | collective-permute-start | bytes 786440 | tf_op jit(solution)/shard_map/ppermute | solution.py:319
  23.1 7.4 %collective-permute-start.2 = (f32[80,128]{1,0:T(8,128)S(1)}, f32[80,128]{1,0:T(8,128)S(1)}, u32[]{:S(2)}, u32[]{:S(2)}) collective-permute-start(f32[80,128]{1,0:T(8,128)S(1)} %get-tuple-element.20.own), channel_id=1, source_target_pairs={{0,3},{1,2},{2,1},{3,0},{4,7},{5,6},{6,5},{7,4},{8,11},{9,10},{10,... | collective-permute-start | bytes 122888 | tf_op jit(solution)/shard_map/ppermute | solution.py:319
  24.5 5.9 %collective-permute-start.1 = (f32[80,128]{1,0:T(8,128)S(1)}, f32[80,128]{1,0:T(8,128)S(1)}, u32[]{:S(2)}, u32[]{:S(2)}) collective-permute-start(f32[80,128]{1,0:T(8,128)S(1)} %get-tuple-element.20.own), channel_id=1, source_target_pairs={{0,2},{1,3},{2,0},{3,1},{4,6},{5,7},{6,4},{7,5},{8,10},{9,11},{10,... | collective-permute-start | bytes 122888 | tf_op jit(solution)/shard_map/ppermute | solution.py:319
  26.1 4.9 %collective-permute-start = (f32[80,128]{1,0:T(8,128)S(1)}, f32[80,128]{1,0:T(8,128)S(1)}, u32[]{:S(2)}, u32[]{:S(2)}) collective-permute-start(f32[80,128]{1,0:T(8,128)S(1)} %get-tuple-element.20.own), channel_id=1, source_target_pairs={{0,1},{1,0},{2,3},{3,2},{4,5},{5,4},{6,7},{7,6},{8,9},{9,8},{10,11... | collective-permute-start | bytes 122888 | tf_op jit(solution)/shard_map/ppermute | solution.py:319
  40.2 8.8 %copy-start.1 = (s32[16]{0:T(128)S(1)}, s32[16]{0:T(128)}, u32[]{:S(2)}) copy-start(s32[16]{0:T(128)} %row_slot.1) | copy-start | bytes 196
  40.2 9.8 %collective-permute-start.10 = (bf16[528,128]{1,0:T(8,128)(2,1)S(1)}, bf16[528,128]{1,0:T(8,128)(2,1)S(1)}, u32[]{:S(2)}, u32[]{:S(2)}) collective-permute-start(bf16[528,128]{1,0:T(8,128)(2,1)S(1)} %pack.1.refs_2_), channel_id=1, source_target_pairs={{0,30},{1,31},{2,0},{3,1},{4,2},{5,3},{6,4},{7,5},{8,6},{9,7},{10,... | collective-permute-start | bytes 405512 | tf_op jit(solution)/shard_map/ppermute | solution.py:315
  41.0 9.0 %collective-permute-start.9 = (bf16[528,128]{1,0:T(8,128)(2,1)S(1)}, bf16[528,128]{1,0:T(8,128)(2,1)S(1)}, u32[]{:S(2)}, u32[]{:S(2)}) collective-permute-start(bf16[528,128]{1,0:T(8,128)(2,1)S(1)} %pack.1.refs_2_), channel_id=1, source_target_pairs={{0,31},{1,0},{2,1},{3,2},{4,3},{5,4},{6,5},{7,6},{8,7},{9,8},{10,9... | collective-permute-start | bytes 405512 | tf_op jit(solution)/shard_map/ppermute | solution.py:315
  42.3 9.4 %collective-permute-start.8 = (bf16[528,128]{1,0:T(8,128)(2,1)S(1)}, bf16[528,128]{1,0:T(8,128)(2,1)S(1)}, u32[]{:S(2)}, u32[]{:S(2)}) collective-permute-start(bf16[528,128]{1,0:T(8,128)(2,1)S(1)} %pack.1.refs_2_), channel_id=1, source_target_pairs={{0,1},{1,2},{2,3},{3,4},{4,5},{5,6},{6,7},{7,8},{8,9},{9,10},{10,1... | collective-permute-start | bytes 405512 | tf_op jit(solution)/shard_map/ppermute | solution.py:315
  43.0 8.6 %collective-permute-start.7 = (bf16[528,128]{1,0:T(8,128)(2,1)S(1)}, bf16[528,128]{1,0:T(8,128)(2,1)S(1)}, u32[]{:S(2)}, u32[]{:S(2)}) collective-permute-start(bf16[528,128]{1,0:T(8,128)(2,1)S(1)} %pack.1.refs_2_), channel_id=1, source_target_pairs={{0,2},{1,3},{2,4},{3,5},{4,6},{5,7},{6,8},{7,9},{8,10},{9,11},{10,... | collective-permute-start | bytes 405512 | tf_op jit(solution)/shard_map/ppermute | solution.py:315
  49.0 2.6 %copy-start.2 = (s32[16]{0:T(128)S(1)}, s32[16]{0:T(128)}, u32[]{:S(2)}) copy-start(s32[16]{0:T(128)} %col_node.1) | copy-start | bytes 196

commit v5 on v4

--- a/solution.py
+++ b/solution.py
@@ -305,8 +305,8 @@
         )
         odd = jnp.dot(half[k], square * below + spread * eye, preferred_element_type=F32)
         held[k] = jnp.where(slot % 2 == 0, even, odd).astype(BF16)
-        if k % 4 == 3:
-            gone += start_all([(held.at[k - 3 : k + 1], out.at[k - 3 : k + 1])], sems, k // 4)
+        if k % 2 == 1:
+            gone += start_all([(held.at[k - 1 : k + 1], out.at[k - 1 : k + 1])], sems, k // 2)
     wait_all(gone)
 
 
@@ -387,10 +387,9 @@
         compiler_params=PARAMS,
         name="pack",
     )(joint)
-    pieces = [
-        packed if offset == 0 else shifted(packed, -offset)
-        for offset in range(-REACH, REACH + 1)
-    ]
+    pieces = []
+    for offset in range(-REACH, REACH + 1):
+        pieces.append(packed if offset == 0 else shifted(packed, -offset))
     share = rank // reps
     orth, fresh, pool, top, four, own = pl.pallas_call(
         finish_kernel,
@@ -433,7 +432,7 @@
         scratch_shapes=[
             pltpu.VMEM(((2 * REACH + 1) * packed.shape[0], rank), BF16),
             pltpu.VMEM((tiles, *square), BF16),
-            pltpu.SemaphoreType.DMA((tiles // 4,)),
+            pltpu.SemaphoreType.DMA((tiles // 2,)),
         ],
         compiler_params=PARAMS,
         name="project",

time: 53.8 us -> 53.8 us (level)
  no operation moved by 1% of the time
where the time goes in v5:
time: 53.8 us; the launch traced here: 53.7 us
  Pallas kernels  20.7 us (38%)
  waiting for transfers between devices  17.8 us (33%)
  starting transfers between devices  14.3 us (27%)
  between operations  0.9 us (2%)
    ppermute x7, waiting for transfers between devices, swapped(): lax.ppermute(value, 'rep', [(i, i ^ flip) for i in range(lax.axis_size('r...  16.2 us
    ppermute x7, starting transfers between devices, swapped(): lax.ppermute(value, 'rep', [(i, i ^ flip) for i in range(lax.axis_size('r...  10.2 us
    pallas_call x1, Pallas kernels, per_device(): pl.pallas_call(factor_kernel, out_shape=jax.ShapeDtypeStruct(nodes, F32),...  9.13 us
    pallas_call x1, Pallas kernels, per_device(): pl.pallas_call(finish_kernel, out_shape=[jax.ShapeDtypeStruct(leaf_basis....  4.64 us
    ppermute x4, starting transfers between devices, shifted(): lax.ppermute(value, ALL, [(i, (i + steps) % count) for i in range(count)])  4.11 us
    pallas_call x1, Pallas kernels, per_device(): pl.pallas_call(gram_kernel, out_shape=[jax.ShapeDtypeStruct((slots, *squa...  3.78 us
    pallas_call x1, Pallas kernels, per_device(): pl.pallas_call(functools.partial(project_kernel, slots), out_shape=jax.Sh...  1.91 us
    ppermute x4, waiting for transfers between devices, shifted(): lax.ppermute(value, ALL, [(i, (i + steps) % count) for i in range(count)])  1.61 us
  transfers between devices with their start and end apart: 11, of which 5 were waited for; matrix products, arithmetic and copies ran while one was open for 0% of the time, Pallas kernels for 28%

profile of v5, /device:TPU:0, one launch (start us, length us, event | category | flops | bytes accessed | tf_op | source)
XLA Modules:
  0.0 53.7 jit_solution(1771528363915635081)
XLA Ops:
  0.6 0.0 copy-start
  0.6 3.8 %grams.1 = (f32[7,128,128]{2,1,0:T(8,128)S(1)}, f32[80,128]{1,0:T(8,128)S(1)}, bf16[2,8,128,128]{3,2,1,0:T(8,128)(2,1)S(1)}, bf16[2,8,128,128]{3,2,1,0:T(8,128)(2,1)S(1)}, bf16[2,8,128,128]{3,2,1,0:T(8,128)(2,1)S(1)}) custom-call(s32[1]{0:T(128)} %bitcast.rep, bf16[4,512,128]{2,1,0:T(8,128)(2,1)} %basis.3, f32[7,128,128]{2,1,0:T(8,128)} %trans.3, ...), custom_call_target="tpu_custom_call" | custom-call | tf_op jit(solution)/shard_map/grams/pallas_call | solution.py:338
  4.4 3.0 %collective-permute-start.3 = (bf16[2,8,128,128]{3,2,1,0:T(8,128)(2,1)S(1)}, bf16[2,8,128,128]{3,2,1,0:T(8,128)(2,1)S(1)}, u32[]{:S(2)}, u32[]{:S(2)}) collective-permute-start(bf16[2,8,128,128]{3,2,1,0:T(8,128)(2,1)S(1)} %get-tuple-element.27), channel_id=1, source_target_pairs={{0,1},{1,0},{2,3},{3,2},{4,5},{5,4},{6,7},{7,6},{8,9},{9,8},{10,11... | collective-permute-start | bytes 1572872 | tf_op jit(solution)/shard_map/ppermute | solution.py:319
  7.5 1.5 %collective-permute-start.4 = (bf16[2,8,128,128]{3,2,1,0:T(8,128)(2,1)S(1)}, bf16[2,8,128,128]{3,2,1,0:T(8,128)(2,1)S(1)}, u32[]{:S(2)}, u32[]{:S(2)}) collective-permute-start(bf16[2,8,128,128]{3,2,1,0:T(8,128)(2,1)S(1)} %get-tuple-element.28), channel_id=1, source_target_pairs={{0,2},{1,3},{2,0},{3,1},{4,6},{5,7},{6,4},{7,5},{8,10},{9,11},{10,... | collective-permute-start | bytes 1572872 | tf_op jit(solution)/shard_map/ppermute | solution.py:319
  9.0 10.4 %collective-permute-done.3.lead = bf16[2,8,128,128]{3,2,1,0:T(8,128)(2,1)S(1)} collective-permute-done((bf16[2,8,128,128]{3,2,1,0:T(8,128)(2,1)S(1)}, bf16[2,8,128,128]{3,2,1,0:T(8,128)(2,1)S(1)}, u32[]{:S(2)}, u32[]{:S(2)}) %collective-permute-start.3) | collective-permute-done | bytes 524320 | tf_op jit(solution)/shard_map/ppermute | solution.py:319
  19.4 1.5 %collective-permute-done.4.tail = bf16[2,8,128,128]{3,2,1,0:T(8,128)(2,1)S(1)} collective-permute-done((bf16[2,8,128,128]{3,2,1,0:T(8,128)(2,1)S(1)}, bf16[2,8,128,128]{3,2,1,0:T(8,128)(2,1)S(1)}, u32[]{:S(2)}, u32[]{:S(2)}) %collective-permute-start.4) | collective-permute-done | bytes 524320 | tf_op jit(solution)/shard_map/ppermute | solution.py:319
  20.9 0.1 fold.1
  21.0 1.6 %collective-permute-start.5 = (bf16[8,128,128]{2,1,0:T(8,128)(2,1)S(1)}, bf16[8,128,128]{2,1,0:T(8,128)(2,1)S(1)}, u32[]{:S(2)}, u32[]{:S(2)}) collective-permute-start(bf16[8,128,128]{2,1,0:T(8,128)(2,1)S(1)} %get-tuple-element.30), channel_id=1, source_target_pairs={{0,2},{1,3},{2,0},{3,1},{4,6},{5,7},{6,4},{7,5},{8,10},{9,11},{10,... | collective-permute-start | bytes 786440 | tf_op jit(solution)/shard_map/ppermute | solution.py:319
  22.6 0.5 collective-permute-start.6
  23.1 1.4 %collective-permute-start.2 = (f32[80,128]{1,0:T(8,128)S(1)}, f32[80,128]{1,0:T(8,128)S(1)}, u32[]{:S(2)}, u32[]{:S(2)}) collective-permute-start(f32[80,128]{1,0:T(8,128)S(1)} %get-tuple-element.20.own), channel_id=1, source_target_pairs={{0,3},{1,2},{2,1},{3,0},{4,7},{5,6},{6,5},{7,4},{8,11},{9,10},{10,... | collective-permute-start | bytes 122888 | tf_op jit(solution)/shard_map/ppermute | solution.py:319
  24.5 1.5 %collective-permute-start.1 = (f32[80,128]{1,0:T(8,128)S(1)}, f32[80,128]{1,0:T(8,128)S(1)}, u32[]{:S(2)}, u32[]{:S(2)}) collective-permute-start(f32[80,128]{1,0:T(8,128)S(1)} %get-tuple-element.20.own), channel_id=1, source_target_pairs={{0,2},{1,3},{2,0},{3,1},{4,6},{5,7},{6,4},{7,5},{8,10},{9,11},{10,... | collective-permute-start | bytes 122888 | tf_op jit(solution)/shard_map/ppermute | solution.py:319
  26.1 0.5 collective-permute-start
  26.6 3.9 %collective-permute-done.2.far_b = f32[80,128]{1,0:T(8,128)S(1)} collective-permute-done((f32[80,128]{1,0:T(8,128)S(1)}, f32[80,128]{1,0:T(8,128)S(1)}, u32[]{:S(2)}, u32[]{:S(2)}) %collective-permute-start.2) | collective-permute-done | bytes 40992 | tf_op jit(solution)/shard_map/ppermute | solution.py:319
  30.5 0.0 collective-permute-done.1.far_a
  30.5 0.5 collective-permute-done.near
  31.0 0.0 copy-done
  31.0 9.1 %factor.1.joint = f32[10,128,128]{2,1,0:T(8,128)S(1)} custom-call(s32[1]{0:T(128)} %bitcast.rep, f32[7,128,128]{2,1,0:T(8,128)S(1)} %get-tuple-element.19.grams, f32[80,128]{1,0:T(8,128)S(1)} %get-tuple-element.20.own, f32[80,128]{1,0:T(8,128)S(1)} %collective-permute-done.near, f32[80,128]{1,0:T(8,128)S(1)} %collective-permute-done.1.far_a, ...), custom_call_target="tpu_custom_call" | custom-call | tf_op jit(solution)/shard_map/factor/pallas_call | solution.py:363
  40.1 0.1 pack.1.refs_2_
  40.2 0.0 copy-start.1
  40.2 0.8 %collective-permute-start.10 = (bf16[528,128]{1,0:T(8,128)(2,1)S(1)}, bf16[528,128]{1,0:T(8,128)(2,1)S(1)}, u32[]{:S(2)}, u32[]{:S(2)}) collective-permute-start(bf16[528,128]{1,0:T(8,128)(2,1)S(1)} %pack.1.refs_2_), channel_id=1, source_target_pairs={{0,30},{1,31},{2,0},{3,1},{4,2},{5,3},{6,4},{7,5},{8,6},{9,7},{10,... | collective-permute-start | bytes 405512 | tf_op jit(solution)/shard_map/ppermute | solution.py:315
  41.0 1.3 %collective-permute-start.9 = (bf16[528,128]{1,0:T(8,128)(2,1)S(1)}, bf16[528,128]{1,0:T(8,128)(2,1)S(1)}, u32[]{:S(2)}, u32[]{:S(2)}) collective-permute-start(bf16[528,128]{1,0:T(8,128)(2,1)S(1)} %pack.1.refs_2_), channel_id=1, source_target_pairs={{0,31},{1,0},{2,1},{3,2},{4,3},{5,4},{6,5},{7,6},{8,7},{9,8},{10,9... | collective-permute-start | bytes 405512 | tf_op jit(solution)/shard_map/ppermute | solution.py:315
  42.3 0.8 %collective-permute-start.8 = (bf16[528,128]{1,0:T(8,128)(2,1)S(1)}, bf16[528,128]{1,0:T(8,128)(2,1)S(1)}, u32[]{:S(2)}, u32[]{:S(2)}) collective-permute-start(bf16[528,128]{1,0:T(8,128)(2,1)S(1)} %pack.1.refs_2_), channel_id=1, source_target_pairs={{0,1},{1,2},{2,3},{3,4},{4,5},{5,6},{6,7},{7,8},{8,9},{9,10},{10,1... | collective-permute-start | bytes 405512 | tf_op jit(solution)/shard_map/ppermute | solution.py:315
  43.0 0.0 collective-permute-done.5.lead_rest
  43.0 1.3 %collective-permute-start.7 = (bf16[528,128]{1,0:T(8,128)(2,1)S(1)}, bf16[528,128]{1,0:T(8,128)(2,1)S(1)}, u32[]{:S(2)}, u32[]{:S(2)}) collective-permute-start(bf16[528,128]{1,0:T(8,128)(2,1)S(1)} %pack.1.refs_2_), channel_id=1, source_target_pairs={{0,2},{1,3},{2,4},{3,5},{4,6},{5,7},{6,8},{7,9},{8,10},{9,11},{10,... | collective-permute-start | bytes 405512 | tf_op jit(solution)/shard_map/ppermute | solution.py:315
  44.3 4.6 %finish.1 = (bf16[4,512,128]{2,1,0:T(8,128)(2,1)}, f32[7,128,128]{2,1,0:T(8,128)}, bf16[7,128,128]{2,1,0:T(8,128)(2,1)S(1)}, f32[2,32,128]{2,1,0:T(8,128)}, f32[...) custom-call(s32[1]{0:T(128)} %bitcast.rep, bf16[4,512,128]{2,1,0:T(8,128)(2,1)} %basis.3, f32[7,128,128]{2,1,0:T(8,128)} %trans.3, ...), custom_call_target="tpu_custom_call" | custom-call | tf_op jit(solution)/shard_map/finish/pallas_call | solution.py:394
  49.0 0.0 copy-start.2
  49.0 0.0 collective-permute-done.6.tail_rest
  49.0 0.0 copy-done.1
  49.0 1.0 %half.1 = bf16[16,128,128]{2,1,0:T(8,128)(2,1)S(1)} custom-call(s32[16]{0:T(128)S(1)} %copy-done.1, bf16[2,8,128,128]{3,2,1,0:T(8,128)(2,1)S(1)} %get-tuple-element.25.own, bf16[2,8,128,128]{3,2,1,0:T(8,128)(2,1)S(1)} %get-tuple-element.29.kept, bf16[8,128,128]{2,1,0:T(8,128)(2,1)S(1)} %collective-permute-done.5.lead_rest, ...), custom_call_target="tpu_custom_call" | custom-call | tf_op jit(solution)/shard_map/half/pallas_call | solution.py:418
  50.0 0.0 collective-permute-done.10.refs_4_
  50.0 0.0 collective-permute-done.9.refs_3_
  50.0 1.6 %collective-permute-done.8.refs_1_ = bf16[528,128]{1,0:T(8,128)(2,1)S(1)} collective-permute-done((bf16[528,128]{1,0:T(8,128)(2,1)S(1)}, bf16[528,128]{1,0:T(8,128)(2,1)S(1)}, u32[]{:S(2)}, u32[]{:S(2)}) %collective-permute-start.8) | collective-permute-done | bytes 135200 | tf_op jit(solution)/shard_map/ppermute | solution.py:315
  51.6 0.0 collective-permute-done.7.refs_0_
  51.6 0.0 copy-done.2
  51.6 1.9 %project.1 = bf16[16,128,128]{2,1,0:T(8,128)(2,1)} custom-call(s32[1]{0:T(128)} %bitcast.2.mine, s32[16]{0:T(128)S(1)} %copy-done.2, bf16[16,128,128]{2,1,0:T(8,128)(2,1)S(1)} %half.1, bf16[528,128]{1,0:T(8,128)(2,1)S(1)} %collective-permute-done.7.refs_0_, bf16[528,128]{1,0:T(8,128)(2,1)S(1)} %collective-permute-done.8.refs_1_, ...), custom_call_target="tpu_custom_call" | custom-call | tf_op jit(solution)/shard_map/project/pallas_call | solution.py:427
Async XLA Ops:
  0.6 30.3 %copy-start = (f32[2,128,128]{2,1,0:T(8,128)S(1)}, f32[2,128,128]{2,1,0:T(8,128)}, u32[]{:S(2)}) copy-start(f32[2,128,128]{2,1,0:T(8,128)} %trans_top.3) | copy-start | bytes 393220
  4.4 15.0 %collective-permute-start.3 = (bf16[2,8,128,128]{3,2,1,0:T(8,128)(2,1)S(1)}, bf16[2,8,128,128]{3,2,1,0:T(8,128)(2,1)S(1)}, u32[]{:S(2)}, u32[]{:S(2)}) collective-permute-start(bf16[2,8,128,128]{3,2,1,0:T(8,128)(2,1)S(1)} %get-tuple-element.27), channel_id=1, source_target_pairs={{0,1},{1,0},{2,3},{3,2},{4,5},{5,4},{6,7},{7,6},{8,9},{9,8},{10,11... | collective-permute-start | bytes 1572872 | tf_op jit(solution)/shard_map/ppermute | solution.py:319
  7.5 13.4 %collective-permute-start.4 = (bf16[2,8,128,128]{3,2,1,0:T(8,128)(2,1)S(1)}, bf16[2,8,128,128]{3,2,1,0:T(8,128)(2,1)S(1)}, u32[]{:S(2)}, u32[]{:S(2)}) collective-permute-start(bf16[2,8,128,128]{3,2,1,0:T(8,128)(2,1)S(1)} %get-tuple-element.28), channel_id=1, source_target_pairs={{0,2},{1,3},{2,0},{3,1},{4,6},{5,7},{6,4},{7,5},{8,10},{9,11},{10,... | collective-permute-start | bytes 1572872 | tf_op jit(solution)/shard_map/ppermute | solution.py:319
  21.0 22.0 %collective-permute-start.5 = (bf16[8,128,128]{2,1,0:T(8,128)(2,1)S(1)}, bf16[8,128,128]{2,1,0:T(8,128)(2,1)S(1)}, u32[]{:S(2)}, u32[]{:S(2)}) collective-permute-start(bf16[8,128,128]{2,1,0:T(8,128)(2,1)S(1)} %get-tuple-element.30), channel_id=1, source_target_pairs={{0,2},{1,3},{2,0},{3,1},{4,6},{5,7},{6,4},{7,5},{8,10},{9,11},{10,... | collective-permute-start | bytes 786440 | tf_op jit(solution)/shard_map/ppermute | solution.py:319
  22.6 26.4 %collective-permute-start.6 = (bf16[8,128,128]{2,1,0:T(8,128)(2,1)S(1)}, bf16[8,128,128]{2,1,0:T(8,128)(2,1)S(1)}, u32[]{:S(2)}, u32[]{:S(2)}) collective-permute-start(bf16[8,128,128]{2,1,0:T(8,128)(2,1)S(1)} %get-tuple-element.31), channel_id=1, source_target_pairs={{0,1},{1,0},{2,3},{3,2},{4,5},{5,4},{6,7},{7,6},{8,9},{9,8},{10,11... | collective-permute-start | bytes 786440 | tf_op jit(solution)/shard_map/ppermute | solution.py:319
  23.1 7.4 %collective-permute-start.2 = (f32[80,128]{1,0:T(8,128)S(1)}, f32[80,128]{1,0:T(8,128)S(1)}, u32[]{:S(2)}, u32[]{:S(2)}) collective-permute-start(f32[80,128]{1,0:T(8,128)S(1)} %get-tuple-element.20.own), channel_id=1, source_target_pairs={{0,3},{1,2},{2,1},{3,0},{4,7},{5,6},{6,5},{7,4},{8,11},{9,10},{10,... | collective-permute-start | bytes 122888 | tf_op jit(solution)/shard_map/ppermute | solution.py:319
  24.5 5.9 %collective-permute-start.1 = (f32[80,128]{1,0:T(8,128)S(1)}, f32[80,128]{1,0:T(8,128)S(1)}, u32[]{:S(2)}, u32[]{:S(2)}) collective-permute-start(f32[80,128]{1,0:T(8,128)S(1)} %get-tuple-element.20.own), channel_id=1, source_target_pairs={{0,2},{1,3},{2,0},{3,1},{4,6},{5,7},{6,4},{7,5},{8,10},{9,11},{10,... | collective-permute-start | bytes 122888 | tf_op jit(solution)/shard_map/ppermute | solution.py:319
  26.1 4.9 %collective-permute-start = (f32[80,128]{1,0:T(8,128)S(1)}, f32[80,128]{1,0:T(8,128)S(1)}, u32[]{:S(2)}, u32[]{:S(2)}) collective-permute-start(f32[80,128]{1,0:T(8,128)S(1)} %get-tuple-element.20.own), channel_id=1, source_target_pairs={{0,1},{1,0},{2,3},{3,2},{4,5},{5,4},{6,7},{7,6},{8,9},{9,8},{10,11... | collective-permute-start | bytes 122888 | tf_op jit(solution)/shard_map/ppermute | solution.py:319
  40.2 8.8 %copy-start.1 = (s32[16]{0:T(128)S(1)}, s32[16]{0:T(128)}, u32[]{:S(2)}) copy-start(s32[16]{0:T(128)} %row_slot.1) | copy-start | bytes 196
  40.2 9.8 %collective-permute-start.10 = (bf16[528,128]{1,0:T(8,128)(2,1)S(1)}, bf16[528,128]{1,0:T(8,128)(2,1)S(1)}, u32[]{:S(2)}, u32[]{:S(2)}) collective-permute-start(bf16[528,128]{1,0:T(8,128)(2,1)S(1)} %pack.1.refs_2_), channel_id=1, source_target_pairs={{0,30},{1,31},{2,0},{3,1},{4,2},{5,3},{6,4},{7,5},{8,6},{9,7},{10,... | collective-permute-start | bytes 405512 | tf_op jit(solution)/shard_map/ppermute | solution.py:315
  41.0 9.0 %collective-permute-start.9 = (bf16[528,128]{1,0:T(8,128)(2,1)S(1)}, bf16[528,128]{1,0:T(8,128)(2,1)S(1)}, u32[]{:S(2)}, u32[]{:S(2)}) collective-permute-start(bf16[528,128]{1,0:T(8,128)(2,1)S(1)} %pack.1.refs_2_), channel_id=1, source_target_pairs={{0,31},{1,0},{2,1},{3,2},{4,3},{5,4},{6,5},{7,6},{8,7},{9,8},{10,9... | collective-permute-start | bytes 405512 | tf_op jit(solution)/shard_map/ppermute | solution.py:315
  42.3 9.4 %collective-permute-start.8 = (bf16[528,128]{1,0:T(8,128)(2,1)S(1)}, bf16[528,128]{1,0:T(8,128)(2,1)S(1)}, u32[]{:S(2)}, u32[]{:S(2)}) collective-permute-start(bf16[528,128]{1,0:T(8,128)(2,1)S(1)} %pack.1.refs_2_), channel_id=1, source_target_pairs={{0,1},{1,2},{2,3},{3,4},{4,5},{5,6},{6,7},{7,8},{8,9},{9,10},{10,1... | collective-permute-start | bytes 405512 | tf_op jit(solution)/shard_map/ppermute | solution.py:315
  43.0 8.6 %collective-permute-start.7 = (bf16[528,128]{1,0:T(8,128)(2,1)S(1)}, bf16[528,128]{1,0:T(8,128)(2,1)S(1)}, u32[]{:S(2)}, u32[]{:S(2)}) collective-permute-start(bf16[528,128]{1,0:T(8,128)(2,1)S(1)} %pack.1.refs_2_), channel_id=1, source_target_pairs={{0,2},{1,3},{2,4},{3,5},{4,6},{5,7},{6,8},{7,9},{8,10},{9,11},{10,... | collective-permute-start | bytes 405512 | tf_op jit(solution)/shard_map/ppermute | solution.py:315
  49.0 2.6 %copy-start.2 = (s32[16]{0:T(128)S(1)}, s32[16]{0:T(128)}, u32[]{:S(2)}) copy-start(s32[16]{0:T(128)} %col_node.1) | copy-start | bytes 196
